TPU v7x, 32 devices: a whole 2x2x4 slice. The times are simulated.
32 devices in a mesh: groups: 2 (over y), samples: 4 (over z), blocks: 2 (over x), folds: 2 (over core).
Axes of the slice: x: 2, y: 2, z: 4, core: 2. Of those that a mesh axis runs over, the one named last changes fastest.
Arguments:
- allele_dosage_table: bfloat16 [1000, 4096], P('blocks', ('groups', 'samples')), parts along dimension 1, may hold values from -6 to 6
- phenotype_values: bfloat16 [20, 4096], P(None, ('groups', 'samples')), parts along dimension 1, may hold values from -8 to 8
- individual_partition_label: int32 [4096], P(('groups', 'samples')), parts along dimension 0, may hold values from 0 to 3, as said below
- shrink_strengths: float32 [2], replicated, may hold values from 0.005 to 2, as said below
Outputs:
- predictions: bfloat16 [4, 2, 2, 20, 1024], P('folds', 'blocks', None, None, ('groups', 'samples')), parts along dimension 4
- level_gram: float32 [8, 2, 2, 20, 2, 2], P(('groups', 'folds'), 'blocks'), parts along dimension 0
- level_cross: float32 [8, 2, 2, 20], P(('groups', 'folds'), 'blocks'), parts along dimension 0
There are 2 independent parts, one for each index of `groups`. A program takes and returns all parts, laid end to end along the dimension named above; an argument that names none is the same for every part. Nothing has to cross between parts.
Inputs may be any that keep to these rules, and one draw needn't show every extreme that they name: `individual_partition_label`: among the 512 samples of each device (aligned runs of 512 indices) every fold number appears equally often, 512 / 4 times. `shrink_strengths`: the first penalty lies between 0.005 and 0.02, every other one between 0.1 and 2.
All inputs are finite; a program needn't handle non-finite values.
Results may differ from a plain program's by a relative error of at most 0.0055.
Values may be sent and summed in bfloat16 or wider, within the bound.
No kernel may reach another device: no remote copies, remote signals or barrier semaphores. Data moves between devices by JAX's collectives and lax.ppermute only.
A program may use at most 64 MiB of HBM per device.

v0:
```python
import jax
import jax.numpy as jnp
from jax import lax
from jax.sharding import PartitionSpec as P

SHRINK_LEVELS = 2
FOLDS = 4


def per_device(allele_dosage_table, phenotype_values, individual_partition_label, shrink_strengths):
    own_count = FOLDS // lax.axis_size("folds")
    first = lax.axis_index("folds") * own_count
    rows_fold = allele_dosage_table.shape[1] // FOLDS
    total_rows = lax.axis_size("samples") * allele_dosage_table.shape[1]
    held_rows = total_rows // FOLDS
    learning_individual_tally = total_rows - held_rows
    sample_order = jnp.argsort(individual_partition_label, stable=True).reshape(FOLDS, rows_fold)
    geno_sorted = jnp.take(allele_dosage_table, sample_order, axis=1)
    trait_sorted = jnp.take(phenotype_values, sample_order, axis=1)
    geno_own = lax.dynamic_slice_in_dim(geno_sorted, first, own_count, 1)
    trait_own = lax.dynamic_slice_in_dim(trait_sorted, first, own_count, 1)
    held_gram = jnp.einsum(
        "bki,cki->kbc", geno_sorted, geno_sorted, preferred_element_type=jnp.float32
    )
    held_cross = jnp.einsum(
        "bki,pki->kbp", geno_sorted, trait_sorted, preferred_element_type=jnp.float32
    )
    own_gram = lax.dynamic_slice_in_dim(held_gram, first, own_count, 0)
    own_cross = lax.dynamic_slice_in_dim(held_cross, first, own_count, 0)
    learning_design_inner, learning_design_response = lax.psum(
        (jnp.sum(held_gram, 0)[None] - own_gram, jnp.sum(held_cross, 0)[None] - own_cross),
        "samples",
    )
    pair_total = own_count * SHRINK_LEVELS
    sample_devices = lax.axis_size("samples")
    per_processor = (pair_total + sample_devices - 1) // sample_devices
    pair_start = lax.axis_index("samples") * per_processor
    pair_ids = jnp.minimum(pair_start + jnp.arange(per_processor, dtype=jnp.int32), pair_total - 1)
    identity = jnp.eye(learning_design_inner.shape[-1], dtype=jnp.float32)

    def one_pair(pair):
        fold_pick = pair // SHRINK_LEVELS
        ridge_pick = pair % SHRINK_LEVELS
        gram_one = lax.dynamic_index_in_dim(learning_design_inner, fold_pick, 0, keepdims=False)
        cross_one = lax.dynamic_index_in_dim(learning_design_response, fold_pick, 0, keepdims=False)
        value = lax.dynamic_index_in_dim(shrink_strengths, ridge_pick, 0, keepdims=False)
        factor = jnp.linalg.cholesky(gram_one / learning_individual_tally + value * identity)
        inner = lax.linalg.triangular_solve(
            factor, cross_one / learning_individual_tally, left_side=True, lower=True
        )
        return lax.linalg.triangular_solve(
            factor, inner, left_side=True, lower=True, transpose_a=True
        )

    local_betas = lax.map(one_pair, pair_ids).astype(jnp.bfloat16)
    gathered = lax.all_gather(local_betas, "samples", axis=0, tiled=True)[:pair_total]
    shaped = gathered.reshape(own_count, SHRINK_LEVELS, gathered.shape[1], gathered.shape[2])
    coefficient_half = jnp.transpose(shaped, (1, 0, 2, 3))
    preds = jnp.einsum(
        "rkbp,bki->krpi", coefficient_half, geno_own, preferred_element_type=jnp.float32
    ).astype(jnp.bfloat16)
    block_preds = preds[:, None]
    contrib = jnp.einsum(
        "krpi,kbspi->krpbs",
        preds,
        lax.all_gather(block_preds, "blocks", axis=1, tiled=True),
        preferred_element_type=jnp.float32,
    )
    cross_rows = jnp.einsum("krpi,pki->krp", preds, trait_own, preferred_element_type=jnp.float32)
    gram_sum, cross_sum = lax.psum((contrib, cross_rows), "samples")
    level_gram = gram_sum[:, None] / held_rows
    level_cross = cross_sum[:, None] / held_rows
    return (block_preds, level_gram, level_cross)


def solution(mesh):
    in_specs = (
        P("blocks", ("groups", "samples")),
        P(None, ("groups", "samples")),
        P(("groups", "samples")),
        P(),
    )
    out_specs = (
        P("folds", "blocks", None, None, ("groups", "samples")),
        P(("groups", "folds"), "blocks", None, None, None, None),
        P(("groups", "folds"), "blocks", None, None),
    )
    return jax.shard_map(
        per_device, mesh=mesh, in_specs=in_specs, out_specs=out_specs, check_vma=False
    )
```

profile of v0, /device:TPU:0, one launch (start us, length us, event | category | flops | bytes accessed | tf_op | source)
XLA Modules:
  0.0 297.1 jit_solution(9942449200774352123)
XLA Ops:
  7.2 4.4 %sort.17 = (s32[512]{0:T(512)}, s32[512]{0:T(512)S(1)}) sort(s32[512]{0:T(512)} %param.6, s32[512]{0:T(512)S(1)} %iota.110), dimensions={0}, to_apply=%region_0.0 | sort | flops 4608 | bytes 8192 | tf_op jit(solution)/shard_map/jit(argsort)/sort | solution.py:17
  11.7 1.2 copy.26
  12.9 2.0 gather_fusion
  14.9 0.3 copy.27
  15.3 2.7 fusion.63
  18.2 1.5 gather_fusion.1
  19.8 0.4 fusion.64
  20.2 3.3 %dynamic-slice_subtract_fusion = f32[2,500,500]{2,1,0:T(8,128)} fusion(f32[4,500,500]{2,1,0:T(8,128)} %get-tuple-element.68, s32[]{:T(128)S(6)} %select_n.66, f32[500,500]{1,0:T(8,128)S(1)} %get-tuple-element.67), kind=kLoop, calls=%fused_computation.4 | loop fusion | flops 500000 | bytes 5000004 | tf_op jit(solution)/shard_map/sub | solution.py:31
  23.5 0.6 dynamic-slice_subtract_fusion.1
  24.2 0.6 dynamic_slice.32
  24.8 90.5 %all-reduce.7.cloned.1.call-done = (f32[2,500,500]{2,1,0:T(8,128)}, f32[2,500,20]{1,2,0:T(8,128)}) async-done(((f32[2,500,500]{2,1,0:T(8,128)}, f32[2,500,20]{1,2,0:T(8,128)}), (f32[2,500,500]{2,1,0:T(8,128)}, f32[2,500,20]{1,2,0:T(8,128)})) %all-reduce.7.cloned.1.call-update) | async-done | bytes 2080016 | tf_op jit(solution)/shard_map/psum | solution.py:30
  115.3 2.0 bitcast_add_fusion.1
  117.3 0.3 copy.28
  117.7 2.1 fusion.1
  119.8 11.7 %cholesky.104 = f32[128,128]{1,0:T(8,128)S(1)} custom-call(f32[128,128]{1,0:T(8,128)S(1)} %cholesky.269), custom_call_target="Cholesky" | custom-call | tf_op jit(solution)/shard_map/while/body/eval_jaxpr/jit(cholesky)/cholesky | solution.py:47
  131.7 9.8 %custom-call.40 = f32[1,128,128]{1,2,0:T(8,128)S(1)} custom-call(f32[1,128,128]{2,1,0:T(8,128)S(1)} %get-tuple-element.64), custom_call_target="InvertDiagBlocksLowerTriangular" | custom-call | tf_op jit(solution)/shard_map/while/body/eval_jaxpr/jit(cholesky)/cholesky | solution.py:47
  141.5 0.5 constant_dynamic-update-slice_fusion
  142.0 0.5 convolution_subtract_fusion
  142.5 11.7 %cholesky.217 = f32[128,128]{1,0:T(8,128)S(1)} custom-call(f32[128,128]{1,0:T(8,128)S(1)} %cholesky.273), custom_call_target="Cholesky" | custom-call | tf_op jit(solution)/shard_map/while/body/eval_jaxpr/jit(cholesky)/cholesky | solution.py:47
  154.2 9.9 %custom-call.41 = f32[1,128,128]{1,2,0:T(8,128)S(1)} custom-call(f32[1,128,128]{2,1,0:T(8,128)S(1)} %get-tuple-element.61), custom_call_target="InvertDiagBlocksLowerTriangular" | custom-call | tf_op jit(solution)/shard_map/while/body/eval_jaxpr/jit(cholesky)/cholesky | solution.py:47
  164.2 0.4 convolution_dynamic-update-slice_fusion
  164.5 0.4 convolution_subtract_fusion.1
  164.9 11.7 %cholesky.238 = f32[128,128]{1,0:T(8,128)S(1)} custom-call(f32[128,128]{1,0:T(8,128)S(1)} %cholesky.278), custom_call_target="Cholesky" | custom-call | tf_op jit(solution)/shard_map/while/body/eval_jaxpr/jit(cholesky)/cholesky | solution.py:47
  176.7 9.8 %custom-call.42 = f32[1,128,128]{1,2,0:T(8,128)S(1)} custom-call(f32[1,128,128]{2,1,0:T(8,128)S(1)} %get-tuple-element.58), custom_call_target="InvertDiagBlocksLowerTriangular" | custom-call | tf_op jit(solution)/shard_map/while/body/eval_jaxpr/jit(cholesky)/cholesky | solution.py:47
  186.5 0.3 convolution_dynamic-update-slice_fusion.1
  186.8 0.4 convolution_subtract_fusion.2
  187.1 10.8 %cholesky.258 = f32[116,116]{1,0:T(8,128)S(1)} custom-call(f32[116,116]{1,0:T(8,128)S(1)} %convolution_subtract_fusion.2), custom_call_target="Cholesky" | custom-call | tf_op jit(solution)/shard_map/while/body/eval_jaxpr/jit(cholesky)/cholesky | solution.py:47
  198.0 0.7 compare_reduce_fusion.1
  198.7 0.6 compare_reduce_fusion
  199.3 0.6 compare_reduce_fusion.2
  202.7 6.0 %while.1 = (s32[]{:T(128)}, f32[500,500]{1,0:T(8,128)S(1)}, s32[3,2]{0,1:T(2,128)S(1)}, f32[3,128,128]{2,1,0:T(8,128)S(1)}, s32[]{:T(128)}) while((s32[]{:T(128)}, f32[500,500]{1,0:T(8,128)S(1)}, s32[3,2]{0,1:T(2,128)S(1)}, f32[3,128,128]{2,1,0:T(8,128)S(1)}, s32[]{:T(128)}) %tuple.38), condition=%wide.while_cond, body=%wide.while_body.sunk | while | flops 2 | bytes 131189 | solution.py:51
  202.8 0.5 fusion.77
  203.3 1.4 bitcast_dynamic-update-slice_fusion.2
  204.8 0.5 fusion.77
  205.3 1.4 bitcast_dynamic-update-slice_fusion.2
  206.8 0.5 fusion.77
  207.3 1.4 bitcast_dynamic-update-slice_fusion.2
  208.8 39.3 %custom-call.43 = f32[4,128,128]{1,2,0:T(8,128)S(1)} custom-call(f32[4,128,128]{2,1,0:T(8,128)S(1)} %pad_maximum_fusion), custom_call_target="InvertDiagBlocksLowerTriangular" | custom-call | tf_op jit(solution)/shard_map/while/body/eval_jaxpr/triangular_solve | solution.py:51
  249.2 0.3 convolution_subtract_fusion.6
  249.4 0.2 fusion.32
  250.5 0.2 fusion.25
  250.8 0.2 convolution_subtract_fusion.3
  251.3 13.3 %all_gather.6 = bf16[4,500,20]{1,2,0:T(8,128)(2,1)S(1)} all-gather(bf16[1,500,20]{1,2,0:T(8,128)(2,1)S(1)} %pad_maximum_fusion.1), channel_id=1, replica_groups=mesh['groups'=2,'samples'=4,'blocks'=2,'folds'=2] {'samples'}, dimensions={0}, use_global_device_ids=true | all-gather | bytes 100000 | tf_op jit(solution)/shard_map/all_gather | solution.py:56
  264.7 4.5 %all-gather = bf16[2,4,20,128]{3,2,1,0:T(8,128)(2,1)S(1)} all-gather(bf16[2,2,20,128]{3,2,1,0:T(8,128)(2,1)S(1)} %convolution_convert_fusion), channel_id=2, replica_groups=mesh['groups'=2,'samples'=4,'blocks'=2,'folds'=2] {'blocks'}, dimensions={1}, use_global_device_ids=true | all-gather | bytes 61440 | tf_op jit(solution)/shard_map/all_gather | solution.py:66
  269.2 0.6 copy.33
  270.3 18.6 %all-reduce.3 = (f32[2,2,20,2,2]{1,4,3,2,0:T(2,128)S(1)}, f32[2,2,20]{2,1,0:T(2,128)S(1)}) all-reduce(f32[2,2,20,2,2]{1,4,3,2,0:T(2,128)S(1)} %convolution_bitcast_fusion, f32[2,2,20]{2,1,0:T(2,128)S(1)} %bitcast.149), channel_id=1, replica_groups=mesh['groups'=2,'samples'=4,'blocks'=2,'folds'=2] {'samples'}, use_global_device_ids=true, to_apply=%region_13.14 | all-reduce | flops 400 | bytes 3200 | tf_op jit(solution)/shard_map/psum | solution.py:70
  289.0 0.7 copy.34
  289.7 0.6 multiply_bitcast_fusion.1
  (57 shorter events, 3.9 us)
Async XLA Ops:
  7.2 108.2 %all-reduce.7.cloned.1.call-start = ((), (), s32[]{:S(2)}) async-start(), calls=%async_computation | async-start | bytes 4325376 | tf_op jit(solution)/shard_map/psum | solution.py:30
  15.3 2.8 copy-start
  23.5 0.7 copy-start.2
  186.7 61.4 %copy-start.1 = (f32[2,500,20]{1,2,0:T(8,128)S(1)}, f32[2,500,20]{1,2,0:T(8,128)}, u32[]{:S(2)}) copy-start(f32[2,500,20]{1,2,0:T(8,128)} %get-tuple-element.54) | copy-start | bytes 240004
Sparse Core Ops, SparseCore 0:
  24.3 90.9 all-reduce.6
where the time goes:
time: 298 us; the launch traced here: 297 us
  other arithmetic  131 us (44%)
  waiting for transfers between devices  90.5 us (30%)
  blocking collectives  36.4 us (12%)
  between operations  17.1 us (6%)
  local copies, waits for them, and re-layouts  13.7 us (5%)
  matrix products  8.83 us (3%)
    psum x1, waiting for transfers between devices, per_device(): lax.psum((jnp.sum(held_gram, 0)[None] - own_gram, jnp.sum(held_cross, 0)[...  90.5 us
    another operation x14, other arithmetic, one_pair(): jnp.linalg.cholesky(gram_one / learning_individual_tally + value * identity)  77.6 us
    another operation x11, other arithmetic, one_pair(): lax.linalg.triangular_solve(factor, inner, left_side=True, lower=True, tr...  39.7 us
    psum x1, blocking collectives, per_device(): gram_sum, cross_sum = lax.psum((contrib, cross_rows), 'samples')  18.6 us
    all_gather x1, blocking collectives, per_device(): lax.all_gather(local_betas, 'samples', axis=0, tiled=True)[:pair_total]  13.3 us
  transfers between devices with their start and end apart: 1, of which 1 were waited for; matrix products, arithmetic and copies ran while one was open for 0% of the time, Pallas kernels for 0%

commit v1 on v0

v1 whole, which is shorter than its diff:
```python
import functools

import jax
import jax.numpy as jnp
from jax import lax
from jax.experimental import pallas as pl
from jax.experimental.pallas import tpu as pltpu
from jax.sharding import PartitionSpec as P

SHRINK_LEVELS = 2
FOLDS = 4
LANES = 128
PANEL = 32
PIVOTS = 8
HIGHEST = lax.Precision.HIGHEST
F32 = jnp.float32
BF16 = jnp.bfloat16


def round_up(value, step):
    return (value + step - 1) // step * step


def dot_nt(left, right):
    return lax.dot_general(left, right, (((1,), (1,)), ((), ())), preferred_element_type=F32)


def spread(value):
    return jnp.broadcast_to(value, (8, LANES))


def sort_kernel(own_count, variants, traits, pad_rows, geno_ref, trait_ref, label_ref, other_ref, own_ref):
    rows = label_ref.shape[1]
    core = lax.axis_index("folds")
    cores = lax.axis_size("folds")
    slot = lax.rem(label_ref[...] + own_count * (cores - 1 - core), FOLDS)
    width = rows // FOLDS
    before = lax.broadcasted_iota(jnp.int32, (rows, rows), 0) < lax.broadcasted_iota(jnp.int32, (rows, rows), 1)
    fold_row = lax.broadcasted_iota(jnp.int32, (16, rows), 0)
    hit = jnp.broadcast_to(slot, (16, rows)) == fold_row
    rank = jnp.dot(
        jnp.where(hit, 1.0, 0.0).astype(BF16),
        jnp.where(before, 1.0, 0.0).astype(BF16),
        preferred_element_type=F32,
    )
    place = jnp.sum(jnp.where(hit, rank + (fold_row * width).astype(F32), 0.0), axis=0, keepdims=True)
    place = place.astype(jnp.int32)
    target = lax.broadcasted_iota(jnp.int32, (rows, rows), 0)
    move = jnp.where(target == jnp.broadcast_to(place, (rows, rows)), 1.0, 0.0).astype(BF16)
    sorted_geno = dot_nt(geno_ref[...], move).astype(BF16)
    sorted_trait = dot_nt(trait_ref[...], move).astype(BF16)
    half = other_ref.shape[1]
    height = other_ref.shape[0]
    low = variants // 16 * 16
    for part, ref in enumerate((other_ref, own_ref)):
        ref[low:height, :] = jnp.zeros((height - low, half), BF16)
        ref[0:variants, :] = sorted_geno[:, part * half : (part + 1) * half]
        ref[pad_rows : pad_rows + traits, :] = sorted_trait[:, part * half : (part + 1) * half]


def eliminate_panel(panels, first, ones):
    lane = lax.broadcasted_iota(jnp.int32, (8, LANES), 1)
    sub = lax.broadcasted_iota(jnp.int32, (8, LANES), 0)
    systems = range(len(panels))
    count = len(panels[0])
    panels = [list(panel) for panel in panels]
    for b in range(count):
        base_col = first + 8 * b
        in_pivot = (lane >= base_col) & (lane < base_col + 8)
        rest = [(b + 1 + i) % count for i in range(count - 1)]
        cols = [[None] * 8 for _ in systems]
        factors = [{i: [None] * 8 for i in rest} for _ in systems]
        for u in range(8):
            for q in systems:
                cols[q][u] = spread(panels[q][b][:, base_col + u : base_col + u + 1]) * ones
        for u in range(8):
            for q in systems:
                for i in rest:
                    factors[q][i][u] = spread(panels[q][i][:, base_col + u : base_col + u + 1])
        for t in range(8):
            for q in systems:
                inverse = 1.0 / spread(cols[q][t][t : t + 1, :])
                factor = jnp.where(sub == t, -1.0, cols[q][t])
                for u in range(t + 1, 8):
                    row = spread(cols[q][u][t : t + 1, :])
                    cols[q][u] = jnp.where(sub == t, 0.0, cols[q][u]) - (factor * row) * inverse
                row = jnp.where(lane == base_col + t, 1.0, spread(panels[q][b][t : t + 1, :]))
                keep = jnp.where((lane == base_col + t) | (sub == t), 0.0, panels[q][b])
                panels[q][b] = keep - (factor * row) * inverse
        for q in systems:
            rows = [spread(panels[q][b][t : t + 1, :]) for t in range(8)]
            for i in rest:
                parts = [factors[q][i][t] * rows[t] for t in range(8)]
                while len(parts) > 1:
                    parts = [parts[k] + parts[k + 1] for k in range(0, len(parts), 2)]
                panels[q][i] = jnp.where(in_pivot, 0.0, panels[q][i]) - parts[0]
    return panels


def invert_blocks(blocks, ones):
    lane = lax.broadcasted_iota(jnp.int32, (LANES, LANES), 1)
    row = lax.broadcasted_iota(jnp.int32, (LANES, LANES), 0)
    blocks = list(blocks)
    for b in range(LANES // PANEL):
        r0 = PANEL * b
        panels = eliminate_panel(
            [[block[r0 + 8 * i : r0 + 8 * i + 8, :] for i in range(PANEL // 8)] for block in blocks], r0, ones
        )
        for q, block in enumerate(blocks):
            pieces = list(panels[q])
            if r0:
                pieces.insert(0, jnp.zeros((r0, LANES), F32))
            if LANES - PANEL - r0:
                pieces.append(jnp.zeros((LANES - PANEL - r0, LANES), F32))
            wide = jnp.concatenate(pieces, axis=0)
            keep = jnp.where((lane >= r0) & (lane < r0 + PANEL), 0.0, block)
            update = keep - jnp.dot(block, wide, precision=HIGHEST, preferred_element_type=F32)
            blocks[q] = jnp.where((row >= r0) & (row < r0 + PANEL), wide, update)
    return blocks


def solve_kernel(sources, own_count, learning_tally, pad_rows, trait_rows, *refs):
    shrink_ref = refs[0]
    others, owns = refs[1 : 1 + sources], refs[1 + sources : 1 + 2 * sources]
    message_ref, mat_ref, inv_ref, ones_ref = refs[1 + 2 * sources :]
    levels = shrink_ref.shape[0]
    half = others[0].shape[1]
    width = half // own_count
    pick = lax.rem(lax.axis_index("samples"), own_count)
    held = pl.multiple_of(pick * width, width)
    train = [
        pl.multiple_of(lax.rem(pick + 1 + i, own_count) * width, width) for i in range(own_count - 1)
    ]
    ones_ref[...] = jnp.ones((8, LANES), F32)
    blocks = pad_rows // LANES
    height = others[0].shape[0]
    total = mat_ref.shape[2]
    lane = lax.broadcasted_iota(jnp.int32, (LANES, LANES), 1)
    diagonal = lane == lax.broadcasted_iota(jnp.int32, (LANES, LANES), 0)
    for j in range(blocks):
        r0 = j * LANES
        acc = None
        for s in range(sources):
            pieces = [(others[s][r0 : r0 + LANES, :], others[s][...])]
            for start in train:
                pieces.append((owns[s][r0 : r0 + LANES, pl.ds(start, width)], owns[s][:, pl.ds(start, width)]))
            for left, right in pieces:
                part = dot_nt(left, right)
                acc = part if acc is None else acc + part
        acc = acc / learning_tally
        for r in range(levels):
            mat_ref[r, r0 : r0 + LANES, 0:height] = acc
            mat_ref[r, r0 : r0 + LANES, height:total] = jnp.zeros((LANES, total - height), F32)
            mat_ref[r, r0 : r0 + LANES, r0 : r0 + LANES] = acc[:, r0 : r0 + LANES] + jnp.where(
                diagonal, shrink_ref[r], 0.0
            )

    def stage(j, carry):
        start = pl.multiple_of(j * LANES, LANES)
        inverses = invert_blocks(
            [mat_ref[r, pl.ds(start, LANES), pl.ds(start, LANES)] for r in range(levels)], ones_ref[...]
        )
        for r in range(levels):
            inv_ref[r] = inverses[r]
        for jj in range(blocks):

            @pl.when(j == jj)
            def _():
                c0 = jj * LANES
                c1 = c0 + LANES
                for r in range(levels):
                    solved = jnp.dot(
                        inv_ref[r], mat_ref[r, c0:c1, c1:total], precision=HIGHEST, preferred_element_type=F32
                    )
                    for lo, hi in ((0, c0), (c1, pad_rows)):
                        if hi > lo:
                            mat_ref[r, lo:hi, c1:total] = mat_ref[r, lo:hi, c1:total] - jnp.dot(
                                mat_ref[r, lo:hi, c0:c1], solved, precision=HIGHEST, preferred_element_type=F32
                            )
                    mat_ref[r, c0:c1, c1:total] = solved

        return carry

    lax.fori_loop(0, blocks, stage, 0)
    for r in range(levels):
        betas = jnp.transpose(mat_ref[r, :, pad_rows : pad_rows + LANES])[0:trait_rows, :].astype(BF16)
        for s in range(sources):
            message_ref[r * trait_rows : (r + 1) * trait_rows, s * width : (s + 1) * width] = jnp.dot(
                betas, owns[s][0:pad_rows, pl.ds(held, width)], preferred_element_type=F32
            ).astype(BF16)
    for s in range(sources):
        message_ref[levels * trait_rows : (levels + 1) * trait_rows, s * width : (s + 1) * width] = owns[s][
            pad_rows : pad_rows + trait_rows, pl.ds(held, width)
        ]


def level_kernel(levels, traits, trait_rows, held_rows, partner_steps, *refs):
    own_count = len(partner_steps)
    n_blocks = (len(refs) - 2) // own_count
    messages = [refs[f * n_blocks : (f + 1) * n_blocks] for f in range(own_count)]
    pred_ref, level_ref = refs[-2:]
    me = lax.axis_index("samples")
    sources = lax.axis_size("samples")
    block = lax.axis_index("blocks")
    pick = lax.rem(me, own_count)
    width = pred_ref.shape[-1]
    lane = lax.broadcasted_iota(jnp.int32, (trait_rows, LANES), 1)
    for f in range(own_count):
        slot = lax.rem(pick + f, own_count)
        partner = me - pick + slot
        mine = messages[f][0]
        where_mine = pl.multiple_of(lax.rem(partner - me + sources, sources) * width, width)
        for r in range(levels):
            pred_ref[slot, r] = mine[r * trait_rows : r * trait_rows + trait_rows, pl.ds(where_mine, width)][0:traits]
        wide = [
            [messages[f][e][s * trait_rows : (s + 1) * trait_rows, :].astype(F32) for s in range(levels)]
            for e in range(n_blocks)
        ]
        trait = mine[levels * trait_rows : (levels + 1) * trait_rows, :].astype(F32)
        for r in range(levels):
            out = jnp.where(lane == n_blocks * levels, jnp.sum(wide[0][r] * trait, axis=1, keepdims=True), 0.0)
            for e in range(n_blocks):
                column = lax.rem(block - e + n_blocks, n_blocks) * levels
                for s in range(levels):
                    total = jnp.sum(wide[0][r] * wide[e][s], axis=1, keepdims=True)
                    out = out + jnp.where(lane == column + s, total, 0.0)
            level_ref[slot, r] = out / held_rows


def per_device(allele_dosage_table, phenotype_values, individual_partition_label, shrink_strengths):
    cores = lax.axis_size("folds")
    sources = lax.axis_size("samples")
    n_blocks = lax.axis_size("blocks")
    own_count = FOLDS // cores
    levels = shrink_strengths.shape[0]
    variants, samples = allele_dosage_table.shape
    traits = phenotype_values.shape[0]
    width = samples // FOLDS
    held_rows = sources * width
    learning_tally = sources * samples - held_rows
    pad_rows = round_up(variants, LANES)
    trait_rows = round_up(traits, 32)
    height = pad_rows + trait_rows
    half = own_count * width
    vmem = pl.BlockSpec(memory_space=pltpu.VMEM)
    smem = pl.BlockSpec(memory_space=pltpu.SMEM)

    other_half, own_half = pl.pallas_call(
        functools.partial(sort_kernel, own_count, variants, traits, pad_rows),
        out_shape=[jax.ShapeDtypeStruct((height, half), BF16)] * 2,
        in_specs=[vmem] * 3,
        out_specs=[vmem] * 2,
        name="sort_samples",
    )(allele_dosage_table, phenotype_values, individual_partition_label.reshape(1, samples))

    others, owns = [other_half], [own_half]
    for shift in range(1, sources):
        others.append(lax.ppermute(other_half, "samples", [(i, (i + shift) % sources) for i in range(sources)]))
    for shift in range(1, sources):
        owns.append(lax.ppermute(others[shift], "folds", [(i, cores - 1 - i) for i in range(cores)]))

    message = pl.pallas_call(
        functools.partial(solve_kernel, sources, own_count, learning_tally, pad_rows, trait_rows),
        out_shape=jax.ShapeDtypeStruct(((levels + 1) * trait_rows, sources * width), BF16),
        in_specs=[smem] + [vmem] * (2 * sources),
        out_specs=vmem,
        scratch_shapes=[
            pltpu.VMEM((levels, pad_rows, pad_rows + LANES), F32),
            pltpu.VMEM((levels, LANES, LANES), F32),
            pltpu.VMEM((8, LANES), F32),
        ],
        name="solve_ridge",
    )(shrink_strengths, *others, *owns)

    messages = []
    for f in range(own_count):
        for e in range(n_blocks):
            if f == 0 and e == 0:
                messages.append(message)
                continue
            pairs = []
            for s in range(sources):
                source = s - s % own_count + (s % own_count + f) % own_count
                for b in range(n_blocks):
                    pairs.append((source * n_blocks + (b - e) % n_blocks, s * n_blocks + b))
            messages.append(lax.ppermute(message, ("samples", "blocks"), pairs))

    preds, level = pl.pallas_call(
        functools.partial(level_kernel, levels, traits, trait_rows, held_rows, tuple(range(own_count))),
        out_shape=[
            jax.ShapeDtypeStruct((own_count, levels, traits, width), BF16),
            jax.ShapeDtypeStruct((own_count, levels, trait_rows, LANES), F32),
        ],
        in_specs=[vmem] * len(messages),
        out_specs=[vmem] * 2,
        name="level_one",
    )(*messages)
    gram = level[:, None, :, :traits, : n_blocks * levels]
    level_gram = gram.reshape(own_count, 1, levels, traits, n_blocks, levels)
    level_cross = level[:, None, :, :traits, n_blocks * levels]
    return (preds[:, None], level_gram, level_cross)


def solution(mesh):
    in_specs = (
        P("blocks", ("groups", "samples")),
        P(None, ("groups", "samples")),
        P(("groups", "samples")),
        P(),
    )
    out_specs = (
        P("folds", "blocks", None, None, ("groups", "samples")),
        P(("groups", "folds"), "blocks", None, None, None, None),
        P(("groups", "folds"), "blocks", None, None),
    )
    return jax.shard_map(
        per_device, mesh=mesh, in_specs=in_specs, out_specs=out_specs, check_vma=False
    )
```

time: 298 us -> 77.1 us (0.26)
  other arithmetic: 131 us -> 0 us
  waiting for transfers between devices: 90.5 us -> 29 us
  blocking collectives: 36.4 us -> 0 us
  Pallas kernels: 0 us -> 31.5 us
  between operations: 17.1 us -> 0.67 us
  starting transfers between devices: 0.04 us -> 10.1 us
  matrix products: 8.83 us -> 0 us
  local copies, waits for them, and re-layouts: 13.7 us -> 5.57 us
    another operation x25 -> x0, other arithmetic: 117 us -> none  [the longest x14 77.6 us: one_pair(): jnp.linalg.cholesky(gram_one / learning_individual_tally + value * identity)]
    psum x1 -> x0, waiting for transfers between devices: 90.5 us -> none  [per_device(): lax.psum((jnp.sum(held_gram, 0)[None] - own_gram, jnp.sum(held_cross, 0)[...]
    pallas_call x0 -> x3, Pallas kernels: none -> 31.5 us  [the longest x1 27 us: per_device(): pl.pallas_call(functools.partial(solve_kernel, sources, own_count, learni...]
    ppermute x0 -> x9, waiting for transfers between devices: none -> 29 us  [the longest x3 22.9 us: per_device(): lax.ppermute(other_half, 'samples', [(i, (i + shift) % sources) for i in...]
    psum x1 -> x0, blocking collectives: 18.6 us -> none  [per_device(): gram_sum, cross_sum = lax.psum((contrib, cross_rows), 'samples')]
    all_gather x2 -> x0, blocking collectives: 17.8 us -> none  [the longest x1 13.3 us: per_device(): lax.all_gather(local_betas, 'samples', axis=0, tiled=True)[:pair_total]]
    ppermute x0 -> x9, starting transfers between devices: none -> 10.1 us  [the longest x3 6.09 us: per_device(): lax.ppermute(other_half, 'samples', [(i, (i + shift) % sources) for i in...]
    another operation x15 -> x0, local copies, waits for them, and re-layouts: 6.09 us -> none
  transfers between devices with their start and end apart: 1 -> 9, of which waited for: 1 -> 7; matrix products, arithmetic and copies ran while one was open for 0% -> 0% of each run, Pallas kernels for 0% -> 0%
where the time goes in v1:
time: 77.1 us; the launch traced here: 76.8 us
  Pallas kernels  31.5 us (41%)
  waiting for transfers between devices  29 us (38%)
  starting transfers between devices  10.1 us (13%)
  local copies, waits for them, and re-layouts  5.57 us (7%)
    pallas_call x1, Pallas kernels, per_device(): pl.pallas_call(functools.partial(solve_kernel, sources, own_count, learni...  27 us
    ppermute x3, waiting for transfers between devices, per_device(): lax.ppermute(other_half, 'samples', [(i, (i + shift) % sources) for i in...  22.9 us
    ppermute x3, starting transfers between devices, per_device(): lax.ppermute(other_half, 'samples', [(i, (i + shift) % sources) for i in...  6.09 us
    ppermute x3, waiting for transfers between devices, per_device(): messages.append(lax.ppermute(message, ('samples', 'blocks'), pairs))  4.67 us
    ppermute x3, starting transfers between devices, per_device(): messages.append(lax.ppermute(message, ('samples', 'blocks'), pairs))  3.49 us
    pallas_call x1, Pallas kernels, per_device(): pl.pallas_call(functools.partial(sort_kernel, own_count, variants, traits...  2.6 us
    unnamed x21, local copies, waits for them, and re-layouts  2.52 us
    pallas_call x1, Pallas kernels, per_device(): pl.pallas_call(functools.partial(level_kernel, levels, traits, trait_rows...  1.84 us
  transfers between devices with their start and end apart: 9, of which 7 were waited for; matrix products, arithmetic and copies ran while one was open for 0% of the time, Pallas kernels for 0%

profile of v1, /device:TPU:0, one launch (start us, length us, event | category | flops | bytes accessed | tf_op | source)
XLA Modules:
  0.0 76.8 jit_solution(9869457490927764932)
XLA Ops:
  0.6 2.6 %sort_samples.1 = (bf16[544,256]{1,0:T(8,128)(2,1)}, bf16[544,256]{1,0:T(8,128)(2,1)}) custom-call(bf16[500,512]{1,0:T(8,128)(2,1)} %geno_ref.1, bf16[20,512]{1,0:T(8,128)(2,1)} %trait_ref.1, s32[1,512]{1,0:T(1,128)} %bitcast.10), custom_call_target="tpu_custom_call" | custom-call | tf_op jit(solution)/shard_map/sort_samples/pallas_call | solution.py:248
  3.2 5.1 %collective-permute-start.2 = (bf16[544,256]{1,0:T(8,128)(2,1)}, bf16[544,256]{1,0:T(8,128)(2,1)S(1)}, u32[]{:S(2)}, u32[]{:S(2)}) collective-permute-start(bf16[544,256]{1,0:T(8,128)(2,1)} %get-tuple-element.7.refs_1_), channel_id=1, source_target_pairs={{0,12},{4,0},{8,4},{12,8},{1,13},{5,1},{9,5},{13,9},{2,14},{6,2},{... | collective-permute-start | bytes 835592 | tf_op jit(solution)/shard_map/ppermute | solution.py:258
  8.3 0.0 collective-permute-start.1
  8.3 1.0 %collective-permute-start = (bf16[544,256]{1,0:T(8,128)(2,1)}, bf16[544,256]{1,0:T(8,128)(2,1)S(1)}, u32[]{:S(2)}, u32[]{:S(2)}) collective-permute-start(bf16[544,256]{1,0:T(8,128)(2,1)} %get-tuple-element.7.refs_1_), channel_id=1, source_target_pairs={{0,4},{4,8},{8,12},{12,0},{1,5},{5,9},{9,13},{13,1},{2,6},{6,10},{... | collective-permute-start | bytes 835592 | tf_op jit(solution)/shard_map/ppermute | solution.py:258
  9.3 6.4 %collective-permute-done.2.refs_4_ = bf16[544,256]{1,0:T(8,128)(2,1)S(1)} collective-permute-done((bf16[544,256]{1,0:T(8,128)(2,1)}, bf16[544,256]{1,0:T(8,128)(2,1)S(1)}, u32[]{:S(2)}, u32[]{:S(2)}) %collective-permute-start.2) | collective-permute-done | bytes 278560 | tf_op jit(solution)/shard_map/ppermute | solution.py:258
  15.7 0.0 copy-start
  15.7 0.0 collective-permute-start.5
  15.7 16.5 %collective-permute-done.1.refs_3_ = bf16[544,256]{1,0:T(8,128)(2,1)S(1)} collective-permute-done((bf16[544,256]{1,0:T(8,128)(2,1)}, bf16[544,256]{1,0:T(8,128)(2,1)S(1)}, u32[]{:S(2)}, u32[]{:S(2)}) %collective-permute-start.1) | collective-permute-done | bytes 278560 | tf_op jit(solution)/shard_map/ppermute | solution.py:258
  32.2 0.0 copy-start.1
  32.2 0.0 collective-permute-start.4
  32.2 0.0 collective-permute-done.refs_2_
  32.2 0.0 copy-start.2
  32.3 0.5 collective-permute-start.3
  32.7 0.0 collective-permute-done.5.refs_8_
  32.8 0.0 copy-start.3
  32.8 1.0 %collective-permute-done.4.refs_7_ = bf16[544,256]{1,0:T(8,128)(2,1)S(1)} collective-permute-done((bf16[544,256]{1,0:T(8,128)(2,1)S(1)}, bf16[544,256]{1,0:T(8,128)(2,1)S(1)}, u32[]{:S(2)}, u32[]{:S(2)}) %collective-permute-start.4) | collective-permute-done | bytes 278560 | tf_op jit(solution)/shard_map/ppermute | solution.py:260
  33.8 0.0 copy-start.4
  33.8 0.4 collective-permute-done.3.refs_6_
  34.2 0.0 copy-start.5
  34.2 0.0 copy-done
  34.2 0.0 copy-done.1
  34.2 0.0 copy-done.2
  34.2 0.0 copy-done.3
  34.2 0.3 copy-done.4
  34.5 0.4 copy-done.5
  34.9 27.0 %solve_ridge.1.refs_0_ = bf16[96,512]{1,0:T(8,128)(2,1)} custom-call(f32[2]{0:T(128)} %refs_0_.1, bf16[544,256]{1,0:T(8,128)(2,1)} %get-tuple-element.7.refs_1_, bf16[544,256]{1,0:T(8,128)(2,1)} %copy-done.2, bf16[544,256]{1,0:T(8,128)(2,1)} %copy-done.1, bf16[544,256]{1,0:T(8,128)(2,1)} %copy-done, bf16[544,256]{1,0:T(8,128)(2,1)} %get-tuple-element.8.refs_5_, ...), custom_call_target="tpu_custom_call" | custom-call | tf_op jit(solution)/shard_map/solve_ridge/pallas_call | solution.py:262
  61.9 1.5 %collective-permute-start.8 = (bf16[96,512]{1,0:T(8,128)(2,1)}, bf16[96,512]{1,0:T(8,128)(2,1)S(1)}, u32[]{:S(2)}, u32[]{:S(2)}) collective-permute-start(bf16[96,512]{1,0:T(8,128)(2,1)} %solve_ridge.1.refs_0_), channel_id=1, source_target_pairs={{6,0},{4,2},{2,4},{0,6},{14,8},{12,10},{10,12},{8,14},{7,1},{5,3},... | collective-permute-start | bytes 294920 | tf_op jit(solution)/shard_map/ppermute | solution.py:286
  63.4 1.5 %collective-permute-start.7 = (bf16[96,512]{1,0:T(8,128)(2,1)}, bf16[96,512]{1,0:T(8,128)(2,1)S(1)}, u32[]{:S(2)}, u32[]{:S(2)}) collective-permute-start(bf16[96,512]{1,0:T(8,128)(2,1)} %solve_ridge.1.refs_0_), channel_id=1, source_target_pairs={{4,0},{6,2},{0,4},{2,6},{12,8},{14,10},{8,12},{10,14},{5,1},{7,3},... | collective-permute-start | bytes 294920 | tf_op jit(solution)/shard_map/ppermute | solution.py:286
  64.9 0.5 collective-permute-start.6
  65.4 3.3 %collective-permute-done.8.refs_3_ = bf16[96,512]{1,0:T(8,128)(2,1)S(1)} collective-permute-done((bf16[96,512]{1,0:T(8,128)(2,1)}, bf16[96,512]{1,0:T(8,128)(2,1)S(1)}, u32[]{:S(2)}, u32[]{:S(2)}) %collective-permute-start.8) | collective-permute-done | bytes 98336 | tf_op jit(solution)/shard_map/ppermute | solution.py:286
  68.7 0.0 copy-start.6
  68.7 1.3 %collective-permute-done.7.refs_2_ = bf16[96,512]{1,0:T(8,128)(2,1)S(1)} collective-permute-done((bf16[96,512]{1,0:T(8,128)(2,1)}, bf16[96,512]{1,0:T(8,128)(2,1)S(1)}, u32[]{:S(2)}, u32[]{:S(2)}) %collective-permute-start.7) | collective-permute-done | bytes 98336 | tf_op jit(solution)/shard_map/ppermute | solution.py:286
  70.0 0.0 copy-start.7
  70.0 0.1 collective-permute-done.6.refs_1_
  70.1 0.0 copy-done.6
  70.1 0.6 copy-done.7
  70.6 0.0 copy-start.8
  70.6 0.6 copy-done.8
  71.3 1.8 %level_one.1 = (bf16[2,2,20,128]{3,2,1,0:T(8,128)(2,1)}, f32[2,2,32,128]{3,2,1,0:T(8,128)}) custom-call(bf16[96,512]{1,0:T(8,128)(2,1)} %solve_ridge.1.refs_0_, bf16[96,512]{1,0:T(8,128)(2,1)} %copy-done.8, bf16[96,512]{1,0:T(8,128)(2,1)} %copy-done.7, bf16[96,512]{1,0:T(8,128)(2,1)} %copy-done.6), custom_call_target="tpu_custom_call" | custom-call | tf_op jit(solution)/shard_map/level_one/pallas_call | solution.py:288
  73.1 1.5 %slice_reduce_fusion = f32[2,2,20]{2,1,0:T(2,128)} fusion(f32[2,2,32,128]{3,2,1,0:T(8,128)} %get-tuple-element.10), kind=kLoop, calls=%fused_computation | loop fusion | bytes 640 | tf_op jit(solution)/shard_map/slice | solution.py:300
  74.7 0.0 copy-start.9
  74.7 0.8 %slice.6 = f32[2,2,20,4]{3,2,1,0:T(8,128)S(1)} slice(f32[2,2,32,128]{3,2,1,0:T(8,128)} %get-tuple-element.10), slice={[0:2], [0:2], [0:20], [0:4]} | slice | bytes 2560 | tf_op jit(solution)/shard_map/slice | solution.py:298
  75.5 0.0 copy-done.9
  75.5 0.6 copy.11
  76.1 0.7 copy.10
Async XLA Ops:
  3.2 12.5 %collective-permute-start.2 = (bf16[544,256]{1,0:T(8,128)(2,1)}, bf16[544,256]{1,0:T(8,128)(2,1)S(1)}, u32[]{:S(2)}, u32[]{:S(2)}) collective-permute-start(bf16[544,256]{1,0:T(8,128)(2,1)} %get-tuple-element.7.refs_1_), channel_id=1, source_target_pairs={{0,12},{4,0},{8,4},{12,8},{1,13},{5,1},{9,5},{13,9},{2,14},{6,2},{... | collective-permute-start | bytes 835592 | tf_op jit(solution)/shard_map/ppermute | solution.py:258
  8.3 23.9 %collective-permute-start.1 = (bf16[544,256]{1,0:T(8,128)(2,1)}, bf16[544,256]{1,0:T(8,128)(2,1)S(1)}, u32[]{:S(2)}, u32[]{:S(2)}) collective-permute-start(bf16[544,256]{1,0:T(8,128)(2,1)} %get-tuple-element.7.refs_1_), channel_id=1, source_target_pairs={{0,8},{4,12},{8,0},{12,4},{1,9},{5,13},{9,1},{13,5},{2,10},{6,14},... | collective-permute-start | bytes 835592 | tf_op jit(solution)/shard_map/ppermute | solution.py:258
  8.3 23.9 %collective-permute-start = (bf16[544,256]{1,0:T(8,128)(2,1)}, bf16[544,256]{1,0:T(8,128)(2,1)S(1)}, u32[]{:S(2)}, u32[]{:S(2)}) collective-permute-start(bf16[544,256]{1,0:T(8,128)(2,1)} %get-tuple-element.7.refs_1_), channel_id=1, source_target_pairs={{0,4},{4,8},{8,12},{12,0},{1,5},{5,9},{9,13},{13,1},{2,6},{6,10},{... | collective-permute-start | bytes 835592 | tf_op jit(solution)/shard_map/ppermute | solution.py:258
  15.7 18.5 %copy-start = (bf16[544,256]{1,0:T(8,128)(2,1)}, bf16[544,256]{1,0:T(8,128)(2,1)S(1)}, u32[]{:S(2)}) copy-start(bf16[544,256]{1,0:T(8,128)(2,1)S(1)} %collective-permute-done.2.refs_4_) | copy-start | bytes 835588
  15.7 17.0 %collective-permute-start.5 = (bf16[544,256]{1,0:T(8,128)(2,1)S(1)}, bf16[544,256]{1,0:T(8,128)(2,1)S(1)}, u32[]{:S(2)}, u32[]{:S(2)}) collective-permute-start(bf16[544,256]{1,0:T(8,128)(2,1)S(1)} %collective-permute-done.2.refs_4_), channel_id=1, source_target_pairs={{0,1},{1,0},{2,3},{3,2},{4,5},{5,4},{6,7},{7,6},{8,9},{9,8},{10,11... | collective-permute-start | bytes 835592 | tf_op jit(solution)/shard_map/ppermute | solution.py:260
  32.2 2.0 %copy-start.1 = (bf16[544,256]{1,0:T(8,128)(2,1)}, bf16[544,256]{1,0:T(8,128)(2,1)S(1)}, u32[]{:S(2)}) copy-start(bf16[544,256]{1,0:T(8,128)(2,1)S(1)} %collective-permute-done.1.refs_3_) | copy-start | bytes 835588
  32.2 1.6 %collective-permute-start.4 = (bf16[544,256]{1,0:T(8,128)(2,1)S(1)}, bf16[544,256]{1,0:T(8,128)(2,1)S(1)}, u32[]{:S(2)}, u32[]{:S(2)}) collective-permute-start(bf16[544,256]{1,0:T(8,128)(2,1)S(1)} %collective-permute-done.1.refs_3_), channel_id=1, source_target_pairs={{0,1},{1,0},{2,3},{3,2},{4,5},{5,4},{6,7},{7,6},{8,9},{9,8},{10,11... | collective-permute-start | bytes 835592 | tf_op jit(solution)/shard_map/ppermute | solution.py:260
  32.2 2.0 %copy-start.2 = (bf16[544,256]{1,0:T(8,128)(2,1)}, bf16[544,256]{1,0:T(8,128)(2,1)S(1)}, u32[]{:S(2)}) copy-start(bf16[544,256]{1,0:T(8,128)(2,1)S(1)} %collective-permute-done.refs_2_) | copy-start | bytes 835588
  32.3 1.9 %collective-permute-start.3 = (bf16[544,256]{1,0:T(8,128)(2,1)S(1)}, bf16[544,256]{1,0:T(8,128)(2,1)S(1)}, u32[]{:S(2)}, u32[]{:S(2)}) collective-permute-start(bf16[544,256]{1,0:T(8,128)(2,1)S(1)} %collective-permute-done.refs_2_), channel_id=1, source_target_pairs={{0,1},{1,0},{2,3},{3,2},{4,5},{5,4},{6,7},{7,6},{8,9},{9,8},{10,11... | collective-permute-start | bytes 835592 | tf_op jit(solution)/shard_map/ppermute | solution.py:260
  32.8 1.5 %copy-start.3 = (bf16[544,256]{1,0:T(8,128)(2,1)}, bf16[544,256]{1,0:T(8,128)(2,1)S(1)}, u32[]{:S(2)}) copy-start(bf16[544,256]{1,0:T(8,128)(2,1)S(1)} %collective-permute-done.5.refs_8_) | copy-start | bytes 835588
  33.8 0.7 copy-start.4
  34.2 0.7 copy-start.5
  61.9 6.8 %collective-permute-start.8 = (bf16[96,512]{1,0:T(8,128)(2,1)}, bf16[96,512]{1,0:T(8,128)(2,1)S(1)}, u32[]{:S(2)}, u32[]{:S(2)}) collective-permute-start(bf16[96,512]{1,0:T(8,128)(2,1)} %solve_ridge.1.refs_0_), channel_id=1, source_target_pairs={{6,0},{4,2},{2,4},{0,6},{14,8},{12,10},{10,12},{8,14},{7,1},{5,3},... | collective-permute-start | bytes 294920 | tf_op jit(solution)/shard_map/ppermute | solution.py:286
  63.4 6.6 %collective-permute-start.7 = (bf16[96,512]{1,0:T(8,128)(2,1)}, bf16[96,512]{1,0:T(8,128)(2,1)S(1)}, u32[]{:S(2)}, u32[]{:S(2)}) collective-permute-start(bf16[96,512]{1,0:T(8,128)(2,1)} %solve_ridge.1.refs_0_), channel_id=1, source_target_pairs={{4,0},{6,2},{0,4},{2,6},{12,8},{14,10},{8,12},{10,14},{5,1},{7,3},... | collective-permute-start | bytes 294920 | tf_op jit(solution)/shard_map/ppermute | solution.py:286
  64.9 5.2 %collective-permute-start.6 = (bf16[96,512]{1,0:T(8,128)(2,1)}, bf16[96,512]{1,0:T(8,128)(2,1)S(1)}, u32[]{:S(2)}, u32[]{:S(2)}) collective-permute-start(bf16[96,512]{1,0:T(8,128)(2,1)} %solve_ridge.1.refs_0_), channel_id=1, source_target_pairs={{2,0},{0,2},{6,4},{4,6},{10,8},{8,10},{14,12},{12,14},{3,1},{1,3},... | collective-permute-start | bytes 294920 | tf_op jit(solution)/shard_map/ppermute | solution.py:286
  68.7 1.4 %copy-start.6 = (bf16[96,512]{1,0:T(8,128)(2,1)}, bf16[96,512]{1,0:T(8,128)(2,1)S(1)}, u32[]{:S(2)}) copy-start(bf16[96,512]{1,0:T(8,128)(2,1)S(1)} %collective-permute-done.8.refs_3_) | copy-start | bytes 294916
  70.0 0.6 copy-start.7
  70.6 0.6 copy-start.8
  74.7 0.8 %copy-start.9 = (bf16[2,2,20,128]{3,2,1,0:T(8,128)(2,1)S(1)}, bf16[2,2,20,128]{3,2,1,0:T(8,128)(2,1)}, u32[]{:S(2)}) copy-start(bf16[2,2,20,128]{3,2,1,0:T(8,128)(2,1)} %get-tuple-element.9) | copy-start | bytes 61444

commit v2 on v1

v2 whole, which is shorter than its diff:
```python
import functools

import jax
import jax.numpy as jnp
from jax import lax
from jax.experimental import pallas as pl
from jax.experimental.pallas import tpu as pltpu
from jax.sharding import PartitionSpec as P

SHRINK_LEVELS = 2
FOLDS = 4
LANES = 128
PANEL = 32
PIVOTS = 8
HIGHEST = lax.Precision.HIGHEST
F32 = jnp.float32
BF16 = jnp.bfloat16


def round_up(value, step):
    return (value + step - 1) // step * step


def dot_nt(left, right):
    return lax.dot_general(left, right, (((1,), (1,)), ((), ())), preferred_element_type=F32)


def spread(value):
    return jnp.broadcast_to(value, (8, LANES))


def sort_kernel(own_count, pad_rows, geno_ref, trait_ref, label_ref, *refs):
    variants, traits = geno_ref.shape[0], trait_ref.shape[0]
    rows = label_ref.shape[1]
    core = lax.axis_index("folds")
    cores = lax.axis_size("folds")
    slot = lax.rem(label_ref[...] + own_count * (cores - 1 - core), FOLDS)
    width = rows // FOLDS
    before = lax.broadcasted_iota(jnp.int32, (rows, rows), 0) < lax.broadcasted_iota(jnp.int32, (rows, rows), 1)
    fold_row = lax.broadcasted_iota(jnp.int32, (16, rows), 0)
    hit = jnp.broadcast_to(slot, (16, rows)) == fold_row
    rank = jnp.dot(
        jnp.where(hit, 1.0, 0.0).astype(BF16),
        jnp.where(before, 1.0, 0.0).astype(BF16),
        preferred_element_type=F32,
    )
    place = jnp.sum(jnp.where(hit, rank + (fold_row * width).astype(F32), 0.0), axis=0, keepdims=True)
    place = place.astype(jnp.int32)
    target = lax.broadcasted_iota(jnp.int32, (rows, rows), 0)
    move = jnp.where(target == jnp.broadcast_to(place, (rows, rows)), 1.0, 0.0).astype(BF16)
    sorted_geno = dot_nt(geno_ref[...], move).astype(BF16)
    sorted_trait = dot_nt(trait_ref[...], move).astype(BF16)
    split = refs[0].shape[0]
    half = refs[0].shape[1]
    height = refs[2].shape[0]
    low = (variants - split) // 16 * 16
    for part in range(2):
        lanes = slice(part * half, (part + 1) * half)
        refs[part][...] = sorted_geno[0:split, lanes]
        ref = refs[2 + part]
        ref[low:height, :] = jnp.zeros((height - low, half), BF16)
        ref[0 : variants - split, :] = sorted_geno[split:variants, lanes]
        ref[pad_rows - split : pad_rows - split + traits, :] = sorted_trait[:, lanes]


def eliminate_panel(panels, first, ones):
    lane = lax.broadcasted_iota(jnp.int32, (8, LANES), 1)
    sub = lax.broadcasted_iota(jnp.int32, (8, LANES), 0)
    systems = range(len(panels))
    count = len(panels[0])
    panels = [list(panel) for panel in panels]
    for b in range(count):
        base_col = first + 8 * b
        in_pivot = (lane >= base_col) & (lane < base_col + 8)
        rest = [(b + 1 + i) % count for i in range(count - 1)]
        cols = [[None] * 8 for _ in systems]
        factors = [{i: [None] * 8 for i in rest} for _ in systems]
        for u in range(8):
            for q in systems:
                cols[q][u] = spread(panels[q][b][:, base_col + u : base_col + u + 1]) * ones
        for u in range(8):
            for q in systems:
                for i in rest:
                    factors[q][i][u] = spread(panels[q][i][:, base_col + u : base_col + u + 1])
        for t in range(8):
            for q in systems:
                inverse = 1.0 / spread(cols[q][t][t : t + 1, :])
                factor = jnp.where(sub == t, -1.0, cols[q][t])
                for u in range(t + 1, 8):
                    row = spread(cols[q][u][t : t + 1, :])
                    cols[q][u] = jnp.where(sub == t, 0.0, cols[q][u]) - (factor * row) * inverse
                row = jnp.where(lane == base_col + t, 1.0, spread(panels[q][b][t : t + 1, :]))
                keep = jnp.where((lane == base_col + t) | (sub == t), 0.0, panels[q][b])
                panels[q][b] = keep - (factor * row) * inverse
        for q in systems:
            rows = [spread(panels[q][b][t : t + 1, :]) for t in range(8)]
            for i in rest:
                parts = [factors[q][i][t] * rows[t] for t in range(8)]
                while len(parts) > 1:
                    parts = [parts[k] + parts[k + 1] for k in range(0, len(parts), 2)]
                panels[q][i] = jnp.where(in_pivot, 0.0, panels[q][i]) - parts[0]
    return panels


def invert_blocks(blocks, ones):
    lane = lax.broadcasted_iota(jnp.int32, (LANES, LANES), 1)
    row = lax.broadcasted_iota(jnp.int32, (LANES, LANES), 0)
    blocks = list(blocks)
    for b in range(LANES // PANEL):
        r0 = PANEL * b
        panels = eliminate_panel(
            [[block[r0 + 8 * i : r0 + 8 * i + 8, :] for i in range(PANEL // 8)] for block in blocks], r0, ones
        )
        for q, block in enumerate(blocks):
            pieces = list(panels[q])
            if r0:
                pieces.insert(0, jnp.zeros((r0, LANES), F32))
            if LANES - PANEL - r0:
                pieces.append(jnp.zeros((LANES - PANEL - r0, LANES), F32))
            wide = jnp.concatenate(pieces, axis=0)
            keep = jnp.where((lane >= r0) & (lane < r0 + PANEL), 0.0, block)
            update = keep - jnp.dot(block, wide, precision=HIGHEST, preferred_element_type=F32)
            blocks[q] = jnp.where((row >= r0) & (row < r0 + PANEL), wide, update)
    return blocks


def dot_f32(left, right):
    return jnp.dot(left, right, precision=HIGHEST, preferred_element_type=F32)


def fold_lanes(own_count, width):
    pick = lax.rem(lax.axis_index("samples"), own_count)
    held = pl.multiple_of(pick * width, width)
    train = [pl.multiple_of(lax.rem(pick + 1 + i, own_count) * width, width) for i in range(own_count - 1)]
    return held, train


def training_product(left, right, train, width, rows):
    acc = None
    for left_other, left_own, right_other, right_own in zip(*left, *right):
        pieces = [(left_other[rows, :], right_other[...])]
        for start in train:
            pieces.append((left_own[rows, pl.ds(start, width)], right_own[:, pl.ds(start, width)]))
        for a, b in pieces:
            part = dot_nt(a, b)
            acc = part if acc is None else acc + part
    return acc


def stages(count, levels, mat_ref, inv_ref, ones_ref, follow):
    def stage(j, carry):
        start = pl.multiple_of(j * LANES, LANES)
        inverses = invert_blocks(
            [mat_ref[r, pl.ds(start, LANES), pl.ds(start, LANES)] for r in range(levels)], ones_ref[...]
        )
        for r in range(levels):
            inv_ref[r] = inverses[r]
        for jj in range(count):

            @pl.when(j == jj)
            def _():
                for r in range(levels):
                    follow(jj, r)

        return carry

    lax.fori_loop(0, count, stage, 0)


def lead_kernel(sources, own_count, learning_tally, *refs):
    shrink_ref = refs[0]
    others, owns = refs[1 : 1 + sources], refs[1 + sources : 1 + 2 * sources]
    out_ref, inv_ref, ones_ref = refs[1 + 2 * sources :]
    levels, size = out_ref.shape[0], out_ref.shape[1]
    width = others[0].shape[1] // own_count
    _, train = fold_lanes(own_count, width)
    ones_ref[...] = jnp.ones((8, LANES), F32)
    diagonal = lax.broadcasted_iota(jnp.int32, (LANES, size), 1) - lax.broadcasted_iota(jnp.int32, (LANES, size), 0)
    for r0 in range(0, size, LANES):
        rows = slice(r0, r0 + LANES)
        acc = training_product((others, owns), (others, owns), train, width, rows) / learning_tally
        for r in range(levels):
            out_ref[r, rows, :] = acc + jnp.where(diagonal == r0, shrink_ref[r], 0.0)

    def follow(j, r):
        c0, c1 = j * LANES, (j + 1) * LANES
        inverse = inv_ref[r]
        spans = [(lo, hi) for lo, hi in ((0, c0), (c1, size)) if hi > lo]
        solved = [dot_f32(inverse, out_ref[r, c0:c1, lo:hi]) for lo, hi in spans]
        for lo, hi in spans:
            column = out_ref[r, lo:hi, c0:c1]
            for (left, right), value in zip(spans, solved):
                out_ref[r, lo:hi, left:right] = out_ref[r, lo:hi, left:right] - dot_f32(column, value)
            out_ref[r, lo:hi, c0:c1] = -dot_f32(column, inverse)
        for (left, right), value in zip(spans, solved):
            out_ref[r, c0:c1, left:right] = value
        out_ref[r, c0:c1, c0:c1] = inverse

    stages(size // LANES, levels, out_ref, inv_ref, ones_ref, follow)


def tail_kernel(sources, own_count, learning_tally, trait_rows, *refs):
    shrink_ref, lead_ref = refs[0:2]
    first = (refs[2 : 2 + sources], refs[2 + sources : 2 + 2 * sources])
    last = (refs[2 + 2 * sources : 2 + 3 * sources], refs[2 + 3 * sources : 2 + 4 * sources])
    message_ref, wide_ref, solved_ref, mat_ref, inv_ref, ones_ref = refs[2 + 4 * sources :]
    levels, lead = lead_ref.shape[0], lead_ref.shape[1]
    size, total = mat_ref.shape[1], mat_ref.shape[2]
    width = first[0][0].shape[1] // own_count
    height = size + trait_rows
    held, train = fold_lanes(own_count, width)
    ones_ref[...] = jnp.ones((8, LANES), F32)
    for r0 in range(0, lead, LANES):
        rows = slice(r0, r0 + LANES)
        wide_ref[rows, 0:height] = training_product(first, last, train, width, rows) / learning_tally
        wide_ref[rows, height:total] = jnp.zeros((LANES, total - height), F32)
    for r in range(levels):
        solved_ref[r] = dot_f32(lead_ref[r], wide_ref[...])
    diagonal = lax.broadcasted_iota(jnp.int32, (LANES, height), 1) - lax.broadcasted_iota(
        jnp.int32, (LANES, height), 0
    )
    for r0 in range(0, size, LANES):
        rows = slice(r0, r0 + LANES)
        side = training_product(last, first, train, width, rows) / learning_tally
        acc = training_product(last, last, train, width, rows) / learning_tally
        for r in range(levels):
            mat_ref[r, rows, 0:height] = acc + jnp.where(diagonal == r0, shrink_ref[r], 0.0)
            mat_ref[r, rows, height:total] = jnp.zeros((LANES, total - height), F32)
            mat_ref[r, rows, :] = mat_ref[r, rows, :] - dot_f32(side, solved_ref[r])

    def follow(j, r):
        c0, c1 = j * LANES, (j + 1) * LANES
        solved = dot_f32(inv_ref[r], mat_ref[r, c0:c1, c1:total])
        for lo, hi in ((0, c0), (c1, size)):
            if hi > lo:
                mat_ref[r, lo:hi, c1:total] = mat_ref[r, lo:hi, c1:total] - dot_f32(mat_ref[r, lo:hi, c0:c1], solved)
        mat_ref[r, c0:c1, c1:total] = solved

    stages(size // LANES, levels, mat_ref, inv_ref, ones_ref, follow)
    for r in range(levels):
        low = mat_ref[r, :, size:total]
        top = solved_ref[r, :, size:total] - dot_f32(solved_ref[r, :, 0:size], low)
        top = jnp.transpose(top)[0:trait_rows, :].astype(BF16)
        low = jnp.transpose(low)[0:trait_rows, :].astype(BF16)
        for s in range(sources):
            value = jnp.dot(top, first[1][s][:, pl.ds(held, width)], preferred_element_type=F32) + jnp.dot(
                low, last[1][s][0:size, pl.ds(held, width)], preferred_element_type=F32
            )
            message_ref[r * trait_rows : (r + 1) * trait_rows, s * width : (s + 1) * width] = value.astype(BF16)
    for s in range(sources):
        message_ref[levels * trait_rows : (levels + 1) * trait_rows, s * width : (s + 1) * width] = last[1][s][
            size : size + trait_rows, pl.ds(held, width)
        ]


def level_kernel(own_count, trait_rows, held_rows, *refs):
    pred_ref, gram_ref, cross_ref = refs[-3:]
    n_blocks = (len(refs) - 3) // own_count
    messages = [refs[f * n_blocks : (f + 1) * n_blocks] for f in range(own_count)]
    levels, traits, width = pred_ref.shape[2:]
    me = lax.axis_index("samples")
    block = lax.axis_index("blocks")
    pick = lax.rem(me, own_count)
    lane = lax.broadcasted_iota(jnp.int32, (trait_rows, LANES), 1)
    for f in range(own_count):
        slot = lax.rem(pick + f, own_count)
        mine = messages[f][0]
        held = pl.multiple_of((me ^ (me - pick + slot)) * width, width)
        for r in range(levels):
            pred_ref[slot, 0, r] = mine[r * trait_rows : (r + 1) * trait_rows, pl.ds(held, width)][0:traits]
        wide = [
            [messages[f][e][s * trait_rows : (s + 1) * trait_rows, :].astype(F32) for s in range(levels)]
            for e in range(n_blocks)
        ]
        trait = mine[levels * trait_rows : (levels + 1) * trait_rows, :].astype(F32)
        columns = [lax.rem(block - e + n_blocks, n_blocks) for e in range(n_blocks)]
        ones = jnp.ones((8, trait.shape[1]), F32)
        for r in range(levels):
            cross = lax.dot_general(
                ones, wide[0][r] * trait, (((1,), (1,)), ((), ())), precision=HIGHEST, preferred_element_type=F32
            )
            cross_ref[slot, 0, r : r + 1, :] = cross[0:1, 0:traits] / held_rows
            sums = [
                [jnp.sum(wide[0][r] * wide[e][s], axis=1, keepdims=True) / held_rows for s in range(levels)]
                for e in range(n_blocks)
            ]
            for c in range(n_blocks):
                out = jnp.zeros((trait_rows, LANES), F32)
                for e in range(n_blocks):
                    for s in range(levels):
                        out = out + jnp.where((lane == s) & (columns[e] == c), sums[e][s], 0.0)
                for p in range(traits):
                    gram_ref[slot, 0, r, p, c : c + 1, :] = out[p : p + 1, 0:levels]


def per_device(allele_dosage_table, phenotype_values, individual_partition_label, shrink_strengths):
    cores = lax.axis_size("folds")
    sources = lax.axis_size("samples")
    n_blocks = lax.axis_size("blocks")
    own_count = FOLDS // cores
    levels = shrink_strengths.shape[0]
    variants, samples = allele_dosage_table.shape
    traits = phenotype_values.shape[0]
    width = samples // FOLDS
    held_rows = sources * width
    learning_tally = sources * samples - held_rows
    pad_rows = round_up(variants, LANES)
    lead = pad_rows // LANES // 2 * LANES
    size = pad_rows - lead
    trait_rows = round_up(traits, 32)
    half = own_count * width
    vmem = pl.BlockSpec(memory_space=pltpu.VMEM)
    smem = pl.BlockSpec(memory_space=pltpu.SMEM)

    other_lead, own_lead, other_tail, own_tail = pl.pallas_call(
        functools.partial(sort_kernel, own_count, pad_rows),
        out_shape=[jax.ShapeDtypeStruct((lead, half), BF16)] * 2
        + [jax.ShapeDtypeStruct((size + trait_rows, half), BF16)] * 2,
        in_specs=[vmem] * 3,
        out_specs=[vmem] * 4,
        name="sort_samples",
    )(allele_dosage_table, phenotype_values, individual_partition_label.reshape(1, samples))

    def fetch(other):
        return [other] + [
            lax.ppermute(other, "samples", [(i, i ^ d) for i in range(sources)]) for d in range(1, sources)
        ]

    def swap(own, others):
        return [own] + [lax.ppermute(x, "folds", [(i, cores - 1 - i) for i in range(cores)]) for x in others[1:]]

    others_lead = fetch(other_lead)
    owns_lead = swap(own_lead, others_lead)
    others_tail = fetch(other_tail)
    lead_inverse = pl.pallas_call(
        functools.partial(lead_kernel, sources, own_count, learning_tally),
        out_shape=jax.ShapeDtypeStruct((levels, lead, lead), F32),
        in_specs=[smem] + [vmem] * (2 * sources),
        out_specs=vmem,
        scratch_shapes=[pltpu.VMEM((levels, LANES, LANES), F32), pltpu.VMEM((8, LANES), F32)],
        name="invert_lead",
    )(shrink_strengths, *others_lead, *owns_lead)
    lead_inverse, *others_tail[1:] = lax.optimization_barrier((lead_inverse, *others_tail[1:]))
    owns_tail = swap(own_tail, others_tail)
    message = pl.pallas_call(
        functools.partial(tail_kernel, sources, own_count, learning_tally, trait_rows),
        out_shape=jax.ShapeDtypeStruct(((levels + 1) * trait_rows, sources * width), BF16),
        in_specs=[smem] + [vmem] * (1 + 4 * sources),
        out_specs=vmem,
        scratch_shapes=[
            pltpu.VMEM((lead, size + LANES), F32),
            pltpu.VMEM((levels, lead, size + LANES), F32),
            pltpu.VMEM((levels, size, size + LANES), F32),
            pltpu.VMEM((levels, LANES, LANES), F32),
            pltpu.VMEM((8, LANES), F32),
        ],
        name="solve_tail",
    )(shrink_strengths, lead_inverse, *others_lead, *owns_lead, *others_tail, *owns_tail)

    messages = []
    for f in range(own_count):
        for e in range(n_blocks):
            if f == 0 and e == 0:
                messages.append(message)
                continue
            pairs = []
            for s in range(sources):
                source = s - s % own_count + (s % own_count + f) % own_count
                for b in range(n_blocks):
                    pairs.append((source * n_blocks + (b - e) % n_blocks, s * n_blocks + b))
            messages.append(lax.ppermute(message, ("samples", "blocks"), pairs))

    return pl.pallas_call(
        functools.partial(level_kernel, own_count, trait_rows, held_rows),
        out_shape=[
            jax.ShapeDtypeStruct((own_count, 1, levels, traits, width), BF16),
            jax.ShapeDtypeStruct((own_count, 1, levels, traits, n_blocks, levels), F32),
            jax.ShapeDtypeStruct((own_count, 1, levels, traits), F32),
        ],
        in_specs=[vmem] * len(messages),
        out_specs=[vmem] * 3,
        name="level_one",
    )(*messages)


def solution(mesh):
    in_specs = (
        P("blocks", ("groups", "samples")),
        P(None, ("groups", "samples")),
        P(("groups", "samples")),
        P(),
    )
    out_specs = (
        P("folds", "blocks", None, None, ("groups", "samples")),
        P(("groups", "folds"), "blocks", None, None, None, None),
        P(("groups", "folds"), "blocks", None, None),
    )
    return jax.shard_map(
        per_device, mesh=mesh, in_specs=in_specs, out_specs=out_specs, check_vma=False
    )
```

time: 77.1 us -> 75.4 us (0.978)
  waiting for transfers between devices: 29 us -> 17.7 us
  starting transfers between devices: 10.1 us -> 17.4 us
  Pallas kernels: 31.5 us -> 33.9 us
    ppermute x6 -> x12, waiting for transfers between devices: 24.3 us -> 12.8 us  [the longest x6 10.7 us: fetch(): lax.ppermute(other, 'samples', [(i, i ^ d) for i in range(sources)])]
    ppermute x6 -> x12, starting transfers between devices: 6.59 us -> 13.9 us  [the longest x6 12.4 us: fetch(): lax.ppermute(other, 'samples', [(i, i ^ d) for i in range(sources)])]
    slice x3 -> x0, local copies, waits for them, and re-layouts: 3.05 us -> none  [the longest x1 1.54 us: per_device(): level_cross = level[:, None, :, :traits, n_blocks * levels]]
    pallas_call x0 -> x2, local copies, waits for them, and re-layouts: none -> 2.96 us  [per_device(): pl.pallas_call(functools.partial(level_kernel, own_count, trait_rows, hel...]
    pallas_call x3 -> x4, Pallas kernels: 31.5 us -> 33.9 us  [the longest x1 17.2 us: per_device(): pl.pallas_call(functools.partial(tail_kernel, sources, own_count, learnin...]
    unnamed x21 -> x30, local copies, waits for them, and re-layouts: 2.52 us -> 2.37 us
  transfers between devices with their start and end apart: 9 -> 15, of which waited for: 7 -> 10; matrix products, arithmetic and copies ran while one was open for 0% -> 0% of each run, Pallas kernels for 0% -> 16%
where the time goes in v2:
time: 75.4 us; the launch traced here: 75.1 us
  Pallas kernels  33.9 us (45%)
  waiting for transfers between devices  17.7 us (23%)
  starting transfers between devices  17.4 us (23%)
  local copies, waits for them, and re-layouts  5.33 us (7%)
    pallas_call x1, Pallas kernels, per_device(): pl.pallas_call(functools.partial(tail_kernel, sources, own_count, learnin...  17.2 us
    ppermute x6, starting transfers between devices, fetch(): lax.ppermute(other, 'samples', [(i, i ^ d) for i in range(sources)])  12.4 us
    pallas_call x1, Pallas kernels, per_device(): pl.pallas_call(functools.partial(lead_kernel, sources, own_count, learnin...  12.2 us
    ppermute x6, waiting for transfers between devices, fetch(): lax.ppermute(other, 'samples', [(i, i ^ d) for i in range(sources)])  10.7 us
    ppermute x3, waiting for transfers between devices, per_device(): messages.append(lax.ppermute(message, ('samples', 'blocks'), pairs))  4.93 us
    ppermute x3, starting transfers between devices, per_device(): messages.append(lax.ppermute(message, ('samples', 'blocks'), pairs))  3.52 us
    pallas_call x2, local copies, waits for them, and re-layouts, per_device(): pl.pallas_call(functools.partial(level_kernel, own_count, trait_rows, hel...  2.96 us
    pallas_call x1, Pallas kernels, per_device(): pl.pallas_call(functools.partial(sort_kernel, own_count, pad_rows), out_s...  2.53 us
  transfers between devices with their start and end apart: 15, of which 10 were waited for; matrix products, arithmetic and copies ran while one was open for 0% of the time, Pallas kernels for 16%

profile of v2, /device:TPU:0, one launch (start us, length us, event | category | flops | bytes accessed | tf_op | source)
XLA Modules:
  0.0 75.1 jit_solution(16996418747284423502)
XLA Ops:
  0.6 2.5 %sort_samples.1 = (bf16[256,256]{1,0:T(8,128)(2,1)}, bf16[256,256]{1,0:T(8,128)(2,1)}, bf16[288,256]{1,0:T(8,128)(2,1)}, bf16[288,256]{1,0:T(8,128)(2,1)}) custom-call(bf16[500,512]{1,0:T(8,128)(2,1)} %geno_ref.1, bf16[20,512]{1,0:T(8,128)(2,1)} %trait_ref.1, s32[1,512]{1,0:T(1,128)} %bitcast.1), custom_call_target="tpu_custom_call" | custom-call | tf_op jit(solution)/shard_map/sort_samples/pallas_call | solution.py:315
  3.2 5.1 %collective-permute-start.2 = (bf16[256,256]{1,0:T(8,128)(2,1)}, bf16[256,256]{1,0:T(8,128)(2,1)S(1)}, u32[]{:S(2)}, u32[]{:S(2)}) collective-permute-start(bf16[256,256]{1,0:T(8,128)(2,1)} %get-tuple-element.11.refs_1_.refs_2_), channel_id=1, source_target_pairs={{0,12},{4,8},{8,4},{12,0},{1,13},{5,9},{9,5},{13,1},{2,14},{6,10},... | collective-permute-start | bytes 393224 | tf_op jit(solution)/shard_map/ppermute | solution.py:326
  8.2 0.0 collective-permute-start.1
  8.2 0.6 collective-permute-start
  8.8 4.1 %collective-permute-done.2.refs_4_.refs_5_ = bf16[256,256]{1,0:T(8,128)(2,1)S(1)} collective-permute-done((bf16[256,256]{1,0:T(8,128)(2,1)}, bf16[256,256]{1,0:T(8,128)(2,1)S(1)}, u32[]{:S(2)}, u32[]{:S(2)}) %collective-permute-start.2) | collective-permute-done | bytes 131104 | tf_op jit(solution)/shard_map/ppermute | solution.py:326
  12.9 0.0 collective-permute-start.5
  12.9 3.8 %collective-permute-start.8 = (bf16[288,256]{1,0:T(8,128)(2,1)}, bf16[288,256]{1,0:T(8,128)(2,1)S(1)}, u32[]{:S(2)}, u32[]{:S(2)}) collective-permute-start(bf16[288,256]{1,0:T(8,128)(2,1)} %get-tuple-element.13.refs_10_), channel_id=1, source_target_pairs={{0,12},{4,8},{8,4},{12,0},{1,13},{5,9},{9,5},{13,1},{2,14},{6,10},... | collective-permute-start | bytes 442376 | tf_op jit(solution)/shard_map/ppermute | solution.py:326
  16.7 3.0 %collective-permute-start.7 = (bf16[288,256]{1,0:T(8,128)(2,1)}, bf16[288,256]{1,0:T(8,128)(2,1)S(1)}, u32[]{:S(2)}, u32[]{:S(2)}) collective-permute-start(bf16[288,256]{1,0:T(8,128)(2,1)} %get-tuple-element.13.refs_10_), channel_id=1, source_target_pairs={{0,8},{4,12},{8,0},{12,4},{1,9},{5,13},{9,1},{13,5},{2,10},{6,14},... | collective-permute-start | bytes 442376 | tf_op jit(solution)/shard_map/ppermute | solution.py:326
  19.7 6.6 %collective-permute-done.1.refs_3_.refs_4_ = bf16[256,256]{1,0:T(8,128)(2,1)S(1)} collective-permute-done((bf16[256,256]{1,0:T(8,128)(2,1)}, bf16[256,256]{1,0:T(8,128)(2,1)S(1)}, u32[]{:S(2)}, u32[]{:S(2)}) %collective-permute-start.1) | collective-permute-done | bytes 131104 | tf_op jit(solution)/shard_map/ppermute | solution.py:326
  26.3 0.0 collective-permute-start.6
  26.3 0.0 collective-permute-done.refs_2_.refs_3_
  26.3 0.0 copy-start.2
  26.3 0.1 collective-permute-start.4
  26.4 0.0 collective-permute-done.5.refs_8_.refs_9_
  26.4 0.0 copy-start.3
  26.4 0.5 collective-permute-start.3
  26.9 0.8 %collective-permute-done.4.refs_7_.refs_8_ = bf16[256,256]{1,0:T(8,128)(2,1)S(1)} collective-permute-done((bf16[256,256]{1,0:T(8,128)(2,1)S(1)}, bf16[256,256]{1,0:T(8,128)(2,1)S(1)}, u32[]{:S(2)}, u32[]{:S(2)}) %collective-permute-start.4) | collective-permute-done | bytes 131104 | tf_op jit(solution)/shard_map/ppermute | solution.py:330
  27.7 0.2 collective-permute-done.3.refs_6_.refs_7_
  27.9 0.0 copy-done.2
  27.9 0.4 copy-done.4
  28.4 0.2 copy-done.5
  28.5 12.2 %invert_lead.1.refs_1_ = f32[2,256,256]{2,1,0:T(8,128)} custom-call(f32[2]{0:T(128)} %refs_0_.3, bf16[256,256]{1,0:T(8,128)(2,1)} %get-tuple-element.11.refs_1_.refs_2_, bf16[256,256]{1,0:T(8,128)(2,1)} %copy-done.2, bf16[256,256]{1,0:T(8,128)(2,1)} %copy-done.1, bf16[256,256]{1,0:T(8,128)(2,1)} %copy-done, ...), custom_call_target="tpu_custom_call" | custom-call | tf_op jit(solution)/shard_map/invert_lead/pallas_call | solution.py:335
  40.7 0.0 collective-permute-done.8.refs_13_
  40.7 0.0 collective-permute-done.7.refs_12_
  40.8 0.0 collective-permute-done.6.refs_11_
  40.8 0.4 collective-permute-start.9
  41.2 0.2 collective-permute-start.10
  41.4 0.3 collective-permute-start.11
  41.7 0.5 collective-permute-done.9.refs_15_
  42.2 0.3 collective-permute-done.10.refs_16_
  42.5 0.2 collective-permute-done.11.refs_17_
  42.8 0.0 copy-done.7
  42.8 0.1 copy-done.9
  42.9 0.3 copy-done.10
  43.2 0.2 copy-done.11
  43.4 17.2 %solve_tail.1.refs_0_ = bf16[96,512]{1,0:T(8,128)(2,1)} custom-call(f32[2]{0:T(128)} %refs_0_.3, f32[2,256,256]{2,1,0:T(8,128)} %invert_lead.1.refs_1_, bf16[256,256]{1,0:T(8,128)(2,1)} %get-tuple-element.11.refs_1_.refs_2_, bf16[256,256]{1,0:T(8,128)(2,1)} %copy-done.2, bf16[256,256]{1,0:T(8,128)(2,1)} %copy-done.1, bf16[256,256]{1,0:T(8,128)(2,1)} %copy-done, ...), custom_call_target="tpu_custom_call" | custom-call | tf_op jit(solution)/shard_map/solve_tail/pallas_call | solution.py:345
  60.7 2.9 %collective-permute-start.14 = (bf16[96,512]{1,0:T(8,128)(2,1)}, bf16[96,512]{1,0:T(8,128)(2,1)S(1)}, u32[]{:S(2)}, u32[]{:S(2)}) collective-permute-start(bf16[96,512]{1,0:T(8,128)(2,1)} %solve_tail.1.refs_0_), channel_id=1, source_target_pairs={{6,0},{4,2},{2,4},{0,6},{14,8},{12,10},{10,12},{8,14},{7,1},{5,3},... | collective-permute-start | bytes 294920 | tf_op jit(solution)/shard_map/ppermute | solution.py:371
  63.5 0.1 collective-permute-start.13
  63.6 0.6 collective-permute-start.12
  64.2 3.3 %collective-permute-done.14.refs_3_ = bf16[96,512]{1,0:T(8,128)(2,1)S(1)} collective-permute-done((bf16[96,512]{1,0:T(8,128)(2,1)}, bf16[96,512]{1,0:T(8,128)(2,1)S(1)}, u32[]{:S(2)}, u32[]{:S(2)}) %collective-permute-start.14) | collective-permute-done | bytes 98336 | tf_op jit(solution)/shard_map/ppermute | solution.py:371
  67.4 1.5 %collective-permute-done.13.refs_2_ = bf16[96,512]{1,0:T(8,128)(2,1)S(1)} collective-permute-done((bf16[96,512]{1,0:T(8,128)(2,1)}, bf16[96,512]{1,0:T(8,128)(2,1)S(1)}, u32[]{:S(2)}, u32[]{:S(2)}) %collective-permute-start.13) | collective-permute-done | bytes 98336 | tf_op jit(solution)/shard_map/ppermute | solution.py:371
  68.9 0.2 collective-permute-done.12.refs_1_
  69.1 0.0 copy-done.12
  69.1 0.4 copy-done.13
  69.5 0.6 copy-done.14
  70.2 2.0 %level_one.1 = (bf16[2,1,2,20,128]{4,3,2,1,0:T(8,128)(2,1)}, f32[2,1,2,20,2,2]{5,4,3,2,1,0:T(2,128)}, f32[2,1,2,20]{3,2,1,0:T(2,128)}) custom-call(bf16[96,512]{1,0:T(8,128)(2,1)} %solve_tail.1.refs_0_, bf16[96,512]{1,0:T(8,128)(2,1)} %copy-done.14, bf16[96,512]{1,0:T(8,128)(2,1)} %copy-done.13, bf16[96,512]{1,0:T(8,128)(2,1)} %copy-done.12), custom_call_target="tpu_custom_call" | custom-call | tf_op jit(solution)/shard_map/level_one/pallas_call | solution.py:373
  72.1 1.4 %copy.7 = bf16[2,1,2,20,128]{4,2,3,1,0:T(2,128)(2,1)} copy(bf16[2,1,2,20,128]{4,3,2,1,0:T(8,128)(2,1)} %get-tuple-element.19) | data formatting | bytes 40960 | tf_op jit(solution)/shard_map/level_one/pallas_call | solution.py:373
  73.5 1.6 %copy.8 = f32[2,1,2,20,2,2]{3,5,4,2,1,0:T(2,128)} copy(f32[2,1,2,20,2,2]{5,4,3,2,1,0:T(2,128)} %get-tuple-element.20) | data formatting | bytes 2560 | tf_op jit(solution)/shard_map/level_one/pallas_call | solution.py:373
  (18 shorter events, 0.0 us)
Async XLA Ops:
  3.2 9.7 %collective-permute-start.2 = (bf16[256,256]{1,0:T(8,128)(2,1)}, bf16[256,256]{1,0:T(8,128)(2,1)S(1)}, u32[]{:S(2)}, u32[]{:S(2)}) collective-permute-start(bf16[256,256]{1,0:T(8,128)(2,1)} %get-tuple-element.11.refs_1_.refs_2_), channel_id=1, source_target_pairs={{0,12},{4,8},{8,4},{12,0},{1,13},{5,9},{9,5},{13,1},{2,14},{6,10},... | collective-permute-start | bytes 393224 | tf_op jit(solution)/shard_map/ppermute | solution.py:326
  8.2 18.0 %collective-permute-start.1 = (bf16[256,256]{1,0:T(8,128)(2,1)}, bf16[256,256]{1,0:T(8,128)(2,1)S(1)}, u32[]{:S(2)}, u32[]{:S(2)}) collective-permute-start(bf16[256,256]{1,0:T(8,128)(2,1)} %get-tuple-element.11.refs_1_.refs_2_), channel_id=1, source_target_pairs={{0,8},{4,12},{8,0},{12,4},{1,9},{5,13},{9,1},{13,5},{2,10},{6,14},... | collective-permute-start | bytes 393224 | tf_op jit(solution)/shard_map/ppermute | solution.py:326
  8.2 18.0 %collective-permute-start = (bf16[256,256]{1,0:T(8,128)(2,1)}, bf16[256,256]{1,0:T(8,128)(2,1)S(1)}, u32[]{:S(2)}, u32[]{:S(2)}) collective-permute-start(bf16[256,256]{1,0:T(8,128)(2,1)} %get-tuple-element.11.refs_1_.refs_2_), channel_id=1, source_target_pairs={{0,4},{4,0},{8,12},{12,8},{1,5},{5,1},{9,13},{13,9},{2,6},{6,2},{1... | collective-permute-start | bytes 393224 | tf_op jit(solution)/shard_map/ppermute | solution.py:326
  12.9 15.0 %copy-start = (bf16[256,256]{1,0:T(8,128)(2,1)}, bf16[256,256]{1,0:T(8,128)(2,1)S(1)}, u32[]{:S(2)}) copy-start(bf16[256,256]{1,0:T(8,128)(2,1)S(1)} %collective-permute-done.2.refs_4_.refs_5_) | copy-start | bytes 393220
  12.9 13.5 %collective-permute-start.5 = (bf16[256,256]{1,0:T(8,128)(2,1)S(1)}, bf16[256,256]{1,0:T(8,128)(2,1)S(1)}, u32[]{:S(2)}, u32[]{:S(2)}) collective-permute-start(bf16[256,256]{1,0:T(8,128)(2,1)S(1)} %collective-permute-done.2.refs_4_.refs_5_), channel_id=1, source_target_pairs={{0,1},{1,0},{2,3},{3,2},{4,5},{5,4},{6,7},{7,6},{8,9},{9,8},{10,11... | collective-permute-start | bytes 393224 | tf_op jit(solution)/shard_map/ppermute | solution.py:330
  12.9 27.8 %collective-permute-start.8 = (bf16[288,256]{1,0:T(8,128)(2,1)}, bf16[288,256]{1,0:T(8,128)(2,1)S(1)}, u32[]{:S(2)}, u32[]{:S(2)}) collective-permute-start(bf16[288,256]{1,0:T(8,128)(2,1)} %get-tuple-element.13.refs_10_), channel_id=1, source_target_pairs={{0,12},{4,8},{8,4},{12,0},{1,13},{5,9},{9,5},{13,1},{2,14},{6,10},... | collective-permute-start | bytes 442376 | tf_op jit(solution)/shard_map/ppermute | solution.py:326
  16.7 24.1 %collective-permute-start.7 = (bf16[288,256]{1,0:T(8,128)(2,1)}, bf16[288,256]{1,0:T(8,128)(2,1)S(1)}, u32[]{:S(2)}, u32[]{:S(2)}) collective-permute-start(bf16[288,256]{1,0:T(8,128)(2,1)} %get-tuple-element.13.refs_10_), channel_id=1, source_target_pairs={{0,8},{4,12},{8,0},{12,4},{1,9},{5,13},{9,1},{13,5},{2,10},{6,14},... | collective-permute-start | bytes 442376 | tf_op jit(solution)/shard_map/ppermute | solution.py:326
  26.3 1.6 %copy-start.1 = (bf16[256,256]{1,0:T(8,128)(2,1)}, bf16[256,256]{1,0:T(8,128)(2,1)S(1)}, u32[]{:S(2)}) copy-start(bf16[256,256]{1,0:T(8,128)(2,1)S(1)} %collective-permute-done.1.refs_3_.refs_4_) | copy-start | bytes 393220
  26.3 14.5 %collective-permute-start.6 = (bf16[288,256]{1,0:T(8,128)(2,1)}, bf16[288,256]{1,0:T(8,128)(2,1)S(1)}, u32[]{:S(2)}, u32[]{:S(2)}) collective-permute-start(bf16[288,256]{1,0:T(8,128)(2,1)} %get-tuple-element.13.refs_10_), channel_id=1, source_target_pairs={{0,4},{4,0},{8,12},{12,8},{1,5},{5,1},{9,13},{13,9},{2,6},{6,2},{1... | collective-permute-start | bytes 442376 | tf_op jit(solution)/shard_map/ppermute | solution.py:326
  26.3 1.6 %copy-start.2 = (bf16[256,256]{1,0:T(8,128)(2,1)}, bf16[256,256]{1,0:T(8,128)(2,1)S(1)}, u32[]{:S(2)}) copy-start(bf16[256,256]{1,0:T(8,128)(2,1)S(1)} %collective-permute-done.refs_2_.refs_3_) | copy-start | bytes 393220
  26.3 1.4 %collective-permute-start.4 = (bf16[256,256]{1,0:T(8,128)(2,1)S(1)}, bf16[256,256]{1,0:T(8,128)(2,1)S(1)}, u32[]{:S(2)}, u32[]{:S(2)}) collective-permute-start(bf16[256,256]{1,0:T(8,128)(2,1)S(1)} %collective-permute-done.1.refs_3_.refs_4_), channel_id=1, source_target_pairs={{0,1},{1,0},{2,3},{3,2},{4,5},{5,4},{6,7},{7,6},{8,9},{9,8},{10,11... | collective-permute-start | bytes 393224 | tf_op jit(solution)/shard_map/ppermute | solution.py:330
  26.4 1.5 %copy-start.3 = (bf16[256,256]{1,0:T(8,128)(2,1)}, bf16[256,256]{1,0:T(8,128)(2,1)S(1)}, u32[]{:S(2)}) copy-start(bf16[256,256]{1,0:T(8,128)(2,1)S(1)} %collective-permute-done.5.refs_8_.refs_9_) | copy-start | bytes 393220
  26.4 1.5 %collective-permute-start.3 = (bf16[256,256]{1,0:T(8,128)(2,1)S(1)}, bf16[256,256]{1,0:T(8,128)(2,1)S(1)}, u32[]{:S(2)}, u32[]{:S(2)}) collective-permute-start(bf16[256,256]{1,0:T(8,128)(2,1)S(1)} %collective-permute-done.refs_2_.refs_3_), channel_id=1, source_target_pairs={{0,1},{1,0},{2,3},{3,2},{4,5},{5,4},{6,7},{7,6},{8,9},{9,8},{10,11... | collective-permute-start | bytes 393224 | tf_op jit(solution)/shard_map/ppermute | solution.py:330
  27.7 0.7 copy-start.4
  27.9 0.6 copy-start.5
  40.7 2.0 %copy-start.6 = (bf16[288,256]{1,0:T(8,128)(2,1)}, bf16[288,256]{1,0:T(8,128)(2,1)S(1)}, u32[]{:S(2)}) copy-start(bf16[288,256]{1,0:T(8,128)(2,1)S(1)} %collective-permute-done.8.refs_13_) | copy-start | bytes 442372
  40.7 2.0 %copy-start.7 = (bf16[288,256]{1,0:T(8,128)(2,1)}, bf16[288,256]{1,0:T(8,128)(2,1)S(1)}, u32[]{:S(2)}) copy-start(bf16[288,256]{1,0:T(8,128)(2,1)S(1)} %collective-permute-done.7.refs_12_) | copy-start | bytes 442372
  40.8 2.0 %copy-start.8 = (bf16[288,256]{1,0:T(8,128)(2,1)}, bf16[288,256]{1,0:T(8,128)(2,1)S(1)}, u32[]{:S(2)}) copy-start(bf16[288,256]{1,0:T(8,128)(2,1)S(1)} %collective-permute-done.6.refs_11_) | copy-start | bytes 442372
  40.8 1.4 %collective-permute-start.9 = (bf16[288,256]{1,0:T(8,128)(2,1)S(1)}, bf16[288,256]{1,0:T(8,128)(2,1)S(1)}, u32[]{:S(2)}, u32[]{:S(2)}) collective-permute-start(bf16[288,256]{1,0:T(8,128)(2,1)S(1)} %collective-permute-done.6.refs_11_), channel_id=1, source_target_pairs={{0,1},{1,0},{2,3},{3,2},{4,5},{5,4},{6,7},{7,6},{8,9},{9,8},{10,11... | collective-permute-start | bytes 442376 | tf_op jit(solution)/shard_map/ppermute | solution.py:330
  41.2 1.4 %collective-permute-start.10 = (bf16[288,256]{1,0:T(8,128)(2,1)S(1)}, bf16[288,256]{1,0:T(8,128)(2,1)S(1)}, u32[]{:S(2)}, u32[]{:S(2)}) collective-permute-start(bf16[288,256]{1,0:T(8,128)(2,1)S(1)} %collective-permute-done.7.refs_12_), channel_id=1, source_target_pairs={{0,1},{1,0},{2,3},{3,2},{4,5},{5,4},{6,7},{7,6},{8,9},{9,8},{10,11... | collective-permute-start | bytes 442376 | tf_op jit(solution)/shard_map/ppermute | solution.py:330
  41.4 1.4 %collective-permute-start.11 = (bf16[288,256]{1,0:T(8,128)(2,1)S(1)}, bf16[288,256]{1,0:T(8,128)(2,1)S(1)}, u32[]{:S(2)}, u32[]{:S(2)}) collective-permute-start(bf16[288,256]{1,0:T(8,128)(2,1)S(1)} %collective-permute-done.8.refs_13_), channel_id=1, source_target_pairs={{0,1},{1,0},{2,3},{3,2},{4,5},{5,4},{6,7},{7,6},{8,9},{9,8},{10,11... | collective-permute-start | bytes 442376 | tf_op jit(solution)/shard_map/ppermute | solution.py:330
  42.2 0.6 copy-start.9
  42.5 0.7 copy-start.10
  42.7 0.7 copy-start.11
  60.7 6.8 %collective-permute-start.14 = (bf16[96,512]{1,0:T(8,128)(2,1)}, bf16[96,512]{1,0:T(8,128)(2,1)S(1)}, u32[]{:S(2)}, u32[]{:S(2)}) collective-permute-start(bf16[96,512]{1,0:T(8,128)(2,1)} %solve_tail.1.refs_0_), channel_id=1, source_target_pairs={{6,0},{4,2},{2,4},{0,6},{14,8},{12,10},{10,12},{8,14},{7,1},{5,3},... | collective-permute-start | bytes 294920 | tf_op jit(solution)/shard_map/ppermute | solution.py:371
  63.5 5.4 %collective-permute-start.13 = (bf16[96,512]{1,0:T(8,128)(2,1)}, bf16[96,512]{1,0:T(8,128)(2,1)S(1)}, u32[]{:S(2)}, u32[]{:S(2)}) collective-permute-start(bf16[96,512]{1,0:T(8,128)(2,1)} %solve_tail.1.refs_0_), channel_id=1, source_target_pairs={{4,0},{6,2},{0,4},{2,6},{12,8},{14,10},{8,12},{10,14},{5,1},{7,3},... | collective-permute-start | bytes 294920 | tf_op jit(solution)/shard_map/ppermute | solution.py:371
  63.6 5.5 %collective-permute-start.12 = (bf16[96,512]{1,0:T(8,128)(2,1)}, bf16[96,512]{1,0:T(8,128)(2,1)S(1)}, u32[]{:S(2)}, u32[]{:S(2)}) collective-permute-start(bf16[96,512]{1,0:T(8,128)(2,1)} %solve_tail.1.refs_0_), channel_id=1, source_target_pairs={{2,0},{0,2},{6,4},{4,6},{10,8},{8,10},{14,12},{12,14},{3,1},{1,3},... | collective-permute-start | bytes 294920 | tf_op jit(solution)/shard_map/ppermute | solution.py:371
  67.4 1.7 %copy-start.12 = (bf16[96,512]{1,0:T(8,128)(2,1)}, bf16[96,512]{1,0:T(8,128)(2,1)S(1)}, u32[]{:S(2)}) copy-start(bf16[96,512]{1,0:T(8,128)(2,1)S(1)} %collective-permute-done.14.refs_3_) | copy-start | bytes 294916
  68.9 0.6 copy-start.13
  69.5 0.6 copy-start.14

commit v3 on v2

--- a/solution.py
+++ b/solution.py
@@ -257,7 +257,7 @@
     pred_ref, gram_ref, cross_ref = refs[-3:]
     n_blocks = (len(refs) - 3) // own_count
     messages = [refs[f * n_blocks : (f + 1) * n_blocks] for f in range(own_count)]
-    levels, traits, width = pred_ref.shape[2:]
+    traits, levels, width = pred_ref.shape[2:]
     me = lax.axis_index("samples")
     block = lax.axis_index("blocks")
     pick = lax.rem(me, own_count)
@@ -266,31 +266,27 @@
         slot = lax.rem(pick + f, own_count)
         mine = messages[f][0]
         held = pl.multiple_of((me ^ (me - pick + slot)) * width, width)
-        for r in range(levels):
-            pred_ref[slot, 0, r] = mine[r * trait_rows : (r + 1) * trait_rows, pl.ds(held, width)][0:traits]
+        own = [
+            mine[r * trait_rows : (r + 1) * trait_rows, pl.ds(held, width)].astype(F32)[0:traits]
+            for r in range(levels)
+        ]
+        pred_ref[slot, 0] = jnp.stack(own, axis=1).astype(BF16)
         wide = [
             [messages[f][e][s * trait_rows : (s + 1) * trait_rows, :].astype(F32) for s in range(levels)]
             for e in range(n_blocks)
         ]
         trait = mine[levels * trait_rows : (levels + 1) * trait_rows, :].astype(F32)
-        columns = [lax.rem(block - e + n_blocks, n_blocks) for e in range(n_blocks)]
-        ones = jnp.ones((8, trait.shape[1]), F32)
         for r in range(levels):
-            cross = lax.dot_general(
-                ones, wide[0][r] * trait, (((1,), (1,)), ((), ())), precision=HIGHEST, preferred_element_type=F32
-            )
-            cross_ref[slot, 0, r : r + 1, :] = cross[0:1, 0:traits] / held_rows
-            sums = [
-                [jnp.sum(wide[0][r] * wide[e][s], axis=1, keepdims=True) / held_rows for s in range(levels)]
-                for e in range(n_blocks)
-            ]
+            out = jnp.where(lane == n_blocks * levels, jnp.sum(wide[0][r] * trait, axis=1, keepdims=True), 0.0)
+            for e in range(n_blocks):
+                column = lax.rem(block - e + n_blocks, n_blocks) * levels
+                for s in range(levels):
+                    total = jnp.sum(wide[0][r] * wide[e][s], axis=1, keepdims=True)
+                    out = out + jnp.where(lane == column + s, total, 0.0)
+            rows = jnp.transpose(out) / held_rows
             for c in range(n_blocks):
-                out = jnp.zeros((trait_rows, LANES), F32)
-                for e in range(n_blocks):
-                    for s in range(levels):
-                        out = out + jnp.where((lane == s) & (columns[e] == c), sums[e][s], 0.0)
-                for p in range(traits):
-                    gram_ref[slot, 0, r, p, c : c + 1, :] = out[p : p + 1, 0:levels]
+                gram_ref[slot, 0, r, c] = rows[c * levels : (c + 1) * levels, 0:traits]
+            cross_ref[slot, 0, r : r + 1, :] = rows[n_blocks * levels : n_blocks * levels + 1, 0:traits]
 
 
 def per_device(allele_dosage_table, phenotype_values, individual_partition_label, shrink_strengths):
@@ -331,6 +327,7 @@
 
     others_lead = fetch(other_lead)
     owns_lead = swap(own_lead, others_lead)
+    other_tail, *others_lead[1:] = lax.optimization_barrier((other_tail, *others_lead[1:]))
     others_tail = fetch(other_tail)
     lead_inverse = pl.pallas_call(
         functools.partial(lead_kernel, sources, own_count, learning_tally),
@@ -370,17 +367,18 @@
                     pairs.append((source * n_blocks + (b - e) % n_blocks, s * n_blocks + b))
             messages.append(lax.ppermute(message, ("samples", "blocks"), pairs))
 
-    return pl.pallas_call(
+    preds, gram, cross = pl.pallas_call(
         functools.partial(level_kernel, own_count, trait_rows, held_rows),
         out_shape=[
-            jax.ShapeDtypeStruct((own_count, 1, levels, traits, width), BF16),
-            jax.ShapeDtypeStruct((own_count, 1, levels, traits, n_blocks, levels), F32),
+            jax.ShapeDtypeStruct((own_count, 1, traits, levels, width), BF16),
+            jax.ShapeDtypeStruct((own_count, 1, levels, n_blocks, levels, traits), F32),
             jax.ShapeDtypeStruct((own_count, 1, levels, traits), F32),
         ],
         in_specs=[vmem] * len(messages),
         out_specs=[vmem] * 3,
         name="level_one",
     )(*messages)
+    return jnp.swapaxes(preds, 2, 3), jnp.moveaxis(gram, 5, 3), cross
 
 
 def solution(mesh):

time: 75.4 us -> 69.9 us (0.927)
  local copies, waits for them, and re-layouts: 5.33 us -> 2.57 us
  starting transfers between devices: 17.4 us -> 15 us
    pallas_call x2 -> x0, local copies, waits for them, and re-layouts: 2.96 us -> none  [per_device(): pl.pallas_call(functools.partial(level_kernel, own_count, trait_rows, hel...]
    ppermute x6, starting transfers between devices: 12.4 us -> 10.1 us  [fetch(): lax.ppermute(other, 'samples', [(i, i ^ d) for i in range(sources)])]
  transfers between devices with their start and end apart: 15 -> 15, of which waited for: 10 -> 9; matrix products, arithmetic and copies ran while one was open for 0% -> 0% of each run, Pallas kernels for 16% -> 17%
where the time goes in v3:
time: 69.9 us; the launch traced here: 69.7 us
  Pallas kernels  33.8 us (48%)
  waiting for transfers between devices  17.6 us (25%)
  starting transfers between devices  15 us (21%)
  local copies, waits for them, and re-layouts  2.57 us (4%)
  between operations  0.71 us (1%)
    pallas_call x1, Pallas kernels, per_device(): pl.pallas_call(functools.partial(tail_kernel, sources, own_count, learnin...  17.2 us
    pallas_call x1, Pallas kernels, per_device(): pl.pallas_call(functools.partial(lead_kernel, sources, own_count, learnin...  12.2 us
    ppermute x6, waiting for transfers between devices, fetch(): lax.ppermute(other, 'samples', [(i, i ^ d) for i in range(sources)])  10.7 us
    ppermute x6, starting transfers between devices, fetch(): lax.ppermute(other, 'samples', [(i, i ^ d) for i in range(sources)])  10.1 us
    ppermute x3, waiting for transfers between devices, per_device(): messages.append(lax.ppermute(message, ('samples', 'blocks'), pairs))  4.75 us
    ppermute x3, starting transfers between devices, per_device(): messages.append(lax.ppermute(message, ('samples', 'blocks'), pairs))  3.49 us
    unnamed x30, local copies, waits for them, and re-layouts  2.57 us
    pallas_call x1, Pallas kernels, per_device(): pl.pallas_call(functools.partial(sort_kernel, own_count, pad_rows), out_s...  2.53 us
  transfers between devices with their start and end apart: 15, of which 9 were waited for; matrix products, arithmetic and copies ran while one was open for 0% of the time, Pallas kernels for 17%

profile of v3, /device:TPU:0, one launch (start us, length us, event | category | flops | bytes accessed | tf_op | source)
XLA Modules:
  0.0 69.7 jit_solution(15345940368686345586)
XLA Ops:
  0.6 2.5 %sort_samples.1 = (bf16[256,256]{1,0:T(8,128)(2,1)}, bf16[256,256]{1,0:T(8,128)(2,1)}, bf16[288,256]{1,0:T(8,128)(2,1)}, bf16[288,256]{1,0:T(8,128)(2,1)}) custom-call(bf16[500,512]{1,0:T(8,128)(2,1)} %geno_ref.1, bf16[20,512]{1,0:T(8,128)(2,1)} %trait_ref.1, s32[1,512]{1,0:T(1,128)} %bitcast.3), custom_call_target="tpu_custom_call" | custom-call | tf_op jit(solution)/shard_map/sort_samples/pallas_call | solution.py:311
  3.2 5.1 %collective-permute-start.2 = (bf16[256,256]{1,0:T(8,128)(2,1)}, bf16[256,256]{1,0:T(8,128)(2,1)S(1)}, u32[]{:S(2)}, u32[]{:S(2)}) collective-permute-start(bf16[256,256]{1,0:T(8,128)(2,1)} %get-tuple-element.18.refs_1_.refs_2_), channel_id=1, source_target_pairs={{0,12},{4,8},{8,4},{12,0},{1,13},{5,9},{9,5},{13,1},{2,14},{6,10},... | collective-permute-start | bytes 393224 | tf_op jit(solution)/shard_map/ppermute | solution.py:322
  8.2 0.0 collective-permute-start.1
  8.2 0.6 collective-permute-start
  8.8 4.1 %collective-permute-done.2.refs_4_.refs_5_ = bf16[256,256]{1,0:T(8,128)(2,1)S(1)} collective-permute-done((bf16[256,256]{1,0:T(8,128)(2,1)}, bf16[256,256]{1,0:T(8,128)(2,1)S(1)}, u32[]{:S(2)}, u32[]{:S(2)}) %collective-permute-start.2) | collective-permute-done | bytes 131104 | tf_op jit(solution)/shard_map/ppermute | solution.py:322
  12.9 0.0 collective-permute-start.5
  12.9 6.6 %collective-permute-done.1.refs_3_.refs_4_ = bf16[256,256]{1,0:T(8,128)(2,1)S(1)} collective-permute-done((bf16[256,256]{1,0:T(8,128)(2,1)}, bf16[256,256]{1,0:T(8,128)(2,1)S(1)}, u32[]{:S(2)}, u32[]{:S(2)}) %collective-permute-start.1) | collective-permute-done | bytes 131104 | tf_op jit(solution)/shard_map/ppermute | solution.py:322
  19.5 0.0 collective-permute-done.refs_2_.refs_3_
  19.5 2.5 %collective-permute-start.8 = (bf16[288,256]{1,0:T(8,128)(2,1)}, bf16[288,256]{1,0:T(8,128)(2,1)S(1)}, u32[]{:S(2)}, u32[]{:S(2)}) collective-permute-start(bf16[288,256]{1,0:T(8,128)(2,1)} %get-tuple-element.24.refs_10_), channel_id=1, source_target_pairs={{0,12},{4,8},{8,4},{12,0},{1,13},{5,9},{9,5},{13,1},{2,14},{6,10},... | collective-permute-start | bytes 442376 | tf_op jit(solution)/shard_map/ppermute | solution.py:322
  22.1 0.0 collective-permute-start.7
  22.1 1.9 %collective-permute-start.6 = (bf16[288,256]{1,0:T(8,128)(2,1)}, bf16[288,256]{1,0:T(8,128)(2,1)S(1)}, u32[]{:S(2)}, u32[]{:S(2)}) collective-permute-start(bf16[288,256]{1,0:T(8,128)(2,1)} %get-tuple-element.24.refs_10_), channel_id=1, source_target_pairs={{0,4},{4,0},{8,12},{12,8},{1,5},{5,1},{9,13},{13,9},{2,6},{6,2},{1... | collective-permute-start | bytes 442376 | tf_op jit(solution)/shard_map/ppermute | solution.py:322
  24.0 0.0 collective-permute-start.4
  24.0 0.0 collective-permute-done.5.refs_8_.refs_9_
  24.0 0.5 collective-permute-start.3
  24.5 0.8 %collective-permute-done.4.refs_7_.refs_8_ = bf16[256,256]{1,0:T(8,128)(2,1)S(1)} collective-permute-done((bf16[256,256]{1,0:T(8,128)(2,1)S(1)}, bf16[256,256]{1,0:T(8,128)(2,1)S(1)}, u32[]{:S(2)}, u32[]{:S(2)}) %collective-permute-start.4) | collective-permute-done | bytes 131104 | tf_op jit(solution)/shard_map/ppermute | solution.py:326
  25.3 0.2 collective-permute-done.3.refs_6_.refs_7_
  25.5 0.0 copy-done
  25.5 0.0 copy-done.1
  25.5 0.0 copy-done.2
  25.5 0.0 copy-done.3
  25.5 0.4 copy-done.4
  26.0 0.2 copy-done.5
  26.2 12.2 %invert_lead.1.refs_1_ = f32[2,256,256]{2,1,0:T(8,128)} custom-call(f32[2]{0:T(128)} %refs_0_.3, bf16[256,256]{1,0:T(8,128)(2,1)} %get-tuple-element.18.refs_1_.refs_2_, bf16[256,256]{1,0:T(8,128)(2,1)} %copy-done.2, bf16[256,256]{1,0:T(8,128)(2,1)} %copy-done.1, bf16[256,256]{1,0:T(8,128)(2,1)} %copy-done, ...), custom_call_target="tpu_custom_call" | custom-call | tf_op jit(solution)/shard_map/invert_lead/pallas_call | solution.py:332
  38.4 0.0 collective-permute-done.8.refs_13_
  38.4 0.0 collective-permute-done.7.refs_12_
  38.4 0.0 copy-start.7
  38.4 0.0 collective-permute-done.6.refs_11_
  38.4 0.0 copy-start.8
  38.4 0.4 collective-permute-start.9
  38.8 0.2 collective-permute-start.10
  39.0 0.3 collective-permute-start.11
  39.3 0.5 collective-permute-done.9.refs_15_
  39.8 0.3 collective-permute-done.10.refs_16_
  40.2 0.2 collective-permute-done.11.refs_17_
  40.4 0.0 copy-done.8
  40.4 0.1 copy-done.9
  40.5 0.4 copy-done.10
  40.8 0.2 copy-done.11
  41.1 17.2 %solve_tail.1.refs_0_ = bf16[96,512]{1,0:T(8,128)(2,1)} custom-call(f32[2]{0:T(128)} %refs_0_.3, f32[2,256,256]{2,1,0:T(8,128)} %invert_lead.1.refs_1_, bf16[256,256]{1,0:T(8,128)(2,1)} %get-tuple-element.18.refs_1_.refs_2_, bf16[256,256]{1,0:T(8,128)(2,1)} %copy-done.2, bf16[256,256]{1,0:T(8,128)(2,1)} %copy-done.1, bf16[256,256]{1,0:T(8,128)(2,1)} %copy-done, ...), custom_call_target="tpu_custom_call" | custom-call | tf_op jit(solution)/shard_map/solve_tail/pallas_call | solution.py:342
  58.3 1.0 %collective-permute-start.14 = (bf16[96,512]{1,0:T(8,128)(2,1)}, bf16[96,512]{1,0:T(8,128)(2,1)S(1)}, u32[]{:S(2)}, u32[]{:S(2)}) collective-permute-start(bf16[96,512]{1,0:T(8,128)(2,1)} %solve_tail.1.refs_0_), channel_id=1, source_target_pairs={{6,0},{4,2},{2,4},{0,6},{14,8},{12,10},{10,12},{8,14},{7,1},{5,3},... | collective-permute-start | bytes 294920 | tf_op jit(solution)/shard_map/ppermute | solution.py:368
  59.3 1.9 %collective-permute-start.13 = (bf16[96,512]{1,0:T(8,128)(2,1)}, bf16[96,512]{1,0:T(8,128)(2,1)S(1)}, u32[]{:S(2)}, u32[]{:S(2)}) collective-permute-start(bf16[96,512]{1,0:T(8,128)(2,1)} %solve_tail.1.refs_0_), channel_id=1, source_target_pairs={{4,0},{6,2},{0,4},{2,6},{12,8},{14,10},{8,12},{10,14},{5,1},{7,3},... | collective-permute-start | bytes 294920 | tf_op jit(solution)/shard_map/ppermute | solution.py:368
  61.2 0.5 collective-permute-start.12
  61.8 3.3 %collective-permute-done.14.refs_3_ = bf16[96,512]{1,0:T(8,128)(2,1)S(1)} collective-permute-done((bf16[96,512]{1,0:T(8,128)(2,1)}, bf16[96,512]{1,0:T(8,128)(2,1)S(1)}, u32[]{:S(2)}, u32[]{:S(2)}) %collective-permute-start.14) | collective-permute-done | bytes 98336 | tf_op jit(solution)/shard_map/ppermute | solution.py:368
  65.1 1.5 %collective-permute-done.13.refs_2_ = bf16[96,512]{1,0:T(8,128)(2,1)S(1)} collective-permute-done((bf16[96,512]{1,0:T(8,128)(2,1)}, bf16[96,512]{1,0:T(8,128)(2,1)S(1)}, u32[]{:S(2)}, u32[]{:S(2)}) %collective-permute-start.13) | collective-permute-done | bytes 98336 | tf_op jit(solution)/shard_map/ppermute | solution.py:368
  66.5 0.0 collective-permute-done.12.refs_1_
  66.6 0.6 copy-done.13
  67.2 0.6 copy-done.14
  67.8 1.9 %level_one.1 = (bf16[2,1,20,2,128]{4,3,2,1,0:T(2,128)(2,1)}, f32[2,1,2,2,2,20]{5,4,3,2,1,0:T(2,128)}, f32[2,1,2,20]{3,2,1,0:T(2,128)}) custom-call(bf16[96,512]{1,0:T(8,128)(2,1)} %solve_tail.1.refs_0_, bf16[96,512]{1,0:T(8,128)(2,1)} %copy-done.14, bf16[96,512]{1,0:T(8,128)(2,1)} %copy-done.13, bf16[96,512]{1,0:T(8,128)(2,1)} %copy-done.12), custom_call_target="tpu_custom_call" | custom-call | tf_op jit(solution)/shard_map/level_one/pallas_call | solution.py:370
  (16 shorter events, 0.0 us)
Async XLA Ops:
  3.2 9.7 %collective-permute-start.2 = (bf16[256,256]{1,0:T(8,128)(2,1)}, bf16[256,256]{1,0:T(8,128)(2,1)S(1)}, u32[]{:S(2)}, u32[]{:S(2)}) collective-permute-start(bf16[256,256]{1,0:T(8,128)(2,1)} %get-tuple-element.18.refs_1_.refs_2_), channel_id=1, source_target_pairs={{0,12},{4,8},{8,4},{12,0},{1,13},{5,9},{9,5},{13,1},{2,14},{6,10},... | collective-permute-start | bytes 393224 | tf_op jit(solution)/shard_map/ppermute | solution.py:322
  8.2 11.3 %collective-permute-start.1 = (bf16[256,256]{1,0:T(8,128)(2,1)}, bf16[256,256]{1,0:T(8,128)(2,1)S(1)}, u32[]{:S(2)}, u32[]{:S(2)}) collective-permute-start(bf16[256,256]{1,0:T(8,128)(2,1)} %get-tuple-element.18.refs_1_.refs_2_), channel_id=1, source_target_pairs={{0,8},{4,12},{8,0},{12,4},{1,9},{5,13},{9,1},{13,5},{2,10},{6,14},... | collective-permute-start | bytes 393224 | tf_op jit(solution)/shard_map/ppermute | solution.py:322
  8.2 11.3 %collective-permute-start = (bf16[256,256]{1,0:T(8,128)(2,1)}, bf16[256,256]{1,0:T(8,128)(2,1)S(1)}, u32[]{:S(2)}, u32[]{:S(2)}) collective-permute-start(bf16[256,256]{1,0:T(8,128)(2,1)} %get-tuple-element.18.refs_1_.refs_2_), channel_id=1, source_target_pairs={{0,4},{4,0},{8,12},{12,8},{1,5},{5,1},{9,13},{13,9},{2,6},{6,2},{1... | collective-permute-start | bytes 393224 | tf_op jit(solution)/shard_map/ppermute | solution.py:322
  12.9 12.6 %copy-start = (bf16[256,256]{1,0:T(8,128)(2,1)}, bf16[256,256]{1,0:T(8,128)(2,1)S(1)}, u32[]{:S(2)}) copy-start(bf16[256,256]{1,0:T(8,128)(2,1)S(1)} %collective-permute-done.2.refs_4_.refs_5_) | copy-start | bytes 393220
  12.9 11.1 %collective-permute-start.5 = (bf16[256,256]{1,0:T(8,128)(2,1)S(1)}, bf16[256,256]{1,0:T(8,128)(2,1)S(1)}, u32[]{:S(2)}, u32[]{:S(2)}) collective-permute-start(bf16[256,256]{1,0:T(8,128)(2,1)S(1)} %collective-permute-done.2.refs_4_.refs_5_), channel_id=1, source_target_pairs={{0,1},{1,0},{2,3},{3,2},{4,5},{5,4},{6,7},{7,6},{8,9},{9,8},{10,11... | collective-permute-start | bytes 393224 | tf_op jit(solution)/shard_map/ppermute | solution.py:326
  19.5 6.0 %copy-start.1 = (bf16[256,256]{1,0:T(8,128)(2,1)}, bf16[256,256]{1,0:T(8,128)(2,1)S(1)}, u32[]{:S(2)}) copy-start(bf16[256,256]{1,0:T(8,128)(2,1)S(1)} %collective-permute-done.1.refs_3_.refs_4_) | copy-start | bytes 393220
  19.5 6.0 %copy-start.2 = (bf16[256,256]{1,0:T(8,128)(2,1)}, bf16[256,256]{1,0:T(8,128)(2,1)S(1)}, u32[]{:S(2)}) copy-start(bf16[256,256]{1,0:T(8,128)(2,1)S(1)} %collective-permute-done.refs_2_.refs_3_) | copy-start | bytes 393220
  19.5 18.8 %collective-permute-start.8 = (bf16[288,256]{1,0:T(8,128)(2,1)}, bf16[288,256]{1,0:T(8,128)(2,1)S(1)}, u32[]{:S(2)}, u32[]{:S(2)}) collective-permute-start(bf16[288,256]{1,0:T(8,128)(2,1)} %get-tuple-element.24.refs_10_), channel_id=1, source_target_pairs={{0,12},{4,8},{8,4},{12,0},{1,13},{5,9},{9,5},{13,1},{2,14},{6,10},... | collective-permute-start | bytes 442376 | tf_op jit(solution)/shard_map/ppermute | solution.py:322
  22.1 16.3 %collective-permute-start.7 = (bf16[288,256]{1,0:T(8,128)(2,1)}, bf16[288,256]{1,0:T(8,128)(2,1)S(1)}, u32[]{:S(2)}, u32[]{:S(2)}) collective-permute-start(bf16[288,256]{1,0:T(8,128)(2,1)} %get-tuple-element.24.refs_10_), channel_id=1, source_target_pairs={{0,8},{4,12},{8,0},{12,4},{1,9},{5,13},{9,1},{13,5},{2,10},{6,14},... | collective-permute-start | bytes 442376 | tf_op jit(solution)/shard_map/ppermute | solution.py:322
  22.1 16.3 %collective-permute-start.6 = (bf16[288,256]{1,0:T(8,128)(2,1)}, bf16[288,256]{1,0:T(8,128)(2,1)S(1)}, u32[]{:S(2)}, u32[]{:S(2)}) collective-permute-start(bf16[288,256]{1,0:T(8,128)(2,1)} %get-tuple-element.24.refs_10_), channel_id=1, source_target_pairs={{0,4},{4,0},{8,12},{12,8},{1,5},{5,1},{9,13},{13,9},{2,6},{6,2},{1... | collective-permute-start | bytes 442376 | tf_op jit(solution)/shard_map/ppermute | solution.py:322
  24.0 1.3 %collective-permute-start.4 = (bf16[256,256]{1,0:T(8,128)(2,1)S(1)}, bf16[256,256]{1,0:T(8,128)(2,1)S(1)}, u32[]{:S(2)}, u32[]{:S(2)}) collective-permute-start(bf16[256,256]{1,0:T(8,128)(2,1)S(1)} %collective-permute-done.1.refs_3_.refs_4_), channel_id=1, source_target_pairs={{0,1},{1,0},{2,3},{3,2},{4,5},{5,4},{6,7},{7,6},{8,9},{9,8},{10,11... | collective-permute-start | bytes 393224 | tf_op jit(solution)/shard_map/ppermute | solution.py:326
  24.0 1.5 %copy-start.3 = (bf16[256,256]{1,0:T(8,128)(2,1)}, bf16[256,256]{1,0:T(8,128)(2,1)S(1)}, u32[]{:S(2)}) copy-start(bf16[256,256]{1,0:T(8,128)(2,1)S(1)} %collective-permute-done.5.refs_8_.refs_9_) | copy-start | bytes 393220
  24.0 1.5 %collective-permute-start.3 = (bf16[256,256]{1,0:T(8,128)(2,1)S(1)}, bf16[256,256]{1,0:T(8,128)(2,1)S(1)}, u32[]{:S(2)}, u32[]{:S(2)}) collective-permute-start(bf16[256,256]{1,0:T(8,128)(2,1)S(1)} %collective-permute-done.refs_2_.refs_3_), channel_id=1, source_target_pairs={{0,1},{1,0},{2,3},{3,2},{4,5},{5,4},{6,7},{7,6},{8,9},{9,8},{10,11... | collective-permute-start | bytes 393224 | tf_op jit(solution)/shard_map/ppermute | solution.py:326
  25.3 0.7 copy-start.4
  25.5 0.6 copy-start.5
  38.4 2.0 %copy-start.6 = (bf16[288,256]{1,0:T(8,128)(2,1)}, bf16[288,256]{1,0:T(8,128)(2,1)S(1)}, u32[]{:S(2)}) copy-start(bf16[288,256]{1,0:T(8,128)(2,1)S(1)} %collective-permute-done.8.refs_13_) | copy-start | bytes 442372
  38.4 2.0 %copy-start.7 = (bf16[288,256]{1,0:T(8,128)(2,1)}, bf16[288,256]{1,0:T(8,128)(2,1)S(1)}, u32[]{:S(2)}) copy-start(bf16[288,256]{1,0:T(8,128)(2,1)S(1)} %collective-permute-done.7.refs_12_) | copy-start | bytes 442372
  38.4 2.0 %copy-start.8 = (bf16[288,256]{1,0:T(8,128)(2,1)}, bf16[288,256]{1,0:T(8,128)(2,1)S(1)}, u32[]{:S(2)}) copy-start(bf16[288,256]{1,0:T(8,128)(2,1)S(1)} %collective-permute-done.6.refs_11_) | copy-start | bytes 442372
  38.4 1.4 %collective-permute-start.9 = (bf16[288,256]{1,0:T(8,128)(2,1)S(1)}, bf16[288,256]{1,0:T(8,128)(2,1)S(1)}, u32[]{:S(2)}, u32[]{:S(2)}) collective-permute-start(bf16[288,256]{1,0:T(8,128)(2,1)S(1)} %collective-permute-done.6.refs_11_), channel_id=1, source_target_pairs={{0,1},{1,0},{2,3},{3,2},{4,5},{5,4},{6,7},{7,6},{8,9},{9,8},{10,11... | collective-permute-start | bytes 442376 | tf_op jit(solution)/shard_map/ppermute | solution.py:326
  38.8 1.4 %collective-permute-start.10 = (bf16[288,256]{1,0:T(8,128)(2,1)S(1)}, bf16[288,256]{1,0:T(8,128)(2,1)S(1)}, u32[]{:S(2)}, u32[]{:S(2)}) collective-permute-start(bf16[288,256]{1,0:T(8,128)(2,1)S(1)} %collective-permute-done.7.refs_12_), channel_id=1, source_target_pairs={{0,1},{1,0},{2,3},{3,2},{4,5},{5,4},{6,7},{7,6},{8,9},{9,8},{10,11... | collective-permute-start | bytes 442376 | tf_op jit(solution)/shard_map/ppermute | solution.py:326
  39.0 1.4 %collective-permute-start.11 = (bf16[288,256]{1,0:T(8,128)(2,1)S(1)}, bf16[288,256]{1,0:T(8,128)(2,1)S(1)}, u32[]{:S(2)}, u32[]{:S(2)}) collective-permute-start(bf16[288,256]{1,0:T(8,128)(2,1)S(1)} %collective-permute-done.8.refs_13_), channel_id=1, source_target_pairs={{0,1},{1,0},{2,3},{3,2},{4,5},{5,4},{6,7},{7,6},{8,9},{9,8},{10,11... | collective-permute-start | bytes 442376 | tf_op jit(solution)/shard_map/ppermute | solution.py:326
  39.8 0.6 copy-start.9
  40.2 0.7 copy-start.10
  40.4 0.7 copy-start.11
  58.3 6.8 %collective-permute-start.14 = (bf16[96,512]{1,0:T(8,128)(2,1)}, bf16[96,512]{1,0:T(8,128)(2,1)S(1)}, u32[]{:S(2)}, u32[]{:S(2)}) collective-permute-start(bf16[96,512]{1,0:T(8,128)(2,1)} %solve_tail.1.refs_0_), channel_id=1, source_target_pairs={{6,0},{4,2},{2,4},{0,6},{14,8},{12,10},{10,12},{8,14},{7,1},{5,3},... | collective-permute-start | bytes 294920 | tf_op jit(solution)/shard_map/ppermute | solution.py:368
  59.3 7.2 %collective-permute-start.13 = (bf16[96,512]{1,0:T(8,128)(2,1)}, bf16[96,512]{1,0:T(8,128)(2,1)S(1)}, u32[]{:S(2)}, u32[]{:S(2)}) collective-permute-start(bf16[96,512]{1,0:T(8,128)(2,1)} %solve_tail.1.refs_0_), channel_id=1, source_target_pairs={{4,0},{6,2},{0,4},{2,6},{12,8},{14,10},{8,12},{10,14},{5,1},{7,3},... | collective-permute-start | bytes 294920 | tf_op jit(solution)/shard_map/ppermute | solution.py:368
  61.2 5.3 %collective-permute-start.12 = (bf16[96,512]{1,0:T(8,128)(2,1)}, bf16[96,512]{1,0:T(8,128)(2,1)S(1)}, u32[]{:S(2)}, u32[]{:S(2)}) collective-permute-start(bf16[96,512]{1,0:T(8,128)(2,1)} %solve_tail.1.refs_0_), channel_id=1, source_target_pairs={{2,0},{0,2},{6,4},{4,6},{10,8},{8,10},{14,12},{12,14},{3,1},{1,3},... | collective-permute-start | bytes 294920 | tf_op jit(solution)/shard_map/ppermute | solution.py:368
  65.1 1.5 %copy-start.12 = (bf16[96,512]{1,0:T(8,128)(2,1)}, bf16[96,512]{1,0:T(8,128)(2,1)S(1)}, u32[]{:S(2)}) copy-start(bf16[96,512]{1,0:T(8,128)(2,1)S(1)} %collective-permute-done.14.refs_3_) | copy-start | bytes 294916
  66.5 0.6 copy-start.13
  67.2 0.6 copy-start.14

commit v4 on v3

--- a/solution.py
+++ b/solution.py
@@ -13,6 +13,7 @@
 PANEL = 32
 PIVOTS = 8
 HIGHEST = lax.Precision.HIGHEST
+VMEM_SHARE = 2 << 20
 F32 = jnp.float32
 BF16 = jnp.bfloat16
 
@@ -289,6 +290,12 @@
             cross_ref[slot, 0, r : r + 1, :] = rows[n_blocks * levels : n_blocks * levels + 1, 0:traits]
 
 
+def land(value, copies):
+    if copies * value.size * value.dtype.itemsize > VMEM_SHARE:
+        return value
+    return pltpu.with_memory_space_constraint(value, pltpu.VMEM)
+
+
 def per_device(allele_dosage_table, phenotype_values, individual_partition_label, shrink_strengths):
     cores = lax.axis_size("folds")
     sources = lax.axis_size("samples")
@@ -319,11 +326,11 @@
 
     def fetch(other):
         return [other] + [
-            lax.ppermute(other, "samples", [(i, i ^ d) for i in range(sources)]) for d in range(1, sources)
+            land(lax.ppermute(other, "samples", [(i, i ^ d) for i in range(sources)]), 2 * sources) for d in range(1, sources)
         ]
 
     def swap(own, others):
-        return [own] + [lax.ppermute(x, "folds", [(i, cores - 1 - i) for i in range(cores)]) for x in others[1:]]
+        return [own] + [land(lax.ppermute(x, "folds", [(i, cores - 1 - i) for i in range(cores)]), 2 * sources) for x in others[1:]]
 
     others_lead = fetch(other_lead)
     owns_lead = swap(own_lead, others_lead)
@@ -337,7 +344,7 @@
         scratch_shapes=[pltpu.VMEM((levels, LANES, LANES), F32), pltpu.VMEM((8, LANES), F32)],
         name="invert_lead",
     )(shrink_strengths, *others_lead, *owns_lead)
-    lead_inverse, *others_tail[1:] = lax.optimization_barrier((lead_inverse, *others_tail[1:]))
+    lead_inverse, *others_tail[1:] = lax.optimization_barrier((land(lead_inverse, 1), *others_tail[1:]))
     owns_tail = swap(own_tail, others_tail)
     message = pl.pallas_call(
         functools.partial(tail_kernel, sources, own_count, learning_tally, trait_rows),
@@ -365,7 +372,7 @@
                 source = s - s % own_count + (s % own_count + f) % own_count
                 for b in range(n_blocks):
                     pairs.append((source * n_blocks + (b - e) % n_blocks, s * n_blocks + b))
-            messages.append(lax.ppermute(message, ("samples", "blocks"), pairs))
+            messages.append(land(lax.ppermute(message, ("samples", "blocks"), pairs), own_count * n_blocks))
 
     preds, gram, cross = pl.pallas_call(
         functools.partial(level_kernel, own_count, trait_rows, held_rows),

time: 69.9 us -> 67.1 us (0.960)
  local copies, waits for them, and re-layouts: 2.57 us -> 1.04 us
  Pallas kernels: 33.8 us -> 32.7 us
    unnamed x30 -> x2, local copies, waits for them, and re-layouts: 2.57 us -> 1.04 us
  transfers between devices with their start and end apart: 15 -> 15, of which waited for: 9 -> 9; matrix products, arithmetic and copies ran while one was open for 0% -> 0% of each run, Pallas kernels for 17% -> 18%
where the time goes in v4:
time: 67.1 us; the launch traced here: 66.9 us
  Pallas kernels  32.7 us (49%)
  waiting for transfers between devices  17.6 us (26%)
  starting transfers between devices  14.9 us (22%)
  local copies, waits for them, and re-layouts  1.04 us (2%)
    pallas_call x1, Pallas kernels, per_device(): pl.pallas_call(functools.partial(tail_kernel, sources, own_count, learnin...  16.6 us
    pallas_call x1, Pallas kernels, per_device(): pl.pallas_call(functools.partial(lead_kernel, sources, own_count, learnin...  11.9 us
    ppermute x6, waiting for transfers between devices, fetch(): lax.ppermute(other, 'samples', [(i, i ^ d) for i in range(sources)])  10.7 us
    ppermute x6, starting transfers between devices, fetch(): lax.ppermute(other, 'samples', [(i, i ^ d) for i in range(sources)])  10 us
    ppermute x3, waiting for transfers between devices, per_device(): lax.ppermute(message, ('samples', 'blocks'), pairs)  4.75 us
    ppermute x3, starting transfers between devices, per_device(): lax.ppermute(message, ('samples', 'blocks'), pairs)  3.49 us
    pallas_call x1, Pallas kernels, per_device(): pl.pallas_call(functools.partial(sort_kernel, own_count, pad_rows), out_s...  2.5 us
    ppermute x6, waiting for transfers between devices, swap(): lax.ppermute(x, 'folds', [(i, cores - 1 - i) for i in range(cores)])  2.09 us
  transfers between devices with their start and end apart: 15, of which 9 were waited for; matrix products, arithmetic and copies ran while one was open for 0% of the time, Pallas kernels for 18%

profile of v4, /device:TPU:0, one launch (start us, length us, event | category | flops | bytes accessed | tf_op | source)
XLA Modules:
  0.0 66.9 jit_solution(1030540244313623433)
XLA Ops:
  0.6 2.5 %sort_samples.1 = (bf16[256,256]{1,0:T(8,128)(2,1)}, bf16[256,256]{1,0:T(8,128)(2,1)}, bf16[288,256]{1,0:T(8,128)(2,1)}, bf16[288,256]{1,0:T(8,128)(2,1)}) custom-call(bf16[500,512]{1,0:T(8,128)(2,1)} %geno_ref.1, bf16[20,512]{1,0:T(8,128)(2,1)} %trait_ref.1, s32[1,512]{1,0:T(1,128)} %bitcast.3), custom_call_target="tpu_custom_call" | custom-call | tf_op jit(solution)/shard_map/sort_samples/pallas_call | solution.py:318
  3.1 5.1 %collective-permute-start.2 = (bf16[256,256]{1,0:T(8,128)(2,1)}, bf16[256,256]{1,0:T(8,128)(2,1)S(1)}, u32[]{:S(2)}, u32[]{:S(2)}) collective-permute-start(bf16[256,256]{1,0:T(8,128)(2,1)} %get-tuple-element.18.refs_1_.refs_2_), channel_id=1, source_target_pairs={{0,12},{4,8},{8,4},{12,0},{1,13},{5,9},{9,5},{13,1},{2,14},{6,10},... | collective-permute-start | bytes 393224 | tf_op jit(solution)/shard_map/ppermute | solution.py:329
  8.2 0.0 collective-permute-start.1
  8.2 0.6 collective-permute-start
  8.8 4.1 %collective-permute-done.2.refs_4_.refs_5_ = bf16[256,256]{1,0:T(8,128)(2,1)S(1)} collective-permute-done((bf16[256,256]{1,0:T(8,128)(2,1)}, bf16[256,256]{1,0:T(8,128)(2,1)S(1)}, u32[]{:S(2)}, u32[]{:S(2)}) %collective-permute-start.2) | collective-permute-done | bytes 131104 | tf_op jit(solution)/shard_map/ppermute | solution.py:329
  12.9 0.0 collective-permute-start.5
  12.9 6.6 %collective-permute-done.1.refs_3_.refs_4_ = bf16[256,256]{1,0:T(8,128)(2,1)S(1)} collective-permute-done((bf16[256,256]{1,0:T(8,128)(2,1)}, bf16[256,256]{1,0:T(8,128)(2,1)S(1)}, u32[]{:S(2)}, u32[]{:S(2)}) %collective-permute-start.1) | collective-permute-done | bytes 131104 | tf_op jit(solution)/shard_map/ppermute | solution.py:329
  19.5 0.0 collective-permute-done.refs_2_.refs_3_
  19.5 2.5 %collective-permute-start.8 = (bf16[288,256]{1,0:T(8,128)(2,1)}, bf16[288,256]{1,0:T(8,128)(2,1)S(1)}, u32[]{:S(2)}, u32[]{:S(2)}) collective-permute-start(bf16[288,256]{1,0:T(8,128)(2,1)} %get-tuple-element.24.refs_10_), channel_id=1, source_target_pairs={{0,12},{4,8},{8,4},{12,0},{1,13},{5,9},{9,5},{13,1},{2,14},{6,10},... | collective-permute-start | bytes 442376 | tf_op jit(solution)/shard_map/ppermute | solution.py:329
  22.0 0.0 collective-permute-start.7
  22.0 1.9 %collective-permute-start.6 = (bf16[288,256]{1,0:T(8,128)(2,1)}, bf16[288,256]{1,0:T(8,128)(2,1)S(1)}, u32[]{:S(2)}, u32[]{:S(2)}) collective-permute-start(bf16[288,256]{1,0:T(8,128)(2,1)} %get-tuple-element.24.refs_10_), channel_id=1, source_target_pairs={{0,4},{4,0},{8,12},{12,8},{1,5},{5,1},{9,13},{13,9},{2,6},{6,2},{1... | collective-permute-start | bytes 442376 | tf_op jit(solution)/shard_map/ppermute | solution.py:329
  23.9 0.0 collective-permute-start.4
  23.9 0.0 collective-permute-done.5.refs_8_.refs_9_
  23.9 0.5 collective-permute-start.3
  24.4 0.8 %collective-permute-done.4.refs_7_.refs_8_ = bf16[256,256]{1,0:T(8,128)(2,1)S(1)} collective-permute-done((bf16[256,256]{1,0:T(8,128)(2,1)S(1)}, bf16[256,256]{1,0:T(8,128)(2,1)S(1)}, u32[]{:S(2)}, u32[]{:S(2)}) %collective-permute-start.4) | collective-permute-done | bytes 131104 | tf_op jit(solution)/shard_map/ppermute | solution.py:333
  25.2 0.2 collective-permute-done.3.refs_6_.refs_7_
  25.4 11.9 %invert_lead.1.refs_1_ = f32[2,256,256]{2,1,0:T(8,128)} custom-call(f32[2]{0:T(128)} %refs_0_.3, bf16[256,256]{1,0:T(8,128)(2,1)} %get-tuple-element.18.refs_1_.refs_2_, bf16[256,256]{1,0:T(8,128)(2,1)S(1)} %collective-permute-done.refs_2_.refs_3_, bf16[256,256]{1,0:T(8,128)(2,1)S(1)} %collective-permute-done.1.refs_3_.refs_4_, ...), custom_call_target="tpu_custom_call" | custom-call | tf_op jit(solution)/shard_map/invert_lead/pallas_call | solution.py:339
  37.3 0.0 collective-permute-done.8.refs_13_
  37.3 0.0 collective-permute-done.7.refs_12_
  37.3 0.0 collective-permute-done.6.refs_11_
  37.3 0.4 collective-permute-start.9
  37.7 0.2 collective-permute-start.10
  37.9 0.3 collective-permute-start.11
  38.2 0.5 collective-permute-done.9.refs_15_
  38.7 0.3 collective-permute-done.10.refs_16_
  39.1 0.2 collective-permute-done.11.refs_17_
  39.3 0.0 copy-start
  39.3 1.0 %copy-done = f32[2,256,256]{2,1,0:T(8,128)S(1)} copy-done((f32[2,256,256]{2,1,0:T(8,128)S(1)}, f32[2,256,256]{2,1,0:T(8,128)}, u32[]{:S(2)}) %copy-start) | copy-done | bytes 524312
  40.3 16.6 %solve_tail.1.refs_0_ = bf16[96,512]{1,0:T(8,128)(2,1)} custom-call(f32[2]{0:T(128)} %refs_0_.3, f32[2,256,256]{2,1,0:T(8,128)S(1)} %copy-done, bf16[256,256]{1,0:T(8,128)(2,1)} %get-tuple-element.18.refs_1_.refs_2_, bf16[256,256]{1,0:T(8,128)(2,1)S(1)} %collective-permute-done.refs_2_.refs_3_, bf16[256,256]{1,0:T(8,128)(2,1)S(1)} %collective-permute-done.1.refs_3_.refs_4_, ...), custom_call_target="tpu_custom_call" | custom-call | tf_op jit(solution)/shard_map/solve_tail/pallas_call | solution.py:349
  56.9 1.0 %collective-permute-start.14 = (bf16[96,512]{1,0:T(8,128)(2,1)}, bf16[96,512]{1,0:T(8,128)(2,1)S(1)}, u32[]{:S(2)}, u32[]{:S(2)}) collective-permute-start(bf16[96,512]{1,0:T(8,128)(2,1)} %solve_tail.1.refs_0_), channel_id=1, source_target_pairs={{6,0},{4,2},{2,4},{0,6},{14,8},{12,10},{10,12},{8,14},{7,1},{5,3},... | collective-permute-start | bytes 294920 | tf_op jit(solution)/shard_map/ppermute | solution.py:375
  57.9 1.9 %collective-permute-start.13 = (bf16[96,512]{1,0:T(8,128)(2,1)}, bf16[96,512]{1,0:T(8,128)(2,1)S(1)}, u32[]{:S(2)}, u32[]{:S(2)}) collective-permute-start(bf16[96,512]{1,0:T(8,128)(2,1)} %solve_tail.1.refs_0_), channel_id=1, source_target_pairs={{4,0},{6,2},{0,4},{2,6},{12,8},{14,10},{8,12},{10,14},{5,1},{7,3},... | collective-permute-start | bytes 294920 | tf_op jit(solution)/shard_map/ppermute | solution.py:375
  59.8 0.5 collective-permute-start.12
  60.4 3.3 %collective-permute-done.14.refs_3_ = bf16[96,512]{1,0:T(8,128)(2,1)S(1)} collective-permute-done((bf16[96,512]{1,0:T(8,128)(2,1)}, bf16[96,512]{1,0:T(8,128)(2,1)S(1)}, u32[]{:S(2)}, u32[]{:S(2)}) %collective-permute-start.14) | collective-permute-done | bytes 98336 | tf_op jit(solution)/shard_map/ppermute | solution.py:375
  63.7 1.5 %collective-permute-done.13.refs_2_ = bf16[96,512]{1,0:T(8,128)(2,1)S(1)} collective-permute-done((bf16[96,512]{1,0:T(8,128)(2,1)}, bf16[96,512]{1,0:T(8,128)(2,1)S(1)}, u32[]{:S(2)}, u32[]{:S(2)}) %collective-permute-start.13) | collective-permute-done | bytes 98336 | tf_op jit(solution)/shard_map/ppermute | solution.py:375
  65.1 0.0 collective-permute-done.12.refs_1_
  65.1 1.7 %level_one.1 = (bf16[2,1,20,2,128]{4,3,2,1,0:T(2,128)(2,1)}, f32[2,1,2,2,2,20]{5,4,3,2,1,0:T(2,128)}, f32[2,1,2,20]{3,2,1,0:T(2,128)}) custom-call(bf16[96,512]{1,0:T(8,128)(2,1)} %solve_tail.1.refs_0_, bf16[96,512]{1,0:T(8,128)(2,1)S(1)} %collective-permute-done.12.refs_1_, bf16[96,512]{1,0:T(8,128)(2,1)S(1)} %collective-permute-done.13.refs_2_, ...), custom_call_target="tpu_custom_call" | custom-call | tf_op jit(solution)/shard_map/level_one/pallas_call | solution.py:377
Async XLA Ops:
  3.1 9.7 %collective-permute-start.2 = (bf16[256,256]{1,0:T(8,128)(2,1)}, bf16[256,256]{1,0:T(8,128)(2,1)S(1)}, u32[]{:S(2)}, u32[]{:S(2)}) collective-permute-start(bf16[256,256]{1,0:T(8,128)(2,1)} %get-tuple-element.18.refs_1_.refs_2_), channel_id=1, source_target_pairs={{0,12},{4,8},{8,4},{12,0},{1,13},{5,9},{9,5},{13,1},{2,14},{6,10},... | collective-permute-start | bytes 393224 | tf_op jit(solution)/shard_map/ppermute | solution.py:329
  8.2 11.3 %collective-permute-start.1 = (bf16[256,256]{1,0:T(8,128)(2,1)}, bf16[256,256]{1,0:T(8,128)(2,1)S(1)}, u32[]{:S(2)}, u32[]{:S(2)}) collective-permute-start(bf16[256,256]{1,0:T(8,128)(2,1)} %get-tuple-element.18.refs_1_.refs_2_), channel_id=1, source_target_pairs={{0,8},{4,12},{8,0},{12,4},{1,9},{5,13},{9,1},{13,5},{2,10},{6,14},... | collective-permute-start | bytes 393224 | tf_op jit(solution)/shard_map/ppermute | solution.py:329
  8.2 11.3 %collective-permute-start = (bf16[256,256]{1,0:T(8,128)(2,1)}, bf16[256,256]{1,0:T(8,128)(2,1)S(1)}, u32[]{:S(2)}, u32[]{:S(2)}) collective-permute-start(bf16[256,256]{1,0:T(8,128)(2,1)} %get-tuple-element.18.refs_1_.refs_2_), channel_id=1, source_target_pairs={{0,4},{4,0},{8,12},{12,8},{1,5},{5,1},{9,13},{13,9},{2,6},{6,2},{1... | collective-permute-start | bytes 393224 | tf_op jit(solution)/shard_map/ppermute | solution.py:329
  12.9 11.0 %collective-permute-start.5 = (bf16[256,256]{1,0:T(8,128)(2,1)S(1)}, bf16[256,256]{1,0:T(8,128)(2,1)S(1)}, u32[]{:S(2)}, u32[]{:S(2)}) collective-permute-start(bf16[256,256]{1,0:T(8,128)(2,1)S(1)} %collective-permute-done.2.refs_4_.refs_5_), channel_id=1, source_target_pairs={{0,1},{1,0},{2,3},{3,2},{4,5},{5,4},{6,7},{7,6},{8,9},{9,8},{10,11... | collective-permute-start | bytes 393224 | tf_op jit(solution)/shard_map/ppermute | solution.py:333
  19.5 17.8 %collective-permute-start.8 = (bf16[288,256]{1,0:T(8,128)(2,1)}, bf16[288,256]{1,0:T(8,128)(2,1)S(1)}, u32[]{:S(2)}, u32[]{:S(2)}) collective-permute-start(bf16[288,256]{1,0:T(8,128)(2,1)} %get-tuple-element.24.refs_10_), channel_id=1, source_target_pairs={{0,12},{4,8},{8,4},{12,0},{1,13},{5,9},{9,5},{13,1},{2,14},{6,10},... | collective-permute-start | bytes 442376 | tf_op jit(solution)/shard_map/ppermute | solution.py:329
  22.0 15.3 %collective-permute-start.7 = (bf16[288,256]{1,0:T(8,128)(2,1)}, bf16[288,256]{1,0:T(8,128)(2,1)S(1)}, u32[]{:S(2)}, u32[]{:S(2)}) collective-permute-start(bf16[288,256]{1,0:T(8,128)(2,1)} %get-tuple-element.24.refs_10_), channel_id=1, source_target_pairs={{0,8},{4,12},{8,0},{12,4},{1,9},{5,13},{9,1},{13,5},{2,10},{6,14},... | collective-permute-start | bytes 442376 | tf_op jit(solution)/shard_map/ppermute | solution.py:329
  22.0 15.3 %collective-permute-start.6 = (bf16[288,256]{1,0:T(8,128)(2,1)}, bf16[288,256]{1,0:T(8,128)(2,1)S(1)}, u32[]{:S(2)}, u32[]{:S(2)}) collective-permute-start(bf16[288,256]{1,0:T(8,128)(2,1)} %get-tuple-element.24.refs_10_), channel_id=1, source_target_pairs={{0,4},{4,0},{8,12},{12,8},{1,5},{5,1},{9,13},{13,9},{2,6},{6,2},{1... | collective-permute-start | bytes 442376 | tf_op jit(solution)/shard_map/ppermute | solution.py:329
  23.9 1.3 %collective-permute-start.4 = (bf16[256,256]{1,0:T(8,128)(2,1)S(1)}, bf16[256,256]{1,0:T(8,128)(2,1)S(1)}, u32[]{:S(2)}, u32[]{:S(2)}) collective-permute-start(bf16[256,256]{1,0:T(8,128)(2,1)S(1)} %collective-permute-done.1.refs_3_.refs_4_), channel_id=1, source_target_pairs={{0,1},{1,0},{2,3},{3,2},{4,5},{5,4},{6,7},{7,6},{8,9},{9,8},{10,11... | collective-permute-start | bytes 393224 | tf_op jit(solution)/shard_map/ppermute | solution.py:333
  23.9 1.5 %collective-permute-start.3 = (bf16[256,256]{1,0:T(8,128)(2,1)S(1)}, bf16[256,256]{1,0:T(8,128)(2,1)S(1)}, u32[]{:S(2)}, u32[]{:S(2)}) collective-permute-start(bf16[256,256]{1,0:T(8,128)(2,1)S(1)} %collective-permute-done.refs_2_.refs_3_), channel_id=1, source_target_pairs={{0,1},{1,0},{2,3},{3,2},{4,5},{5,4},{6,7},{7,6},{8,9},{9,8},{10,11... | collective-permute-start | bytes 393224 | tf_op jit(solution)/shard_map/ppermute | solution.py:333
  37.3 1.4 %collective-permute-start.9 = (bf16[288,256]{1,0:T(8,128)(2,1)S(1)}, bf16[288,256]{1,0:T(8,128)(2,1)S(1)}, u32[]{:S(2)}, u32[]{:S(2)}) collective-permute-start(bf16[288,256]{1,0:T(8,128)(2,1)S(1)} %collective-permute-done.6.refs_11_), channel_id=1, source_target_pairs={{0,1},{1,0},{2,3},{3,2},{4,5},{5,4},{6,7},{7,6},{8,9},{9,8},{10,11... | collective-permute-start | bytes 442376 | tf_op jit(solution)/shard_map/ppermute | solution.py:333
  37.7 1.4 %collective-permute-start.10 = (bf16[288,256]{1,0:T(8,128)(2,1)S(1)}, bf16[288,256]{1,0:T(8,128)(2,1)S(1)}, u32[]{:S(2)}, u32[]{:S(2)}) collective-permute-start(bf16[288,256]{1,0:T(8,128)(2,1)S(1)} %collective-permute-done.7.refs_12_), channel_id=1, source_target_pairs={{0,1},{1,0},{2,3},{3,2},{4,5},{5,4},{6,7},{7,6},{8,9},{9,8},{10,11... | collective-permute-start | bytes 442376 | tf_op jit(solution)/shard_map/ppermute | solution.py:333
  37.9 1.4 %collective-permute-start.11 = (bf16[288,256]{1,0:T(8,128)(2,1)S(1)}, bf16[288,256]{1,0:T(8,128)(2,1)S(1)}, u32[]{:S(2)}, u32[]{:S(2)}) collective-permute-start(bf16[288,256]{1,0:T(8,128)(2,1)S(1)} %collective-permute-done.8.refs_13_), channel_id=1, source_target_pairs={{0,1},{1,0},{2,3},{3,2},{4,5},{5,4},{6,7},{7,6},{8,9},{9,8},{10,11... | collective-permute-start | bytes 442376 | tf_op jit(solution)/shard_map/ppermute | solution.py:333
  39.3 1.0 %copy-start = (f32[2,256,256]{2,1,0:T(8,128)S(1)}, f32[2,256,256]{2,1,0:T(8,128)}, u32[]{:S(2)}) copy-start(f32[2,256,256]{2,1,0:T(8,128)} %invert_lead.1.refs_1_) | copy-start | bytes 1572868
  56.9 6.8 %collective-permute-start.14 = (bf16[96,512]{1,0:T(8,128)(2,1)}, bf16[96,512]{1,0:T(8,128)(2,1)S(1)}, u32[]{:S(2)}, u32[]{:S(2)}) collective-permute-start(bf16[96,512]{1,0:T(8,128)(2,1)} %solve_tail.1.refs_0_), channel_id=1, source_target_pairs={{6,0},{4,2},{2,4},{0,6},{14,8},{12,10},{10,12},{8,14},{7,1},{5,3},... | collective-permute-start | bytes 294920 | tf_op jit(solution)/shard_map/ppermute | solution.py:375
  57.9 7.2 %collective-permute-start.13 = (bf16[96,512]{1,0:T(8,128)(2,1)}, bf16[96,512]{1,0:T(8,128)(2,1)S(1)}, u32[]{:S(2)}, u32[]{:S(2)}) collective-permute-start(bf16[96,512]{1,0:T(8,128)(2,1)} %solve_tail.1.refs_0_), channel_id=1, source_target_pairs={{4,0},{6,2},{0,4},{2,6},{12,8},{14,10},{8,12},{10,14},{5,1},{7,3},... | collective-permute-start | bytes 294920 | tf_op jit(solution)/shard_map/ppermute | solution.py:375
  59.8 5.3 %collective-permute-start.12 = (bf16[96,512]{1,0:T(8,128)(2,1)}, bf16[96,512]{1,0:T(8,128)(2,1)S(1)}, u32[]{:S(2)}, u32[]{:S(2)}) collective-permute-start(bf16[96,512]{1,0:T(8,128)(2,1)} %solve_tail.1.refs_0_), channel_id=1, source_target_pairs={{2,0},{0,2},{6,4},{4,6},{10,8},{8,10},{14,12},{12,14},{3,1},{1,3},... | collective-permute-start | bytes 294920 | tf_op jit(solution)/shard_map/ppermute | solution.py:375

commit v5 on v4

--- a/solution.py
+++ b/solution.py
@@ -137,15 +137,14 @@
 
 
 def training_product(left, right, train, width, rows):
-    acc = None
+    lefts, rights = [], []
     for left_other, left_own, right_other, right_own in zip(*left, *right):
-        pieces = [(left_other[rows, :], right_other[...])]
+        lefts.append(left_other[rows, :])
+        rights.append(right_other[...])
         for start in train:
-            pieces.append((left_own[rows, pl.ds(start, width)], right_own[:, pl.ds(start, width)]))
-        for a, b in pieces:
-            part = dot_nt(a, b)
-            acc = part if acc is None else acc + part
-    return acc
+            lefts.append(left_own[rows, pl.ds(start, width)])
+            rights.append(right_own[:, pl.ds(start, width)])
+    return dot_nt(jnp.concatenate(lefts, axis=1), jnp.concatenate(rights, axis=1))
 
 
 def stages(count, levels, mat_ref, inv_ref, ones_ref, follow):
@@ -344,7 +343,7 @@
         scratch_shapes=[pltpu.VMEM((levels, LANES, LANES), F32), pltpu.VMEM((8, LANES), F32)],
         name="invert_lead",
     )(shrink_strengths, *others_lead, *owns_lead)
-    lead_inverse, *others_tail[1:] = lax.optimization_barrier((land(lead_inverse, 1), *others_tail[1:]))
+    lead_inverse, *others_tail[1:] = lax.optimization_barrier((lead_inverse, *others_tail[1:]))
     owns_tail = swap(own_tail, others_tail)
     message = pl.pallas_call(
         functools.partial(tail_kernel, sources, own_count, learning_tally, trait_rows),

time: 67.1 us -> 65.9 us (0.982)
  local copies, waits for them, and re-layouts: 1.04 us -> 0 us
    unnamed x2 -> x0, local copies, waits for them, and re-layouts: 1.04 us -> none
where the time goes in v5:
time: 65.9 us; the launch traced here: 65.7 us
  Pallas kernels  32.6 us (49%)
  waiting for transfers between devices  17.6 us (27%)
  starting transfers between devices  14.9 us (23%)
    pallas_call x1, Pallas kernels, per_device(): pl.pallas_call(functools.partial(tail_kernel, sources, own_count, learnin...  16.5 us
    pallas_call x1, Pallas kernels, per_device(): pl.pallas_call(functools.partial(lead_kernel, sources, own_count, learnin...  11.8 us
    ppermute x6, waiting for transfers between devices, fetch(): lax.ppermute(other, 'samples', [(i, i ^ d) for i in range(sources)])  10.7 us
    ppermute x6, starting transfers between devices, fetch(): lax.ppermute(other, 'samples', [(i, i ^ d) for i in range(sources)])  10 us
    ppermute x3, waiting for transfers between devices, per_device(): lax.ppermute(message, ('samples', 'blocks'), pairs)  4.76 us
    ppermute x3, starting transfers between devices, per_device(): lax.ppermute(message, ('samples', 'blocks'), pairs)  3.49 us
    pallas_call x1, Pallas kernels, per_device(): pl.pallas_call(functools.partial(sort_kernel, own_count, pad_rows), out_s...  2.5 us
    ppermute x6, waiting for transfers between devices, swap(): lax.ppermute(x, 'folds', [(i, cores - 1 - i) for i in range(cores)])  2.09 us
  transfers between devices with their start and end apart: 15, of which 9 were waited for; matrix products, arithmetic and copies ran while one was open for 0% of the time, Pallas kernels for 18%

profile of v5, /device:TPU:0, one launch (start us, length us, event | category | flops | bytes accessed | tf_op | source)
XLA Modules:
  0.0 65.7 jit_solution(15160735264154600663)
XLA Ops:
  0.6 2.5 %sort_samples.1 = (bf16[256,256]{1,0:T(8,128)(2,1)}, bf16[256,256]{1,0:T(8,128)(2,1)}, bf16[288,256]{1,0:T(8,128)(2,1)}, bf16[288,256]{1,0:T(8,128)(2,1)}) custom-call(bf16[500,512]{1,0:T(8,128)(2,1)} %geno_ref.1, bf16[20,512]{1,0:T(8,128)(2,1)} %trait_ref.1, s32[1,512]{1,0:T(1,128)} %bitcast.3), custom_call_target="tpu_custom_call" | custom-call | tf_op jit(solution)/shard_map/sort_samples/pallas_call | solution.py:317
  3.1 5.1 %collective-permute-start.2 = (bf16[256,256]{1,0:T(8,128)(2,1)}, bf16[256,256]{1,0:T(8,128)(2,1)S(1)}, u32[]{:S(2)}, u32[]{:S(2)}) collective-permute-start(bf16[256,256]{1,0:T(8,128)(2,1)} %get-tuple-element.18.refs_1_.refs_2_), channel_id=1, source_target_pairs={{0,12},{4,8},{8,4},{12,0},{1,13},{5,9},{9,5},{13,1},{2,14},{6,10},... | collective-permute-start | bytes 393224 | tf_op jit(solution)/shard_map/ppermute | solution.py:328
  8.2 0.0 collective-permute-start.1
  8.2 0.6 collective-permute-start
  8.8 4.1 %collective-permute-done.2.refs_4_.refs_5_ = bf16[256,256]{1,0:T(8,128)(2,1)S(1)} collective-permute-done((bf16[256,256]{1,0:T(8,128)(2,1)}, bf16[256,256]{1,0:T(8,128)(2,1)S(1)}, u32[]{:S(2)}, u32[]{:S(2)}) %collective-permute-start.2) | collective-permute-done | bytes 131104 | tf_op jit(solution)/shard_map/ppermute | solution.py:328
  12.9 0.0 collective-permute-start.5
  12.9 6.6 %collective-permute-done.1.refs_3_.refs_4_ = bf16[256,256]{1,0:T(8,128)(2,1)S(1)} collective-permute-done((bf16[256,256]{1,0:T(8,128)(2,1)}, bf16[256,256]{1,0:T(8,128)(2,1)S(1)}, u32[]{:S(2)}, u32[]{:S(2)}) %collective-permute-start.1) | collective-permute-done | bytes 131104 | tf_op jit(solution)/shard_map/ppermute | solution.py:328
  19.5 0.0 collective-permute-done.refs_2_.refs_3_
  19.5 2.5 %collective-permute-start.8 = (bf16[288,256]{1,0:T(8,128)(2,1)}, bf16[288,256]{1,0:T(8,128)(2,1)S(1)}, u32[]{:S(2)}, u32[]{:S(2)}) collective-permute-start(bf16[288,256]{1,0:T(8,128)(2,1)} %get-tuple-element.24.refs_10_), channel_id=1, source_target_pairs={{0,12},{4,8},{8,4},{12,0},{1,13},{5,9},{9,5},{13,1},{2,14},{6,10},... | collective-permute-start | bytes 442376 | tf_op jit(solution)/shard_map/ppermute | solution.py:328
  22.0 0.0 collective-permute-start.7
  22.0 1.9 %collective-permute-start.6 = (bf16[288,256]{1,0:T(8,128)(2,1)}, bf16[288,256]{1,0:T(8,128)(2,1)S(1)}, u32[]{:S(2)}, u32[]{:S(2)}) collective-permute-start(bf16[288,256]{1,0:T(8,128)(2,1)} %get-tuple-element.24.refs_10_), channel_id=1, source_target_pairs={{0,4},{4,0},{8,12},{12,8},{1,5},{5,1},{9,13},{13,9},{2,6},{6,2},{1... | collective-permute-start | bytes 442376 | tf_op jit(solution)/shard_map/ppermute | solution.py:328
  23.9 0.0 collective-permute-start.4
  23.9 0.0 collective-permute-done.5.refs_8_.refs_9_
  23.9 0.5 collective-permute-start.3
  24.4 0.8 %collective-permute-done.4.refs_7_.refs_8_ = bf16[256,256]{1,0:T(8,128)(2,1)S(1)} collective-permute-done((bf16[256,256]{1,0:T(8,128)(2,1)S(1)}, bf16[256,256]{1,0:T(8,128)(2,1)S(1)}, u32[]{:S(2)}, u32[]{:S(2)}) %collective-permute-start.4) | collective-permute-done | bytes 131104 | tf_op jit(solution)/shard_map/ppermute | solution.py:332
  25.2 0.2 collective-permute-done.3.refs_6_.refs_7_
  25.4 11.8 %invert_lead.1.refs_1_ = f32[2,256,256]{2,1,0:T(8,128)} custom-call(f32[2]{0:T(128)} %refs_0_.3, bf16[256,256]{1,0:T(8,128)(2,1)} %get-tuple-element.18.refs_1_.refs_2_, bf16[256,256]{1,0:T(8,128)(2,1)S(1)} %collective-permute-done.refs_2_.refs_3_, bf16[256,256]{1,0:T(8,128)(2,1)S(1)} %collective-permute-done.1.refs_3_.refs_4_, ...), custom_call_target="tpu_custom_call" | custom-call | tf_op jit(solution)/shard_map/invert_lead/pallas_call | solution.py:338
  37.3 0.0 collective-permute-done.8.refs_13_
  37.3 0.0 collective-permute-done.7.refs_12_
  37.3 0.0 collective-permute-done.6.refs_11_
  37.3 0.4 collective-permute-start.9
  37.7 0.2 collective-permute-start.10
  37.9 0.3 collective-permute-start.11
  38.2 0.5 collective-permute-done.9.refs_15_
  38.7 0.3 collective-permute-done.10.refs_16_
  39.0 0.2 collective-permute-done.11.refs_17_
  39.3 16.5 %solve_tail.1.refs_0_ = bf16[96,512]{1,0:T(8,128)(2,1)} custom-call(f32[2]{0:T(128)} %refs_0_.3, f32[2,256,256]{2,1,0:T(8,128)} %invert_lead.1.refs_1_, bf16[256,256]{1,0:T(8,128)(2,1)} %get-tuple-element.18.refs_1_.refs_2_, bf16[256,256]{1,0:T(8,128)(2,1)S(1)} %collective-permute-done.refs_2_.refs_3_, ...), custom_call_target="tpu_custom_call" | custom-call | tf_op jit(solution)/shard_map/solve_tail/pallas_call | solution.py:348
  55.7 1.0 %collective-permute-start.14 = (bf16[96,512]{1,0:T(8,128)(2,1)}, bf16[96,512]{1,0:T(8,128)(2,1)S(1)}, u32[]{:S(2)}, u32[]{:S(2)}) collective-permute-start(bf16[96,512]{1,0:T(8,128)(2,1)} %solve_tail.1.refs_0_), channel_id=1, source_target_pairs={{6,0},{4,2},{2,4},{0,6},{14,8},{12,10},{10,12},{8,14},{7,1},{5,3},... | collective-permute-start | bytes 294920 | tf_op jit(solution)/shard_map/ppermute | solution.py:374
  56.8 1.9 %collective-permute-start.13 = (bf16[96,512]{1,0:T(8,128)(2,1)}, bf16[96,512]{1,0:T(8,128)(2,1)S(1)}, u32[]{:S(2)}, u32[]{:S(2)}) collective-permute-start(bf16[96,512]{1,0:T(8,128)(2,1)} %solve_tail.1.refs_0_), channel_id=1, source_target_pairs={{4,0},{6,2},{0,4},{2,6},{12,8},{14,10},{8,12},{10,14},{5,1},{7,3},... | collective-permute-start | bytes 294920 | tf_op jit(solution)/shard_map/ppermute | solution.py:374
  58.7 0.5 collective-permute-start.12
  59.2 3.3 %collective-permute-done.14.refs_3_ = bf16[96,512]{1,0:T(8,128)(2,1)S(1)} collective-permute-done((bf16[96,512]{1,0:T(8,128)(2,1)}, bf16[96,512]{1,0:T(8,128)(2,1)S(1)}, u32[]{:S(2)}, u32[]{:S(2)}) %collective-permute-start.14) | collective-permute-done | bytes 98336 | tf_op jit(solution)/shard_map/ppermute | solution.py:374
  62.5 1.5 %collective-permute-done.13.refs_2_ = bf16[96,512]{1,0:T(8,128)(2,1)S(1)} collective-permute-done((bf16[96,512]{1,0:T(8,128)(2,1)}, bf16[96,512]{1,0:T(8,128)(2,1)S(1)}, u32[]{:S(2)}, u32[]{:S(2)}) %collective-permute-start.13) | collective-permute-done | bytes 98336 | tf_op jit(solution)/shard_map/ppermute | solution.py:374
  64.0 0.0 collective-permute-done.12.refs_1_
  64.0 1.7 %level_one.1 = (bf16[2,1,20,2,128]{4,3,2,1,0:T(2,128)(2,1)}, f32[2,1,2,2,2,20]{5,4,3,2,1,0:T(2,128)}, f32[2,1,2,20]{3,2,1,0:T(2,128)}) custom-call(bf16[96,512]{1,0:T(8,128)(2,1)} %solve_tail.1.refs_0_, bf16[96,512]{1,0:T(8,128)(2,1)S(1)} %collective-permute-done.12.refs_1_, bf16[96,512]{1,0:T(8,128)(2,1)S(1)} %collective-permute-done.13.refs_2_, ...), custom_call_target="tpu_custom_call" | custom-call | tf_op jit(solution)/shard_map/level_one/pallas_call | solution.py:376
Async XLA Ops:
  3.1 9.7 %collective-permute-start.2 = (bf16[256,256]{1,0:T(8,128)(2,1)}, bf16[256,256]{1,0:T(8,128)(2,1)S(1)}, u32[]{:S(2)}, u32[]{:S(2)}) collective-permute-start(bf16[256,256]{1,0:T(8,128)(2,1)} %get-tuple-element.18.refs_1_.refs_2_), channel_id=1, source_target_pairs={{0,12},{4,8},{8,4},{12,0},{1,13},{5,9},{9,5},{13,1},{2,14},{6,10},... | collective-permute-start | bytes 393224 | tf_op jit(solution)/shard_map/ppermute | solution.py:328
  8.2 11.3 %collective-permute-start.1 = (bf16[256,256]{1,0:T(8,128)(2,1)}, bf16[256,256]{1,0:T(8,128)(2,1)S(1)}, u32[]{:S(2)}, u32[]{:S(2)}) collective-permute-start(bf16[256,256]{1,0:T(8,128)(2,1)} %get-tuple-element.18.refs_1_.refs_2_), channel_id=1, source_target_pairs={{0,8},{4,12},{8,0},{12,4},{1,9},{5,13},{9,1},{13,5},{2,10},{6,14},... | collective-permute-start | bytes 393224 | tf_op jit(solution)/shard_map/ppermute | solution.py:328
  8.2 11.3 %collective-permute-start = (bf16[256,256]{1,0:T(8,128)(2,1)}, bf16[256,256]{1,0:T(8,128)(2,1)S(1)}, u32[]{:S(2)}, u32[]{:S(2)}) collective-permute-start(bf16[256,256]{1,0:T(8,128)(2,1)} %get-tuple-element.18.refs_1_.refs_2_), channel_id=1, source_target_pairs={{0,4},{4,0},{8,12},{12,8},{1,5},{5,1},{9,13},{13,9},{2,6},{6,2},{1... | collective-permute-start | bytes 393224 | tf_op jit(solution)/shard_map/ppermute | solution.py:328
  12.9 11.0 %collective-permute-start.5 = (bf16[256,256]{1,0:T(8,128)(2,1)S(1)}, bf16[256,256]{1,0:T(8,128)(2,1)S(1)}, u32[]{:S(2)}, u32[]{:S(2)}) collective-permute-start(bf16[256,256]{1,0:T(8,128)(2,1)S(1)} %collective-permute-done.2.refs_4_.refs_5_), channel_id=1, source_target_pairs={{0,1},{1,0},{2,3},{3,2},{4,5},{5,4},{6,7},{7,6},{8,9},{9,8},{10,11... | collective-permute-start | bytes 393224 | tf_op jit(solution)/shard_map/ppermute | solution.py:332
  19.5 17.8 %collective-permute-start.8 = (bf16[288,256]{1,0:T(8,128)(2,1)}, bf16[288,256]{1,0:T(8,128)(2,1)S(1)}, u32[]{:S(2)}, u32[]{:S(2)}) collective-permute-start(bf16[288,256]{1,0:T(8,128)(2,1)} %get-tuple-element.24.refs_10_), channel_id=1, source_target_pairs={{0,12},{4,8},{8,4},{12,0},{1,13},{5,9},{9,5},{13,1},{2,14},{6,10},... | collective-permute-start | bytes 442376 | tf_op jit(solution)/shard_map/ppermute | solution.py:328
  22.0 15.3 %collective-permute-start.7 = (bf16[288,256]{1,0:T(8,128)(2,1)}, bf16[288,256]{1,0:T(8,128)(2,1)S(1)}, u32[]{:S(2)}, u32[]{:S(2)}) collective-permute-start(bf16[288,256]{1,0:T(8,128)(2,1)} %get-tuple-element.24.refs_10_), channel_id=1, source_target_pairs={{0,8},{4,12},{8,0},{12,4},{1,9},{5,13},{9,1},{13,5},{2,10},{6,14},... | collective-permute-start | bytes 442376 | tf_op jit(solution)/shard_map/ppermute | solution.py:328
  22.0 15.3 %collective-permute-start.6 = (bf16[288,256]{1,0:T(8,128)(2,1)}, bf16[288,256]{1,0:T(8,128)(2,1)S(1)}, u32[]{:S(2)}, u32[]{:S(2)}) collective-permute-start(bf16[288,256]{1,0:T(8,128)(2,1)} %get-tuple-element.24.refs_10_), channel_id=1, source_target_pairs={{0,4},{4,0},{8,12},{12,8},{1,5},{5,1},{9,13},{13,9},{2,6},{6,2},{1... | collective-permute-start | bytes 442376 | tf_op jit(solution)/shard_map/ppermute | solution.py:328
  23.9 1.3 %collective-permute-start.4 = (bf16[256,256]{1,0:T(8,128)(2,1)S(1)}, bf16[256,256]{1,0:T(8,128)(2,1)S(1)}, u32[]{:S(2)}, u32[]{:S(2)}) collective-permute-start(bf16[256,256]{1,0:T(8,128)(2,1)S(1)} %collective-permute-done.1.refs_3_.refs_4_), channel_id=1, source_target_pairs={{0,1},{1,0},{2,3},{3,2},{4,5},{5,4},{6,7},{7,6},{8,9},{9,8},{10,11... | collective-permute-start | bytes 393224 | tf_op jit(solution)/shard_map/ppermute | solution.py:332
  23.9 1.5 %collective-permute-start.3 = (bf16[256,256]{1,0:T(8,128)(2,1)S(1)}, bf16[256,256]{1,0:T(8,128)(2,1)S(1)}, u32[]{:S(2)}, u32[]{:S(2)}) collective-permute-start(bf16[256,256]{1,0:T(8,128)(2,1)S(1)} %collective-permute-done.refs_2_.refs_3_), channel_id=1, source_target_pairs={{0,1},{1,0},{2,3},{3,2},{4,5},{5,4},{6,7},{7,6},{8,9},{9,8},{10,11... | collective-permute-start | bytes 393224 | tf_op jit(solution)/shard_map/ppermute | solution.py:332
  37.3 1.4 %collective-permute-start.9 = (bf16[288,256]{1,0:T(8,128)(2,1)S(1)}, bf16[288,256]{1,0:T(8,128)(2,1)S(1)}, u32[]{:S(2)}, u32[]{:S(2)}) collective-permute-start(bf16[288,256]{1,0:T(8,128)(2,1)S(1)} %collective-permute-done.6.refs_11_), channel_id=1, source_target_pairs={{0,1},{1,0},{2,3},{3,2},{4,5},{5,4},{6,7},{7,6},{8,9},{9,8},{10,11... | collective-permute-start | bytes 442376 | tf_op jit(solution)/shard_map/ppermute | solution.py:332
  37.7 1.4 %collective-permute-start.10 = (bf16[288,256]{1,0:T(8,128)(2,1)S(1)}, bf16[288,256]{1,0:T(8,128)(2,1)S(1)}, u32[]{:S(2)}, u32[]{:S(2)}) collective-permute-start(bf16[288,256]{1,0:T(8,128)(2,1)S(1)} %collective-permute-done.7.refs_12_), channel_id=1, source_target_pairs={{0,1},{1,0},{2,3},{3,2},{4,5},{5,4},{6,7},{7,6},{8,9},{9,8},{10,11... | collective-permute-start | bytes 442376 | tf_op jit(solution)/shard_map/ppermute | solution.py:332
  37.9 1.4 %collective-permute-start.11 = (bf16[288,256]{1,0:T(8,128)(2,1)S(1)}, bf16[288,256]{1,0:T(8,128)(2,1)S(1)}, u32[]{:S(2)}, u32[]{:S(2)}) collective-permute-start(bf16[288,256]{1,0:T(8,128)(2,1)S(1)} %collective-permute-done.8.refs_13_), channel_id=1, source_target_pairs={{0,1},{1,0},{2,3},{3,2},{4,5},{5,4},{6,7},{7,6},{8,9},{9,8},{10,11... | collective-permute-start | bytes 442376 | tf_op jit(solution)/shard_map/ppermute | solution.py:332
  55.7 6.8 %collective-permute-start.14 = (bf16[96,512]{1,0:T(8,128)(2,1)}, bf16[96,512]{1,0:T(8,128)(2,1)S(1)}, u32[]{:S(2)}, u32[]{:S(2)}) collective-permute-start(bf16[96,512]{1,0:T(8,128)(2,1)} %solve_tail.1.refs_0_), channel_id=1, source_target_pairs={{6,0},{4,2},{2,4},{0,6},{14,8},{12,10},{10,12},{8,14},{7,1},{5,3},... | collective-permute-start | bytes 294920 | tf_op jit(solution)/shard_map/ppermute | solution.py:374
  56.8 7.2 %collective-permute-start.13 = (bf16[96,512]{1,0:T(8,128)(2,1)}, bf16[96,512]{1,0:T(8,128)(2,1)S(1)}, u32[]{:S(2)}, u32[]{:S(2)}) collective-permute-start(bf16[96,512]{1,0:T(8,128)(2,1)} %solve_tail.1.refs_0_), channel_id=1, source_target_pairs={{4,0},{6,2},{0,4},{2,6},{12,8},{14,10},{8,12},{10,14},{5,1},{7,3},... | collective-permute-start | bytes 294920 | tf_op jit(solution)/shard_map/ppermute | solution.py:374
  58.7 5.3 %collective-permute-start.12 = (bf16[96,512]{1,0:T(8,128)(2,1)}, bf16[96,512]{1,0:T(8,128)(2,1)S(1)}, u32[]{:S(2)}, u32[]{:S(2)}) collective-permute-start(bf16[96,512]{1,0:T(8,128)(2,1)} %solve_tail.1.refs_0_), channel_id=1, source_target_pairs={{2,0},{0,2},{6,4},{4,6},{10,8},{8,10},{14,12},{12,14},{3,1},{1,3},... | collective-permute-start | bytes 294920 | tf_op jit(solution)/shard_map/ppermute | solution.py:374

commit v6 on v5

--- a/solution.py
+++ b/solution.py
@@ -83,16 +83,33 @@
             for q in systems:
                 for i in rest:
                     factors[q][i][u] = spread(panels[q][i][:, base_col + u : base_col + u + 1])
-        for t in range(8):
+        for t in range(0, 8, 2):
+            first_lane, second_lane = lane == base_col + t, lane == base_col + t + 1
+            first_row, second_row = sub == t, sub == t + 1
             for q in systems:
-                inverse = 1.0 / spread(cols[q][t][t : t + 1, :])
-                factor = jnp.where(sub == t, -1.0, cols[q][t])
-                for u in range(t + 1, 8):
-                    row = spread(cols[q][u][t : t + 1, :])
-                    cols[q][u] = jnp.where(sub == t, 0.0, cols[q][u]) - (factor * row) * inverse
-                row = jnp.where(lane == base_col + t, 1.0, spread(panels[q][b][t : t + 1, :]))
-                keep = jnp.where((lane == base_col + t) | (sub == t), 0.0, panels[q][b])
-                panels[q][b] = keep - (factor * row) * inverse
+                left, right, panel = cols[q][t], cols[q][t + 1], panels[q][b]
+                corner = spread(left[t : t + 1, :])
+                upper = spread(right[t : t + 1, :])
+                lower = spread(left[t + 1 : t + 2, :])
+                other = spread(right[t + 1 : t + 2, :])
+                inverse = 1.0 / corner
+                second = corner * (1.0 / (corner * other - upper * lower))
+                ratio = lower * inverse
+                factor = jnp.where(first_row, -1.0, left) * inverse
+                after = jnp.where(first_row, 0.0, right) - factor * upper
+                after = jnp.where(second_row, -1.0, after) * second
+                factor = jnp.where(second_row, 0.0, factor)
+                pair = first_row | second_row
+                for u in range(t + 2, 8):
+                    col = cols[q][u]
+                    row = spread(col[t : t + 1, :])
+                    next_row = spread(col[t + 1 : t + 2, :]) - ratio * row
+                    cols[q][u] = jnp.where(pair, 0.0, col) - factor * row - after * next_row
+                row = jnp.where(first_lane, 1.0, jnp.where(second_lane, 0.0, spread(panel[t : t + 1, :])))
+                next_row = jnp.where(first_lane, 0.0, spread(panel[t + 1 : t + 2, :])) - ratio * row
+                next_row = jnp.where(second_lane, 1.0, next_row)
+                keep = jnp.where(pair | first_lane | second_lane, 0.0, panel)
+                panels[q][b] = keep - factor * row - after * next_row
         for q in systems:
             rows = [spread(panels[q][b][t : t + 1, :]) for t in range(8)]
             for i in rest:
@@ -132,7 +149,7 @@
 def fold_lanes(own_count, width):
     pick = lax.rem(lax.axis_index("samples"), own_count)
     held = pl.multiple_of(pick * width, width)
-    train = [pl.multiple_of(lax.rem(pick + 1 + i, own_count) * width, width) for i in range(own_count - 1)]
+    train = [pl.multiple_of((pick ^ f) * width, width) for f in range(1, own_count)]
     return held, train
 
 
@@ -199,11 +216,11 @@
     stages(size // LANES, levels, out_ref, inv_ref, ones_ref, follow)
 
 
-def tail_kernel(sources, own_count, learning_tally, trait_rows, *refs):
+def tail_kernel(sources, own_count, learning_tally, traits, trait_rows, *refs):
     shrink_ref, lead_ref = refs[0:2]
     first = (refs[2 : 2 + sources], refs[2 + sources : 2 + 2 * sources])
     last = (refs[2 + 2 * sources : 2 + 3 * sources], refs[2 + 3 * sources : 2 + 4 * sources])
-    message_ref, wide_ref, solved_ref, mat_ref, inv_ref, ones_ref = refs[2 + 4 * sources :]
+    message_ref, trait_ref, wide_ref, solved_ref, mat_ref, inv_ref, ones_ref, beta_ref = refs[2 + 4 * sources :]
     levels, lead = lead_ref.shape[0], lead_ref.shape[1]
     size, total = mat_ref.shape[1], mat_ref.shape[2]
     width = first[0][0].shape[1] // own_count
@@ -237,45 +254,41 @@
         mat_ref[r, c0:c1, c1:total] = solved
 
     stages(size // LANES, levels, mat_ref, inv_ref, ones_ref, follow)
+    beta_ref[...] = jnp.zeros(beta_ref.shape, F32)
     for r in range(levels):
         low = mat_ref[r, :, size:total]
         top = solved_ref[r, :, size:total] - dot_f32(solved_ref[r, :, 0:size], low)
-        top = jnp.transpose(top)[0:trait_rows, :].astype(BF16)
-        low = jnp.transpose(low)[0:trait_rows, :].astype(BF16)
-        for s in range(sources):
-            value = jnp.dot(top, first[1][s][:, pl.ds(held, width)], preferred_element_type=F32) + jnp.dot(
-                low, last[1][s][0:size, pl.ds(held, width)], preferred_element_type=F32
-            )
-            message_ref[r * trait_rows : (r + 1) * trait_rows, s * width : (s + 1) * width] = value.astype(BF16)
+        beta_ref[r * traits : (r + 1) * traits, 0:lead] = jnp.transpose(top)[0:traits, :]
+        beta_ref[r * traits : (r + 1) * traits, lead : lead + size] = jnp.transpose(low)[0:traits, :]
+    betas = beta_ref[...].astype(BF16)
     for s in range(sources):
-        message_ref[levels * trait_rows : (levels + 1) * trait_rows, s * width : (s + 1) * width] = last[1][s][
-            size : size + trait_rows, pl.ds(held, width)
-        ]
-
-
-def level_kernel(own_count, trait_rows, held_rows, *refs):
-    pred_ref, gram_ref, cross_ref = refs[-3:]
-    n_blocks = (len(refs) - 3) // own_count
-    messages = [refs[f * n_blocks : (f + 1) * n_blocks] for f in range(own_count)]
+        lanes = slice(s * width, (s + 1) * width)
+        held_geno = jnp.concatenate(
+            [first[1][s][:, pl.ds(held, width)], last[1][s][0:size, pl.ds(held, width)]], axis=0
+        )
+        message_ref[:, lanes] = jnp.dot(betas, held_geno, preferred_element_type=F32).astype(BF16)
+        for f, start in enumerate([held] + train):
+            trait_ref[f, :, lanes] = last[1][s ^ f][size : size + trait_rows, pl.ds(start, width)]
+
+
+def level_kernel(own_count, trait_rows, held_rows, trait_ref, *refs):
+    pred_ref, gram_ref, cross_ref, wide_ref = refs[-4:]
+    n_blocks = (len(refs) - 4) // own_count
     traits, levels, width = pred_ref.shape[2:]
+    rows = round_up(traits, 8)
     me = lax.axis_index("samples")
     block = lax.axis_index("blocks")
     pick = lax.rem(me, own_count)
-    lane = lax.broadcasted_iota(jnp.int32, (trait_rows, LANES), 1)
+    lane = lax.broadcasted_iota(jnp.int32, (rows, LANES), 1)
     for f in range(own_count):
-        slot = lax.rem(pick + f, own_count)
-        mine = messages[f][0]
-        held = pl.multiple_of((me ^ (me - pick + slot)) * width, width)
-        own = [
-            mine[r * trait_rows : (r + 1) * trait_rows, pl.ds(held, width)].astype(F32)[0:traits]
-            for r in range(levels)
-        ]
-        pred_ref[slot, 0] = jnp.stack(own, axis=1).astype(BF16)
-        wide = [
-            [messages[f][e][s * trait_rows : (s + 1) * trait_rows, :].astype(F32) for s in range(levels)]
-            for e in range(n_blocks)
-        ]
-        trait = mine[levels * trait_rows : (levels + 1) * trait_rows, :].astype(F32)
+        slot = pick ^ f
+        for e in range(n_blocks):
+            wide_ref[e] = refs[f * n_blocks + e][...].astype(F32)
+        pred_ref[slot, 0] = jnp.stack(
+            [wide_ref[0, r * traits : (r + 1) * traits, f * width : (f + 1) * width] for r in range(levels)], axis=1
+        ).astype(BF16)
+        wide = [[wide_ref[e, s * traits : s * traits + rows, :] for s in range(levels)] for e in range(n_blocks)]
+        trait = trait_ref[f].astype(F32)[0:rows]
         for r in range(levels):
             out = jnp.where(lane == n_blocks * levels, jnp.sum(wide[0][r] * trait, axis=1, keepdims=True), 0.0)
             for e in range(n_blocks):
@@ -283,10 +296,10 @@
                 for s in range(levels):
                     total = jnp.sum(wide[0][r] * wide[e][s], axis=1, keepdims=True)
                     out = out + jnp.where(lane == column + s, total, 0.0)
-            rows = jnp.transpose(out) / held_rows
+            turned = jnp.transpose(out) / held_rows
             for c in range(n_blocks):
-                gram_ref[slot, 0, r, c] = rows[c * levels : (c + 1) * levels, 0:traits]
-            cross_ref[slot, 0, r : r + 1, :] = rows[n_blocks * levels : n_blocks * levels + 1, 0:traits]
+                gram_ref[slot, 0, r, c] = turned[c * levels : (c + 1) * levels, 0:traits]
+            cross_ref[slot, 0, r : r + 1, :] = turned[n_blocks * levels : n_blocks * levels + 1, 0:traits]
 
 
 def land(value, copies):
@@ -345,17 +358,22 @@
     )(shrink_strengths, *others_lead, *owns_lead)
     lead_inverse, *others_tail[1:] = lax.optimization_barrier((lead_inverse, *others_tail[1:]))
     owns_tail = swap(own_tail, others_tail)
-    message = pl.pallas_call(
-        functools.partial(tail_kernel, sources, own_count, learning_tally, trait_rows),
-        out_shape=jax.ShapeDtypeStruct(((levels + 1) * trait_rows, sources * width), BF16),
+    message_rows = round_up((levels - 1) * traits + round_up(traits, 8), 16)
+    message, trait_rows_held = pl.pallas_call(
+        functools.partial(tail_kernel, sources, own_count, learning_tally, traits, trait_rows),
+        out_shape=[
+            jax.ShapeDtypeStruct((message_rows, sources * width), BF16),
+            jax.ShapeDtypeStruct((own_count, trait_rows, sources * width), BF16),
+        ],
         in_specs=[smem] + [vmem] * (1 + 4 * sources),
-        out_specs=vmem,
+        out_specs=[vmem] * 2,
         scratch_shapes=[
             pltpu.VMEM((lead, size + LANES), F32),
             pltpu.VMEM((levels, lead, size + LANES), F32),
             pltpu.VMEM((levels, size, size + LANES), F32),
             pltpu.VMEM((levels, LANES, LANES), F32),
             pltpu.VMEM((8, LANES), F32),
+            pltpu.VMEM((message_rows, pad_rows), F32),
         ],
         name="solve_tail",
     )(shrink_strengths, lead_inverse, *others_lead, *owns_lead, *others_tail, *owns_tail)
@@ -368,9 +386,8 @@
                 continue
             pairs = []
             for s in range(sources):
-                source = s - s % own_count + (s % own_count + f) % own_count
                 for b in range(n_blocks):
-                    pairs.append((source * n_blocks + (b - e) % n_blocks, s * n_blocks + b))
+                    pairs.append(((s ^ f) * n_blocks + (b - e) % n_blocks, s * n_blocks + b))
             messages.append(land(lax.ppermute(message, ("samples", "blocks"), pairs), own_count * n_blocks))
 
     preds, gram, cross = pl.pallas_call(
@@ -380,10 +397,11 @@
             jax.ShapeDtypeStruct((own_count, 1, levels, n_blocks, levels, traits), F32),
             jax.ShapeDtypeStruct((own_count, 1, levels, traits), F32),
         ],
-        in_specs=[vmem] * len(messages),
+        in_specs=[vmem] * (1 + len(messages)),
         out_specs=[vmem] * 3,
+        scratch_shapes=[pltpu.VMEM((n_blocks, message_rows, sources * width), F32)],
         name="level_one",
-    )(*messages)
+    )(trait_rows_held, *messages)
     return jnp.swapaxes(preds, 2, 3), jnp.moveaxis(gram, 5, 3), cross
 
 

time: 65.9 us -> 62.7 us (0.951)
  Pallas kernels: 32.6 us -> 30.3 us
  waiting for transfers between devices: 17.6 us -> 16.6 us
    pallas_call x1, Pallas kernels: 16.5 us -> 15 us  [per_device(): pl.pallas_call(functools.partial(tail_kernel, sources, own_count, learnin...]
    ppermute x3, waiting for transfers between devices: 4.76 us -> 3.76 us  [per_device(): lax.ppermute(message, ('samples', 'blocks'), pairs)]
    pallas_call x1, Pallas kernels: 11.8 us -> 11 us  [per_device(): pl.pallas_call(functools.partial(lead_kernel, sources, own_count, learnin...]
  transfers between devices with their start and end apart: 15 -> 15, of which waited for: 9 -> 10; matrix products, arithmetic and copies ran while one was open for 0% -> 0% of each run, Pallas kernels for 18% -> 18%
where the time goes in v6:
time: 62.7 us; the launch traced here: 62.4 us
  Pallas kernels  30.3 us (48%)
  waiting for transfers between devices  16.6 us (26%)
  starting transfers between devices  14.9 us (24%)
  between operations  0.65 us (1%)
    pallas_call x1, Pallas kernels, per_device(): pl.pallas_call(functools.partial(tail_kernel, sources, own_count, learnin...  15 us
    pallas_call x1, Pallas kernels, per_device(): pl.pallas_call(functools.partial(lead_kernel, sources, own_count, learnin...  11 us
    ppermute x6, waiting for transfers between devices, fetch(): lax.ppermute(other, 'samples', [(i, i ^ d) for i in range(sources)])  10.7 us
    ppermute x6, starting transfers between devices, fetch(): lax.ppermute(other, 'samples', [(i, i ^ d) for i in range(sources)])  10 us
    ppermute x3, waiting for transfers between devices, per_device(): lax.ppermute(message, ('samples', 'blocks'), pairs)  3.76 us
    ppermute x3, starting transfers between devices, per_device(): lax.ppermute(message, ('samples', 'blocks'), pairs)  3.49 us
    pallas_call x1, Pallas kernels, per_device(): pl.pallas_call(functools.partial(sort_kernel, own_count, pad_rows), out_s...  2.5 us
    ppermute x6, waiting for transfers between devices, swap(): lax.ppermute(x, 'folds', [(i, cores - 1 - i) for i in range(cores)])  2.09 us
  transfers between devices with their start and end apart: 15, of which 10 were waited for; matrix products, arithmetic and copies ran while one was open for 0% of the time, Pallas kernels for 18%

profile of v6, /device:TPU:0, one launch (start us, length us, event | category | flops | bytes accessed | tf_op | source)
XLA Modules:
  0.0 62.4 jit_solution(5471358290621139612)
XLA Ops:
  0.6 2.5 %sort_samples.1 = (bf16[256,256]{1,0:T(8,128)(2,1)}, bf16[256,256]{1,0:T(8,128)(2,1)}, bf16[288,256]{1,0:T(8,128)(2,1)}, bf16[288,256]{1,0:T(8,128)(2,1)}) custom-call(bf16[500,512]{1,0:T(8,128)(2,1)} %geno_ref.1, bf16[20,512]{1,0:T(8,128)(2,1)} %trait_ref.1, s32[1,512]{1,0:T(1,128)} %bitcast.3), custom_call_target="tpu_custom_call" | custom-call | tf_op jit(solution)/shard_map/sort_samples/pallas_call | solution.py:330
  3.1 5.1 %collective-permute-start.2 = (bf16[256,256]{1,0:T(8,128)(2,1)}, bf16[256,256]{1,0:T(8,128)(2,1)S(1)}, u32[]{:S(2)}, u32[]{:S(2)}) collective-permute-start(bf16[256,256]{1,0:T(8,128)(2,1)} %get-tuple-element.20.refs_1_.refs_2_), channel_id=1, source_target_pairs={{0,12},{4,8},{8,4},{12,0},{1,13},{5,9},{9,5},{13,1},{2,14},{6,10},... | collective-permute-start | bytes 393224 | tf_op jit(solution)/shard_map/ppermute | solution.py:341
  8.2 0.0 collective-permute-start.1
  8.2 0.6 collective-permute-start
  8.8 4.1 %collective-permute-done.2.refs_4_.refs_5_ = bf16[256,256]{1,0:T(8,128)(2,1)S(1)} collective-permute-done((bf16[256,256]{1,0:T(8,128)(2,1)}, bf16[256,256]{1,0:T(8,128)(2,1)S(1)}, u32[]{:S(2)}, u32[]{:S(2)}) %collective-permute-start.2) | collective-permute-done | bytes 131104 | tf_op jit(solution)/shard_map/ppermute | solution.py:341
  12.9 0.0 collective-permute-start.5
  12.9 6.6 %collective-permute-done.1.refs_3_.refs_4_ = bf16[256,256]{1,0:T(8,128)(2,1)S(1)} collective-permute-done((bf16[256,256]{1,0:T(8,128)(2,1)}, bf16[256,256]{1,0:T(8,128)(2,1)S(1)}, u32[]{:S(2)}, u32[]{:S(2)}) %collective-permute-start.1) | collective-permute-done | bytes 131104 | tf_op jit(solution)/shard_map/ppermute | solution.py:341
  19.5 0.0 collective-permute-done.refs_2_.refs_3_
  19.5 2.5 %collective-permute-start.8 = (bf16[288,256]{1,0:T(8,128)(2,1)}, bf16[288,256]{1,0:T(8,128)(2,1)S(1)}, u32[]{:S(2)}, u32[]{:S(2)}) collective-permute-start(bf16[288,256]{1,0:T(8,128)(2,1)} %get-tuple-element.26.refs_10_), channel_id=1, source_target_pairs={{0,12},{4,8},{8,4},{12,0},{1,13},{5,9},{9,5},{13,1},{2,14},{6,10},... | collective-permute-start | bytes 442376 | tf_op jit(solution)/shard_map/ppermute | solution.py:341
  22.0 0.0 collective-permute-start.7
  22.0 1.9 %collective-permute-start.6 = (bf16[288,256]{1,0:T(8,128)(2,1)}, bf16[288,256]{1,0:T(8,128)(2,1)S(1)}, u32[]{:S(2)}, u32[]{:S(2)}) collective-permute-start(bf16[288,256]{1,0:T(8,128)(2,1)} %get-tuple-element.26.refs_10_), channel_id=1, source_target_pairs={{0,4},{4,0},{8,12},{12,8},{1,5},{5,1},{9,13},{13,9},{2,6},{6,2},{1... | collective-permute-start | bytes 442376 | tf_op jit(solution)/shard_map/ppermute | solution.py:341
  23.9 0.0 collective-permute-start.4
  23.9 0.0 collective-permute-done.5.refs_8_.refs_9_
  23.9 0.5 collective-permute-start.3
  24.4 0.8 %collective-permute-done.4.refs_7_.refs_8_ = bf16[256,256]{1,0:T(8,128)(2,1)S(1)} collective-permute-done((bf16[256,256]{1,0:T(8,128)(2,1)S(1)}, bf16[256,256]{1,0:T(8,128)(2,1)S(1)}, u32[]{:S(2)}, u32[]{:S(2)}) %collective-permute-start.4) | collective-permute-done | bytes 131104 | tf_op jit(solution)/shard_map/ppermute | solution.py:345
  25.2 0.2 collective-permute-done.3.refs_6_.refs_7_
  25.4 11.0 %invert_lead.1.refs_1_ = f32[2,256,256]{2,1,0:T(8,128)} custom-call(f32[2]{0:T(128)} %refs_0_.3, bf16[256,256]{1,0:T(8,128)(2,1)} %get-tuple-element.20.refs_1_.refs_2_, bf16[256,256]{1,0:T(8,128)(2,1)S(1)} %collective-permute-done.refs_2_.refs_3_, bf16[256,256]{1,0:T(8,128)(2,1)S(1)} %collective-permute-done.1.refs_3_.refs_4_, ...), custom_call_target="tpu_custom_call" | custom-call | tf_op jit(solution)/shard_map/invert_lead/pallas_call | solution.py:351
  36.4 0.0 collective-permute-done.8.refs_13_
  36.4 0.0 collective-permute-done.7.refs_12_
  36.5 0.0 collective-permute-done.6.refs_11_
  36.5 0.4 collective-permute-start.9
  36.9 0.2 collective-permute-start.10
  37.0 0.3 collective-permute-start.11
  37.4 0.5 collective-permute-done.9.refs_15_
  37.9 0.3 collective-permute-done.10.refs_16_
  38.2 0.2 collective-permute-done.11.refs_17_
  38.4 15.0 %solve_tail.1 = (bf16[48,512]{1,0:T(8,128)(2,1)}, bf16[2,32,512]{2,1,0:T(8,128)(2,1)}) custom-call(f32[2]{0:T(128)} %refs_0_.3, f32[2,256,256]{2,1,0:T(8,128)} %invert_lead.1.refs_1_, bf16[256,256]{1,0:T(8,128)(2,1)} %get-tuple-element.20.refs_1_.refs_2_, bf16[256,256]{1,0:T(8,128)(2,1)S(1)} %collective-permute-done.refs_2_.refs_3_, ...), custom_call_target="tpu_custom_call" | custom-call | tf_op jit(solution)/shard_map/solve_tail/pallas_call | solution.py:362
  53.5 1.0 %collective-permute-start.14 = (bf16[48,512]{1,0:T(8,128)(2,1)}, bf16[48,512]{1,0:T(8,128)(2,1)S(1)}, u32[]{:S(2)}, u32[]{:S(2)}) collective-permute-start(bf16[48,512]{1,0:T(8,128)(2,1)} %get-tuple-element.33.refs_0_), channel_id=1, source_target_pairs={{6,0},{4,2},{2,4},{0,6},{14,8},{12,10},{10,12},{8,14},{7,1},{5,3},... | collective-permute-start | bytes 147464 | tf_op jit(solution)/shard_map/ppermute | solution.py:391
  54.5 1.9 %collective-permute-start.13 = (bf16[48,512]{1,0:T(8,128)(2,1)}, bf16[48,512]{1,0:T(8,128)(2,1)S(1)}, u32[]{:S(2)}, u32[]{:S(2)}) collective-permute-start(bf16[48,512]{1,0:T(8,128)(2,1)} %get-tuple-element.33.refs_0_), channel_id=1, source_target_pairs={{4,0},{6,2},{0,4},{2,6},{12,8},{14,10},{8,12},{10,14},{5,1},{7,3},... | collective-permute-start | bytes 147464 | tf_op jit(solution)/shard_map/ppermute | solution.py:391
  56.4 0.5 collective-permute-start.12
  57.0 2.1 %collective-permute-done.14.refs_3_ = bf16[48,512]{1,0:T(8,128)(2,1)S(1)} collective-permute-done((bf16[48,512]{1,0:T(8,128)(2,1)}, bf16[48,512]{1,0:T(8,128)(2,1)S(1)}, u32[]{:S(2)}, u32[]{:S(2)}) %collective-permute-start.14) | collective-permute-done | bytes 49184 | tf_op jit(solution)/shard_map/ppermute | solution.py:391
  59.1 0.5 collective-permute-done.13.refs_2_
  59.6 1.1 %collective-permute-done.12.refs_1_ = bf16[48,512]{1,0:T(8,128)(2,1)S(1)} collective-permute-done((bf16[48,512]{1,0:T(8,128)(2,1)}, bf16[48,512]{1,0:T(8,128)(2,1)S(1)}, u32[]{:S(2)}, u32[]{:S(2)}) %collective-permute-start.12) | collective-permute-done | bytes 49184 | tf_op jit(solution)/shard_map/ppermute | solution.py:391
  60.7 1.7 %level_one.1 = (bf16[2,1,20,2,128]{4,3,2,1,0:T(2,128)(2,1)}, f32[2,1,2,2,2,20]{5,4,3,2,1,0:T(2,128)}, f32[2,1,2,20]{3,2,1,0:T(2,128)}) custom-call(bf16[2,32,512]{2,1,0:T(8,128)(2,1)} %get-tuple-element.32.trait_ref, bf16[48,512]{1,0:T(8,128)(2,1)} %get-tuple-element.33.refs_0_, bf16[48,512]{1,0:T(8,128)(2,1)S(1)} %collective-permute-done.12.refs_1_, ...), custom_call_target="tpu_custom_call" | custom-call | tf_op jit(solution)/shard_map/level_one/pallas_call | solution.py:393
Async XLA Ops:
  3.1 9.7 %collective-permute-start.2 = (bf16[256,256]{1,0:T(8,128)(2,1)}, bf16[256,256]{1,0:T(8,128)(2,1)S(1)}, u32[]{:S(2)}, u32[]{:S(2)}) collective-permute-start(bf16[256,256]{1,0:T(8,128)(2,1)} %get-tuple-element.20.refs_1_.refs_2_), channel_id=1, source_target_pairs={{0,12},{4,8},{8,4},{12,0},{1,13},{5,9},{9,5},{13,1},{2,14},{6,10},... | collective-permute-start | bytes 393224 | tf_op jit(solution)/shard_map/ppermute | solution.py:341
  8.2 11.3 %collective-permute-start.1 = (bf16[256,256]{1,0:T(8,128)(2,1)}, bf16[256,256]{1,0:T(8,128)(2,1)S(1)}, u32[]{:S(2)}, u32[]{:S(2)}) collective-permute-start(bf16[256,256]{1,0:T(8,128)(2,1)} %get-tuple-element.20.refs_1_.refs_2_), channel_id=1, source_target_pairs={{0,8},{4,12},{8,0},{12,4},{1,9},{5,13},{9,1},{13,5},{2,10},{6,14},... | collective-permute-start | bytes 393224 | tf_op jit(solution)/shard_map/ppermute | solution.py:341
  8.2 11.3 %collective-permute-start = (bf16[256,256]{1,0:T(8,128)(2,1)}, bf16[256,256]{1,0:T(8,128)(2,1)S(1)}, u32[]{:S(2)}, u32[]{:S(2)}) collective-permute-start(bf16[256,256]{1,0:T(8,128)(2,1)} %get-tuple-element.20.refs_1_.refs_2_), channel_id=1, source_target_pairs={{0,4},{4,0},{8,12},{12,8},{1,5},{5,1},{9,13},{13,9},{2,6},{6,2},{1... | collective-permute-start | bytes 393224 | tf_op jit(solution)/shard_map/ppermute | solution.py:341
  12.9 11.0 %collective-permute-start.5 = (bf16[256,256]{1,0:T(8,128)(2,1)S(1)}, bf16[256,256]{1,0:T(8,128)(2,1)S(1)}, u32[]{:S(2)}, u32[]{:S(2)}) collective-permute-start(bf16[256,256]{1,0:T(8,128)(2,1)S(1)} %collective-permute-done.2.refs_4_.refs_5_), channel_id=1, source_target_pairs={{0,1},{1,0},{2,3},{3,2},{4,5},{5,4},{6,7},{7,6},{8,9},{9,8},{10,11... | collective-permute-start | bytes 393224 | tf_op jit(solution)/shard_map/ppermute | solution.py:345
  19.5 17.0 %collective-permute-start.8 = (bf16[288,256]{1,0:T(8,128)(2,1)}, bf16[288,256]{1,0:T(8,128)(2,1)S(1)}, u32[]{:S(2)}, u32[]{:S(2)}) collective-permute-start(bf16[288,256]{1,0:T(8,128)(2,1)} %get-tuple-element.26.refs_10_), channel_id=1, source_target_pairs={{0,12},{4,8},{8,4},{12,0},{1,13},{5,9},{9,5},{13,1},{2,14},{6,10},... | collective-permute-start | bytes 442376 | tf_op jit(solution)/shard_map/ppermute | solution.py:341
  22.0 14.5 %collective-permute-start.7 = (bf16[288,256]{1,0:T(8,128)(2,1)}, bf16[288,256]{1,0:T(8,128)(2,1)S(1)}, u32[]{:S(2)}, u32[]{:S(2)}) collective-permute-start(bf16[288,256]{1,0:T(8,128)(2,1)} %get-tuple-element.26.refs_10_), channel_id=1, source_target_pairs={{0,8},{4,12},{8,0},{12,4},{1,9},{5,13},{9,1},{13,5},{2,10},{6,14},... | collective-permute-start | bytes 442376 | tf_op jit(solution)/shard_map/ppermute | solution.py:341
  22.0 14.5 %collective-permute-start.6 = (bf16[288,256]{1,0:T(8,128)(2,1)}, bf16[288,256]{1,0:T(8,128)(2,1)S(1)}, u32[]{:S(2)}, u32[]{:S(2)}) collective-permute-start(bf16[288,256]{1,0:T(8,128)(2,1)} %get-tuple-element.26.refs_10_), channel_id=1, source_target_pairs={{0,4},{4,0},{8,12},{12,8},{1,5},{5,1},{9,13},{13,9},{2,6},{6,2},{1... | collective-permute-start | bytes 442376 | tf_op jit(solution)/shard_map/ppermute | solution.py:341
  23.9 1.3 %collective-permute-start.4 = (bf16[256,256]{1,0:T(8,128)(2,1)S(1)}, bf16[256,256]{1,0:T(8,128)(2,1)S(1)}, u32[]{:S(2)}, u32[]{:S(2)}) collective-permute-start(bf16[256,256]{1,0:T(8,128)(2,1)S(1)} %collective-permute-done.1.refs_3_.refs_4_), channel_id=1, source_target_pairs={{0,1},{1,0},{2,3},{3,2},{4,5},{5,4},{6,7},{7,6},{8,9},{9,8},{10,11... | collective-permute-start | bytes 393224 | tf_op jit(solution)/shard_map/ppermute | solution.py:345
  23.9 1.5 %collective-permute-start.3 = (bf16[256,256]{1,0:T(8,128)(2,1)S(1)}, bf16[256,256]{1,0:T(8,128)(2,1)S(1)}, u32[]{:S(2)}, u32[]{:S(2)}) collective-permute-start(bf16[256,256]{1,0:T(8,128)(2,1)S(1)} %collective-permute-done.refs_2_.refs_3_), channel_id=1, source_target_pairs={{0,1},{1,0},{2,3},{3,2},{4,5},{5,4},{6,7},{7,6},{8,9},{9,8},{10,11... | collective-permute-start | bytes 393224 | tf_op jit(solution)/shard_map/ppermute | solution.py:345
  36.5 1.4 %collective-permute-start.9 = (bf16[288,256]{1,0:T(8,128)(2,1)S(1)}, bf16[288,256]{1,0:T(8,128)(2,1)S(1)}, u32[]{:S(2)}, u32[]{:S(2)}) collective-permute-start(bf16[288,256]{1,0:T(8,128)(2,1)S(1)} %collective-permute-done.6.refs_11_), channel_id=1, source_target_pairs={{0,1},{1,0},{2,3},{3,2},{4,5},{5,4},{6,7},{7,6},{8,9},{9,8},{10,11... | collective-permute-start | bytes 442376 | tf_op jit(solution)/shard_map/ppermute | solution.py:345
  36.9 1.4 %collective-permute-start.10 = (bf16[288,256]{1,0:T(8,128)(2,1)S(1)}, bf16[288,256]{1,0:T(8,128)(2,1)S(1)}, u32[]{:S(2)}, u32[]{:S(2)}) collective-permute-start(bf16[288,256]{1,0:T(8,128)(2,1)S(1)} %collective-permute-done.7.refs_12_), channel_id=1, source_target_pairs={{0,1},{1,0},{2,3},{3,2},{4,5},{5,4},{6,7},{7,6},{8,9},{9,8},{10,11... | collective-permute-start | bytes 442376 | tf_op jit(solution)/shard_map/ppermute | solution.py:345
  37.0 1.4 %collective-permute-start.11 = (bf16[288,256]{1,0:T(8,128)(2,1)S(1)}, bf16[288,256]{1,0:T(8,128)(2,1)S(1)}, u32[]{:S(2)}, u32[]{:S(2)}) collective-permute-start(bf16[288,256]{1,0:T(8,128)(2,1)S(1)} %collective-permute-done.8.refs_13_), channel_id=1, source_target_pairs={{0,1},{1,0},{2,3},{3,2},{4,5},{5,4},{6,7},{7,6},{8,9},{9,8},{10,11... | collective-permute-start | bytes 442376 | tf_op jit(solution)/shard_map/ppermute | solution.py:345
  53.5 5.6 %collective-permute-start.14 = (bf16[48,512]{1,0:T(8,128)(2,1)}, bf16[48,512]{1,0:T(8,128)(2,1)S(1)}, u32[]{:S(2)}, u32[]{:S(2)}) collective-permute-start(bf16[48,512]{1,0:T(8,128)(2,1)} %get-tuple-element.33.refs_0_), channel_id=1, source_target_pairs={{6,0},{4,2},{2,4},{0,6},{14,8},{12,10},{10,12},{8,14},{7,1},{5,3},... | collective-permute-start | bytes 147464 | tf_op jit(solution)/shard_map/ppermute | solution.py:391
  54.5 5.1 %collective-permute-start.13 = (bf16[48,512]{1,0:T(8,128)(2,1)}, bf16[48,512]{1,0:T(8,128)(2,1)S(1)}, u32[]{:S(2)}, u32[]{:S(2)}) collective-permute-start(bf16[48,512]{1,0:T(8,128)(2,1)} %get-tuple-element.33.refs_0_), channel_id=1, source_target_pairs={{4,0},{6,2},{0,4},{2,6},{12,8},{14,10},{8,12},{10,14},{5,1},{7,3},... | collective-permute-start | bytes 147464 | tf_op jit(solution)/shard_map/ppermute | solution.py:391
  56.4 4.3 %collective-permute-start.12 = (bf16[48,512]{1,0:T(8,128)(2,1)}, bf16[48,512]{1,0:T(8,128)(2,1)S(1)}, u32[]{:S(2)}, u32[]{:S(2)}) collective-permute-start(bf16[48,512]{1,0:T(8,128)(2,1)} %get-tuple-element.33.refs_0_), channel_id=1, source_target_pairs={{2,0},{0,2},{6,4},{4,6},{10,8},{8,10},{14,12},{12,14},{3,1},{1,3},... | collective-permute-start | bytes 147464 | tf_op jit(solution)/shard_map/ppermute | solution.py:391

commit v7 on v6

--- a/solution.py
+++ b/solution.py
@@ -30,8 +30,7 @@
     return jnp.broadcast_to(value, (8, LANES))
 
 
-def sort_kernel(own_count, pad_rows, geno_ref, trait_ref, label_ref, *refs):
-    variants, traits = geno_ref.shape[0], trait_ref.shape[0]
+def sort_kernel(own_count, offset, variants, geno_ref, trait_ref, label_ref, other_ref, own_ref):
     rows = label_ref.shape[1]
     core = lax.axis_index("folds")
     cores = lax.axis_size("folds")
@@ -49,19 +48,17 @@
     place = place.astype(jnp.int32)
     target = lax.broadcasted_iota(jnp.int32, (rows, rows), 0)
     move = jnp.where(target == jnp.broadcast_to(place, (rows, rows)), 1.0, 0.0).astype(BF16)
-    sorted_geno = dot_nt(geno_ref[...], move).astype(BF16)
-    sorted_trait = dot_nt(trait_ref[...], move).astype(BF16)
-    split = refs[0].shape[0]
-    half = refs[0].shape[1]
-    height = refs[2].shape[0]
-    low = (variants - split) // 16 * 16
-    for part in range(2):
+    sorted_geno = dot_nt(geno_ref[offset : offset + variants, :], move).astype(BF16)
+    height, half = other_ref.shape
+    size = height if trait_ref is None else height - round_up(trait_ref.shape[0], 32)
+    for part, ref in enumerate((other_ref, own_ref)):
         lanes = slice(part * half, (part + 1) * half)
-        refs[part][...] = sorted_geno[0:split, lanes]
-        ref = refs[2 + part]
-        ref[low:height, :] = jnp.zeros((height - low, half), BF16)
-        ref[0 : variants - split, :] = sorted_geno[split:variants, lanes]
-        ref[pad_rows - split : pad_rows - split + traits, :] = sorted_trait[:, lanes]
+        low = variants // 16 * 16
+        if low < height:
+            ref[low:height, :] = jnp.zeros((height - low, half), BF16)
+        ref[0:variants, :] = sorted_geno[:, lanes]
+        if trait_ref is not None:
+            ref[size : size + trait_ref.shape[0], :] = dot_nt(trait_ref[...], move)[:, lanes].astype(BF16)
 
 
 def eliminate_panel(panels, first, ones):
@@ -232,7 +229,7 @@
         wide_ref[rows, 0:height] = training_product(first, last, train, width, rows) / learning_tally
         wide_ref[rows, height:total] = jnp.zeros((LANES, total - height), F32)
     for r in range(levels):
-        solved_ref[r] = dot_f32(lead_ref[r], wide_ref[...])
+        solved_ref[:, r * total : (r + 1) * total] = dot_f32(lead_ref[r], wide_ref[...])
     diagonal = lax.broadcasted_iota(jnp.int32, (LANES, height), 1) - lax.broadcasted_iota(
         jnp.int32, (LANES, height), 0
     )
@@ -240,10 +237,12 @@
         rows = slice(r0, r0 + LANES)
         side = training_product(last, first, train, width, rows) / learning_tally
         acc = training_product(last, last, train, width, rows) / learning_tally
+        known = dot_f32(side, solved_ref[...])
         for r in range(levels):
-            mat_ref[r, rows, 0:height] = acc + jnp.where(diagonal == r0, shrink_ref[r], 0.0)
+            mat_ref[r, rows, 0:height] = (
+                acc + jnp.where(diagonal == r0, shrink_ref[r], 0.0) - known[:, r * total : r * total + height]
+            )
             mat_ref[r, rows, height:total] = jnp.zeros((LANES, total - height), F32)
-            mat_ref[r, rows, :] = mat_ref[r, rows, :] - dot_f32(side, solved_ref[r])
 
     def follow(j, r):
         c0, c1 = j * LANES, (j + 1) * LANES
@@ -257,7 +256,9 @@
     beta_ref[...] = jnp.zeros(beta_ref.shape, F32)
     for r in range(levels):
         low = mat_ref[r, :, size:total]
-        top = solved_ref[r, :, size:total] - dot_f32(solved_ref[r, :, 0:size], low)
+        top = solved_ref[:, r * total + size : (r + 1) * total] - dot_f32(
+            solved_ref[:, r * total : r * total + size], low
+        )
         beta_ref[r * traits : (r + 1) * traits, 0:lead] = jnp.transpose(top)[0:traits, :]
         beta_ref[r * traits : (r + 1) * traits, lead : lead + size] = jnp.transpose(low)[0:traits, :]
     betas = beta_ref[...].astype(BF16)
@@ -327,14 +328,33 @@
     vmem = pl.BlockSpec(memory_space=pltpu.VMEM)
     smem = pl.BlockSpec(memory_space=pltpu.SMEM)
 
-    other_lead, own_lead, other_tail, own_tail = pl.pallas_call(
-        functools.partial(sort_kernel, own_count, pad_rows),
-        out_shape=[jax.ShapeDtypeStruct((lead, half), BF16)] * 2
-        + [jax.ShapeDtypeStruct((size + trait_rows, half), BF16)] * 2,
-        in_specs=[vmem] * 3,
-        out_specs=[vmem] * 4,
-        name="sort_samples",
-    )(allele_dosage_table, phenotype_values, individual_partition_label.reshape(1, samples))
+    def sort(offset, height, with_traits):
+        count = min(variants - offset, height)
+        inputs = [allele_dosage_table, phenotype_values, individual_partition_label.reshape(1, samples)]
+        block = lead if lead == size else variants
+        specs = [
+            pl.BlockSpec((block, samples), lambda i: (offset // block, 0)),
+            pl.BlockSpec((traits, samples), lambda i: (0, 0)),
+            pl.BlockSpec((1, samples), lambda i: (0, 0)),
+        ]
+        kernel = functools.partial(sort_kernel, own_count, offset % block, count)
+        if not with_traits:
+            del inputs[1], specs[1]
+
+            def kernel(geno_ref, label_ref, *outs):
+                sort_kernel(own_count, offset % block, count, geno_ref, None, label_ref, *outs)
+
+        return pl.pallas_call(
+            kernel,
+            grid=(1,),
+            out_shape=[jax.ShapeDtypeStruct((height, half), BF16)] * 2,
+            in_specs=specs,
+            out_specs=[pl.BlockSpec((height, half), lambda i: (0, 0))] * 2,
+            name="sort_samples",
+        )(*inputs)
+
+    other_lead, own_lead = sort(0, lead, False)
+    other_tail, own_tail = sort(lead, size + trait_rows, True)
 
     def fetch(other):
         return [other] + [
@@ -369,7 +389,7 @@
         out_specs=[vmem] * 2,
         scratch_shapes=[
             pltpu.VMEM((lead, size + LANES), F32),
-            pltpu.VMEM((levels, lead, size + LANES), F32),
+            pltpu.VMEM((lead, levels * (size + LANES)), F32),
             pltpu.VMEM((levels, size, size + LANES), F32),
             pltpu.VMEM((levels, LANES, LANES), F32),
             pltpu.VMEM((8, LANES), F32),

time: 62.7 us -> 62.1 us (level)
  waiting for transfers between devices: 16.6 us -> 14.3 us
  Pallas kernels: 30.3 us -> 32 us
    ppermute x6, waiting for transfers between devices: 10.7 us -> 8.45 us  [fetch(): lax.ppermute(other, 'samples', [(i, i ^ d) for i in range(sources)])]
    pallas_call x1 -> x2, Pallas kernels: 2.5 us -> 4.42 us  [sort(): pl.pallas_call(kernel, grid=(1,), out_shape=[jax.ShapeDtypeStruct((height...]
  transfers between devices with their start and end apart: 15 -> 15, of which waited for: 10 -> 10; matrix products, arithmetic and copies ran while one was open for 0% -> 0% of each run, Pallas kernels for 18% -> 22%
where the time goes in v7:
time: 62.1 us; the launch traced here: 61.9 us
  Pallas kernels  32 us (52%)
  starting transfers between devices  14.9 us (24%)
  waiting for transfers between devices  14.3 us (23%)
  between operations  0.65 us (1%)
    pallas_call x1, Pallas kernels, per_device(): pl.pallas_call(functools.partial(tail_kernel, sources, own_count, learnin...  14.8 us
    pallas_call x1, Pallas kernels, per_device(): pl.pallas_call(functools.partial(lead_kernel, sources, own_count, learnin...  11 us
    ppermute x6, starting transfers between devices, fetch(): lax.ppermute(other, 'samples', [(i, i ^ d) for i in range(sources)])  10 us
    ppermute x6, waiting for transfers between devices, fetch(): lax.ppermute(other, 'samples', [(i, i ^ d) for i in range(sources)])  8.45 us
    pallas_call x2, Pallas kernels, sort(): pl.pallas_call(kernel, grid=(1,), out_shape=[jax.ShapeDtypeStruct((height...  4.42 us
    ppermute x3, waiting for transfers between devices, per_device(): lax.ppermute(message, ('samples', 'blocks'), pairs)  3.77 us
    ppermute x3, starting transfers between devices, per_device(): lax.ppermute(message, ('samples', 'blocks'), pairs)  3.49 us
    ppermute x6, waiting for transfers between devices, swap(): lax.ppermute(x, 'folds', [(i, cores - 1 - i) for i in range(cores)])  2.09 us
  transfers between devices with their start and end apart: 15, of which 10 were waited for; matrix products, arithmetic and copies ran while one was open for 0% of the time, Pallas kernels for 22%

profile of v7, /device:TPU:0, one launch (start us, length us, event | category | flops | bytes accessed | tf_op | source)
XLA Modules:
  0.0 61.9 jit_solution(6691386935121316522)
XLA Ops:
  0.6 2.2 %sort_samples.2 = (bf16[256,256]{1,0:T(8,128)(2,1)}, bf16[256,256]{1,0:T(8,128)(2,1)}) custom-call(bf16[500,512]{1,0:T(8,128)(2,1)} %geno_ref.3, s32[1,512]{1,0:T(1,128)} %bitcast.3), custom_call_target="tpu_custom_call" | custom-call | tf_op jit(solution)/shard_map/sort_samples/pallas_call | solution.py:347
  2.8 5.1 %collective-permute-start.2 = (bf16[256,256]{1,0:T(8,128)(2,1)}, bf16[256,256]{1,0:T(8,128)(2,1)S(1)}, u32[]{:S(2)}, u32[]{:S(2)}) collective-permute-start(bf16[256,256]{1,0:T(8,128)(2,1)} %get-tuple-element.20.refs_1_.refs_2_), channel_id=1, source_target_pairs={{0,12},{4,8},{8,4},{12,0},{1,13},{5,9},{9,5},{13,1},{2,14},{6,10},... | collective-permute-start | bytes 393224 | tf_op jit(solution)/shard_map/ppermute | solution.py:361
  7.9 0.0 collective-permute-start.1
  7.9 0.6 collective-permute-start
  8.4 4.1 %collective-permute-done.2.refs_4_.refs_5_ = bf16[256,256]{1,0:T(8,128)(2,1)S(1)} collective-permute-done((bf16[256,256]{1,0:T(8,128)(2,1)}, bf16[256,256]{1,0:T(8,128)(2,1)S(1)}, u32[]{:S(2)}, u32[]{:S(2)}) %collective-permute-start.2) | collective-permute-done | bytes 131104 | tf_op jit(solution)/shard_map/ppermute | solution.py:361
  12.5 0.0 collective-permute-start.5
  12.5 2.3 %sort_samples.3 = (bf16[288,256]{1,0:T(8,128)(2,1)}, bf16[288,256]{1,0:T(8,128)(2,1)}) custom-call(bf16[500,512]{1,0:T(8,128)(2,1)} %geno_ref.3, bf16[20,512]{1,0:T(8,128)(2,1)} %trait_ref.1, s32[1,512]{1,0:T(1,128)} %bitcast.4), custom_call_target="tpu_custom_call" | custom-call | tf_op jit(solution)/shard_map/sort_samples/pallas_call | solution.py:347
  14.8 4.3 %collective-permute-done.1.refs_3_.refs_4_ = bf16[256,256]{1,0:T(8,128)(2,1)S(1)} collective-permute-done((bf16[256,256]{1,0:T(8,128)(2,1)}, bf16[256,256]{1,0:T(8,128)(2,1)S(1)}, u32[]{:S(2)}, u32[]{:S(2)}) %collective-permute-start.1) | collective-permute-done | bytes 131104 | tf_op jit(solution)/shard_map/ppermute | solution.py:361
  19.1 0.0 collective-permute-done.refs_2_.refs_3_
  19.2 2.5 %collective-permute-start.8 = (bf16[288,256]{1,0:T(8,128)(2,1)}, bf16[288,256]{1,0:T(8,128)(2,1)S(1)}, u32[]{:S(2)}, u32[]{:S(2)}) collective-permute-start(bf16[288,256]{1,0:T(8,128)(2,1)} %get-tuple-element.26.refs_10_), channel_id=1, source_target_pairs={{0,12},{4,8},{8,4},{12,0},{1,13},{5,9},{9,5},{13,1},{2,14},{6,10},... | collective-permute-start | bytes 442376 | tf_op jit(solution)/shard_map/ppermute | solution.py:361
  21.6 0.0 collective-permute-start.7
  21.7 1.9 %collective-permute-start.6 = (bf16[288,256]{1,0:T(8,128)(2,1)}, bf16[288,256]{1,0:T(8,128)(2,1)S(1)}, u32[]{:S(2)}, u32[]{:S(2)}) collective-permute-start(bf16[288,256]{1,0:T(8,128)(2,1)} %get-tuple-element.26.refs_10_), channel_id=1, source_target_pairs={{0,4},{4,0},{8,12},{12,8},{1,5},{5,1},{9,13},{13,9},{2,6},{6,2},{1... | collective-permute-start | bytes 442376 | tf_op jit(solution)/shard_map/ppermute | solution.py:361
  23.5 0.0 collective-permute-start.4
  23.5 0.0 collective-permute-done.5.refs_8_.refs_9_
  23.5 0.5 collective-permute-start.3
  24.1 0.8 %collective-permute-done.4.refs_7_.refs_8_ = bf16[256,256]{1,0:T(8,128)(2,1)S(1)} collective-permute-done((bf16[256,256]{1,0:T(8,128)(2,1)S(1)}, bf16[256,256]{1,0:T(8,128)(2,1)S(1)}, u32[]{:S(2)}, u32[]{:S(2)}) %collective-permute-start.4) | collective-permute-done | bytes 131104 | tf_op jit(solution)/shard_map/ppermute | solution.py:365
  24.9 0.2 collective-permute-done.3.refs_6_.refs_7_
  25.1 11.0 %invert_lead.1.refs_1_ = f32[2,256,256]{2,1,0:T(8,128)} custom-call(f32[2]{0:T(128)} %refs_0_.3, bf16[256,256]{1,0:T(8,128)(2,1)} %get-tuple-element.20.refs_1_.refs_2_, bf16[256,256]{1,0:T(8,128)(2,1)S(1)} %collective-permute-done.refs_2_.refs_3_, bf16[256,256]{1,0:T(8,128)(2,1)S(1)} %collective-permute-done.1.refs_3_.refs_4_, ...), custom_call_target="tpu_custom_call" | custom-call | tf_op jit(solution)/shard_map/invert_lead/pallas_call | solution.py:371
  36.1 0.0 collective-permute-done.8.refs_13_
  36.1 0.0 collective-permute-done.7.refs_12_
  36.1 0.0 collective-permute-done.6.refs_11_
  36.1 0.4 collective-permute-start.9
  36.5 0.2 collective-permute-start.10
  36.7 0.3 collective-permute-start.11
  37.0 0.5 collective-permute-done.9.refs_15_
  37.6 0.3 collective-permute-done.10.refs_16_
  37.9 0.2 collective-permute-done.11.refs_17_
  38.1 14.8 %solve_tail.1 = (bf16[48,512]{1,0:T(8,128)(2,1)}, bf16[2,32,512]{2,1,0:T(8,128)(2,1)}) custom-call(f32[2]{0:T(128)} %refs_0_.3, f32[2,256,256]{2,1,0:T(8,128)} %invert_lead.1.refs_1_, bf16[256,256]{1,0:T(8,128)(2,1)} %get-tuple-element.20.refs_1_.refs_2_, bf16[256,256]{1,0:T(8,128)(2,1)S(1)} %collective-permute-done.refs_2_.refs_3_, ...), custom_call_target="tpu_custom_call" | custom-call | tf_op jit(solution)/shard_map/solve_tail/pallas_call | solution.py:382
  52.9 1.1 %collective-permute-start.14 = (bf16[48,512]{1,0:T(8,128)(2,1)}, bf16[48,512]{1,0:T(8,128)(2,1)S(1)}, u32[]{:S(2)}, u32[]{:S(2)}) collective-permute-start(bf16[48,512]{1,0:T(8,128)(2,1)} %get-tuple-element.33.refs_0_), channel_id=1, source_target_pairs={{6,0},{4,2},{2,4},{0,6},{14,8},{12,10},{10,12},{8,14},{7,1},{5,3},... | collective-permute-start | bytes 147464 | tf_op jit(solution)/shard_map/ppermute | solution.py:411
  54.0 1.9 %collective-permute-start.13 = (bf16[48,512]{1,0:T(8,128)(2,1)}, bf16[48,512]{1,0:T(8,128)(2,1)S(1)}, u32[]{:S(2)}, u32[]{:S(2)}) collective-permute-start(bf16[48,512]{1,0:T(8,128)(2,1)} %get-tuple-element.33.refs_0_), channel_id=1, source_target_pairs={{4,0},{6,2},{0,4},{2,6},{12,8},{14,10},{8,12},{10,14},{5,1},{7,3},... | collective-permute-start | bytes 147464 | tf_op jit(solution)/shard_map/ppermute | solution.py:411
  55.9 0.5 collective-permute-start.12
  56.4 2.1 %collective-permute-done.14.refs_3_ = bf16[48,512]{1,0:T(8,128)(2,1)S(1)} collective-permute-done((bf16[48,512]{1,0:T(8,128)(2,1)}, bf16[48,512]{1,0:T(8,128)(2,1)S(1)}, u32[]{:S(2)}, u32[]{:S(2)}) %collective-permute-start.14) | collective-permute-done | bytes 49184 | tf_op jit(solution)/shard_map/ppermute | solution.py:411
  58.5 0.6 collective-permute-done.13.refs_2_
  59.0 1.1 %collective-permute-done.12.refs_1_ = bf16[48,512]{1,0:T(8,128)(2,1)S(1)} collective-permute-done((bf16[48,512]{1,0:T(8,128)(2,1)}, bf16[48,512]{1,0:T(8,128)(2,1)S(1)}, u32[]{:S(2)}, u32[]{:S(2)}) %collective-permute-start.12) | collective-permute-done | bytes 49184 | tf_op jit(solution)/shard_map/ppermute | solution.py:411
  60.2 1.7 %level_one.1 = (bf16[2,1,20,2,128]{4,3,2,1,0:T(2,128)(2,1)}, f32[2,1,2,2,2,20]{5,4,3,2,1,0:T(2,128)}, f32[2,1,2,20]{3,2,1,0:T(2,128)}) custom-call(bf16[2,32,512]{2,1,0:T(8,128)(2,1)} %get-tuple-element.32.trait_ref, bf16[48,512]{1,0:T(8,128)(2,1)} %get-tuple-element.33.refs_0_, bf16[48,512]{1,0:T(8,128)(2,1)S(1)} %collective-permute-done.12.refs_1_, ...), custom_call_target="tpu_custom_call" | custom-call | tf_op jit(solution)/shard_map/level_one/pallas_call | solution.py:413
Async XLA Ops:
  2.8 9.7 %collective-permute-start.2 = (bf16[256,256]{1,0:T(8,128)(2,1)}, bf16[256,256]{1,0:T(8,128)(2,1)S(1)}, u32[]{:S(2)}, u32[]{:S(2)}) collective-permute-start(bf16[256,256]{1,0:T(8,128)(2,1)} %get-tuple-element.20.refs_1_.refs_2_), channel_id=1, source_target_pairs={{0,12},{4,8},{8,4},{12,0},{1,13},{5,9},{9,5},{13,1},{2,14},{6,10},... | collective-permute-start | bytes 393224 | tf_op jit(solution)/shard_map/ppermute | solution.py:361
  7.9 11.3 %collective-permute-start.1 = (bf16[256,256]{1,0:T(8,128)(2,1)}, bf16[256,256]{1,0:T(8,128)(2,1)S(1)}, u32[]{:S(2)}, u32[]{:S(2)}) collective-permute-start(bf16[256,256]{1,0:T(8,128)(2,1)} %get-tuple-element.20.refs_1_.refs_2_), channel_id=1, source_target_pairs={{0,8},{4,12},{8,0},{12,4},{1,9},{5,13},{9,1},{13,5},{2,10},{6,14},... | collective-permute-start | bytes 393224 | tf_op jit(solution)/shard_map/ppermute | solution.py:361
  7.9 11.3 %collective-permute-start = (bf16[256,256]{1,0:T(8,128)(2,1)}, bf16[256,256]{1,0:T(8,128)(2,1)S(1)}, u32[]{:S(2)}, u32[]{:S(2)}) collective-permute-start(bf16[256,256]{1,0:T(8,128)(2,1)} %get-tuple-element.20.refs_1_.refs_2_), channel_id=1, source_target_pairs={{0,4},{4,0},{8,12},{12,8},{1,5},{5,1},{9,13},{13,9},{2,6},{6,2},{1... | collective-permute-start | bytes 393224 | tf_op jit(solution)/shard_map/ppermute | solution.py:361
  12.5 11.0 %collective-permute-start.5 = (bf16[256,256]{1,0:T(8,128)(2,1)S(1)}, bf16[256,256]{1,0:T(8,128)(2,1)S(1)}, u32[]{:S(2)}, u32[]{:S(2)}) collective-permute-start(bf16[256,256]{1,0:T(8,128)(2,1)S(1)} %collective-permute-done.2.refs_4_.refs_5_), channel_id=1, source_target_pairs={{0,1},{1,0},{2,3},{3,2},{4,5},{5,4},{6,7},{7,6},{8,9},{9,8},{10,11... | collective-permute-start | bytes 393224 | tf_op jit(solution)/shard_map/ppermute | solution.py:365
  19.2 17.0 %collective-permute-start.8 = (bf16[288,256]{1,0:T(8,128)(2,1)}, bf16[288,256]{1,0:T(8,128)(2,1)S(1)}, u32[]{:S(2)}, u32[]{:S(2)}) collective-permute-start(bf16[288,256]{1,0:T(8,128)(2,1)} %get-tuple-element.26.refs_10_), channel_id=1, source_target_pairs={{0,12},{4,8},{8,4},{12,0},{1,13},{5,9},{9,5},{13,1},{2,14},{6,10},... | collective-permute-start | bytes 442376 | tf_op jit(solution)/shard_map/ppermute | solution.py:361
  21.6 14.5 %collective-permute-start.7 = (bf16[288,256]{1,0:T(8,128)(2,1)}, bf16[288,256]{1,0:T(8,128)(2,1)S(1)}, u32[]{:S(2)}, u32[]{:S(2)}) collective-permute-start(bf16[288,256]{1,0:T(8,128)(2,1)} %get-tuple-element.26.refs_10_), channel_id=1, source_target_pairs={{0,8},{4,12},{8,0},{12,4},{1,9},{5,13},{9,1},{13,5},{2,10},{6,14},... | collective-permute-start | bytes 442376 | tf_op jit(solution)/shard_map/ppermute | solution.py:361
  21.7 14.5 %collective-permute-start.6 = (bf16[288,256]{1,0:T(8,128)(2,1)}, bf16[288,256]{1,0:T(8,128)(2,1)S(1)}, u32[]{:S(2)}, u32[]{:S(2)}) collective-permute-start(bf16[288,256]{1,0:T(8,128)(2,1)} %get-tuple-element.26.refs_10_), channel_id=1, source_target_pairs={{0,4},{4,0},{8,12},{12,8},{1,5},{5,1},{9,13},{13,9},{2,6},{6,2},{1... | collective-permute-start | bytes 442376 | tf_op jit(solution)/shard_map/ppermute | solution.py:361
  23.5 1.3 %collective-permute-start.4 = (bf16[256,256]{1,0:T(8,128)(2,1)S(1)}, bf16[256,256]{1,0:T(8,128)(2,1)S(1)}, u32[]{:S(2)}, u32[]{:S(2)}) collective-permute-start(bf16[256,256]{1,0:T(8,128)(2,1)S(1)} %collective-permute-done.1.refs_3_.refs_4_), channel_id=1, source_target_pairs={{0,1},{1,0},{2,3},{3,2},{4,5},{5,4},{6,7},{7,6},{8,9},{9,8},{10,11... | collective-permute-start | bytes 393224 | tf_op jit(solution)/shard_map/ppermute | solution.py:365
  23.5 1.5 %collective-permute-start.3 = (bf16[256,256]{1,0:T(8,128)(2,1)S(1)}, bf16[256,256]{1,0:T(8,128)(2,1)S(1)}, u32[]{:S(2)}, u32[]{:S(2)}) collective-permute-start(bf16[256,256]{1,0:T(8,128)(2,1)S(1)} %collective-permute-done.refs_2_.refs_3_), channel_id=1, source_target_pairs={{0,1},{1,0},{2,3},{3,2},{4,5},{5,4},{6,7},{7,6},{8,9},{9,8},{10,11... | collective-permute-start | bytes 393224 | tf_op jit(solution)/shard_map/ppermute | solution.py:365
  36.1 1.4 %collective-permute-start.9 = (bf16[288,256]{1,0:T(8,128)(2,1)S(1)}, bf16[288,256]{1,0:T(8,128)(2,1)S(1)}, u32[]{:S(2)}, u32[]{:S(2)}) collective-permute-start(bf16[288,256]{1,0:T(8,128)(2,1)S(1)} %collective-permute-done.6.refs_11_), channel_id=1, source_target_pairs={{0,1},{1,0},{2,3},{3,2},{4,5},{5,4},{6,7},{7,6},{8,9},{9,8},{10,11... | collective-permute-start | bytes 442376 | tf_op jit(solution)/shard_map/ppermute | solution.py:365
  36.5 1.4 %collective-permute-start.10 = (bf16[288,256]{1,0:T(8,128)(2,1)S(1)}, bf16[288,256]{1,0:T(8,128)(2,1)S(1)}, u32[]{:S(2)}, u32[]{:S(2)}) collective-permute-start(bf16[288,256]{1,0:T(8,128)(2,1)S(1)} %collective-permute-done.7.refs_12_), channel_id=1, source_target_pairs={{0,1},{1,0},{2,3},{3,2},{4,5},{5,4},{6,7},{7,6},{8,9},{9,8},{10,11... | collective-permute-start | bytes 442376 | tf_op jit(solution)/shard_map/ppermute | solution.py:365
  36.7 1.4 %collective-permute-start.11 = (bf16[288,256]{1,0:T(8,128)(2,1)S(1)}, bf16[288,256]{1,0:T(8,128)(2,1)S(1)}, u32[]{:S(2)}, u32[]{:S(2)}) collective-permute-start(bf16[288,256]{1,0:T(8,128)(2,1)S(1)} %collective-permute-done.8.refs_13_), channel_id=1, source_target_pairs={{0,1},{1,0},{2,3},{3,2},{4,5},{5,4},{6,7},{7,6},{8,9},{9,8},{10,11... | collective-permute-start | bytes 442376 | tf_op jit(solution)/shard_map/ppermute | solution.py:365
  52.9 5.6 %collective-permute-start.14 = (bf16[48,512]{1,0:T(8,128)(2,1)}, bf16[48,512]{1,0:T(8,128)(2,1)S(1)}, u32[]{:S(2)}, u32[]{:S(2)}) collective-permute-start(bf16[48,512]{1,0:T(8,128)(2,1)} %get-tuple-element.33.refs_0_), channel_id=1, source_target_pairs={{6,0},{4,2},{2,4},{0,6},{14,8},{12,10},{10,12},{8,14},{7,1},{5,3},... | collective-permute-start | bytes 147464 | tf_op jit(solution)/shard_map/ppermute | solution.py:411
  54.0 5.1 %collective-permute-start.13 = (bf16[48,512]{1,0:T(8,128)(2,1)}, bf16[48,512]{1,0:T(8,128)(2,1)S(1)}, u32[]{:S(2)}, u32[]{:S(2)}) collective-permute-start(bf16[48,512]{1,0:T(8,128)(2,1)} %get-tuple-element.33.refs_0_), channel_id=1, source_target_pairs={{4,0},{6,2},{0,4},{2,6},{12,8},{14,10},{8,12},{10,14},{5,1},{7,3},... | collective-permute-start | bytes 147464 | tf_op jit(solution)/shard_map/ppermute | solution.py:411
  55.9 4.3 %collective-permute-start.12 = (bf16[48,512]{1,0:T(8,128)(2,1)}, bf16[48,512]{1,0:T(8,128)(2,1)S(1)}, u32[]{:S(2)}, u32[]{:S(2)}) collective-permute-start(bf16[48,512]{1,0:T(8,128)(2,1)} %get-tuple-element.33.refs_0_), channel_id=1, source_target_pairs={{2,0},{0,2},{6,4},{4,6},{10,8},{8,10},{14,12},{12,14},{3,1},{1,3},... | collective-permute-start | bytes 147464 | tf_op jit(solution)/shard_map/ppermute | solution.py:411

commit v8 on v7

--- a/solution.py
+++ b/solution.py
@@ -309,6 +309,13 @@
     return pltpu.with_memory_space_constraint(value, pltpu.VMEM)
 
 
+def kept(shape, dtype, copies):
+    struct = jax.ShapeDtypeStruct(shape, dtype)
+    if copies * struct.size * struct.dtype.itemsize > VMEM_SHARE:
+        return struct
+    return pltpu.VMEM(shape, dtype)
+
+
 def per_device(allele_dosage_table, phenotype_values, individual_partition_label, shrink_strengths):
     cores = lax.axis_size("folds")
     sources = lax.axis_size("samples")
@@ -347,7 +354,7 @@
         return pl.pallas_call(
             kernel,
             grid=(1,),
-            out_shape=[jax.ShapeDtypeStruct((height, half), BF16)] * 2,
+            out_shape=[kept((height, half), BF16, 2 * sources)] * 2,
             in_specs=specs,
             out_specs=[pl.BlockSpec((height, half), lambda i: (0, 0))] * 2,
             name="sort_samples",
@@ -357,12 +364,12 @@
     other_tail, own_tail = sort(lead, size + trait_rows, True)
 
     def fetch(other):
-        return [other] + [
+        return [land(other, 2 * sources)] + [
             land(lax.ppermute(other, "samples", [(i, i ^ d) for i in range(sources)]), 2 * sources) for d in range(1, sources)
         ]
 
     def swap(own, others):
-        return [own] + [land(lax.ppermute(x, "folds", [(i, cores - 1 - i) for i in range(cores)]), 2 * sources) for x in others[1:]]
+        return [land(own, 2 * sources)] + [land(lax.ppermute(x, "folds", [(i, cores - 1 - i) for i in range(cores)]), 2 * sources) for x in others[1:]]
 
     others_lead = fetch(other_lead)
     owns_lead = swap(own_lead, others_lead)
@@ -370,20 +377,21 @@
     others_tail = fetch(other_tail)
     lead_inverse = pl.pallas_call(
         functools.partial(lead_kernel, sources, own_count, learning_tally),
-        out_shape=jax.ShapeDtypeStruct((levels, lead, lead), F32),
+        out_shape=kept((levels, lead, lead), F32, sources // 2),
         in_specs=[smem] + [vmem] * (2 * sources),
         out_specs=vmem,
         scratch_shapes=[pltpu.VMEM((levels, LANES, LANES), F32), pltpu.VMEM((8, LANES), F32)],
         name="invert_lead",
     )(shrink_strengths, *others_lead, *owns_lead)
     lead_inverse, *others_tail[1:] = lax.optimization_barrier((lead_inverse, *others_tail[1:]))
+    lead_inverse = land(lead_inverse, sources // 2)
     owns_tail = swap(own_tail, others_tail)
     message_rows = round_up((levels - 1) * traits + round_up(traits, 8), 16)
     message, trait_rows_held = pl.pallas_call(
         functools.partial(tail_kernel, sources, own_count, learning_tally, traits, trait_rows),
         out_shape=[
-            jax.ShapeDtypeStruct((message_rows, sources * width), BF16),
-            jax.ShapeDtypeStruct((own_count, trait_rows, sources * width), BF16),
+            kept((message_rows, sources * width), BF16, sources),
+            kept((own_count, trait_rows, sources * width), BF16, sources),
         ],
         in_specs=[smem] + [vmem] * (1 + 4 * sources),
         out_specs=[vmem] * 2,
@@ -402,7 +410,7 @@
     for f in range(own_count):
         for e in range(n_blocks):
             if f == 0 and e == 0:
-                messages.append(message)
+                messages.append(land(message, own_count * n_blocks))
                 continue
             pairs = []
             for s in range(sources):
@@ -421,7 +429,7 @@
         out_specs=[vmem] * 3,
         scratch_shapes=[pltpu.VMEM((n_blocks, message_rows, sources * width), F32)],
         name="level_one",
-    )(trait_rows_held, *messages)
+    )(land(trait_rows_held, sources), *messages)
     return jnp.swapaxes(preds, 2, 3), jnp.moveaxis(gram, 5, 3), cross
 
 

time: 62.1 us -> 57.9 us (0.932)
  Pallas kernels: 32 us -> 27.4 us
    pallas_call x2, Pallas kernels: 4.42 us -> 3.02 us  [sort(): pl.pallas_call(kernel, grid=(1,), out_shape=[kept((height, half), BF16, 2...]
    pallas_call x1, Pallas kernels: 14.8 us -> 13.5 us  [per_device(): pl.pallas_call(functools.partial(tail_kernel, sources, own_count, learnin...]
    pallas_call x1, Pallas kernels: 11 us -> 9.92 us  [per_device(): pl.pallas_call(functools.partial(lead_kernel, sources, own_count, learnin...]
    pallas_call x1, Pallas kernels: 1.71 us -> 0.87 us  [per_device(): pl.pallas_call(functools.partial(level_kernel, own_count, trait_rows, hel...]
  transfers between devices with their start and end apart: 15 -> 15, of which waited for: 10 -> 10; matrix products, arithmetic and copies ran while one was open for 0% -> 0% of each run, Pallas kernels for 22% -> 20%
where the time goes in v8:
time: 57.9 us; the launch traced here: 57.7 us
  Pallas kernels  27.4 us (47%)
  starting transfers between devices  15.1 us (26%)
  waiting for transfers between devices  14.5 us (25%)
  between operations  0.69 us (1%)
    pallas_call x1, Pallas kernels, per_device(): pl.pallas_call(functools.partial(tail_kernel, sources, own_count, learnin...  13.5 us
    ppermute x6, starting transfers between devices, fetch(): lax.ppermute(other, 'samples', [(i, i ^ d) for i in range(sources)])  10.2 us
    pallas_call x1, Pallas kernels, per_device(): pl.pallas_call(functools.partial(lead_kernel, sources, own_count, learnin...  9.92 us
    ppermute x6, waiting for transfers between devices, fetch(): lax.ppermute(other, 'samples', [(i, i ^ d) for i in range(sources)])  8.88 us
    ppermute x3, waiting for transfers between devices, per_device(): lax.ppermute(message, ('samples', 'blocks'), pairs)  3.56 us
    ppermute x3, starting transfers between devices, per_device(): lax.ppermute(message, ('samples', 'blocks'), pairs)  3.55 us
    pallas_call x2, Pallas kernels, sort(): pl.pallas_call(kernel, grid=(1,), out_shape=[kept((height, half), BF16, 2...  3.02 us
    ppermute x6, waiting for transfers between devices, swap(): lax.ppermute(x, 'folds', [(i, cores - 1 - i) for i in range(cores)])  2.09 us
  transfers between devices with their start and end apart: 15, of which 10 were waited for; matrix products, arithmetic and copies ran while one was open for 0% of the time, Pallas kernels for 20%

profile of v8, /device:TPU:0, one launch (start us, length us, event | category | flops | bytes accessed | tf_op | source)
XLA Modules:
  0.0 57.7 jit_solution(14139971651013004963)
XLA Ops:
  0.6 1.5 %sort_samples.2 = (bf16[256,256]{1,0:T(8,128)(2,1)S(1)}, bf16[256,256]{1,0:T(8,128)(2,1)S(1)}) custom-call(bf16[500,512]{1,0:T(8,128)(2,1)} %geno_ref.3, s32[1,512]{1,0:T(1,128)} %bitcast.3), custom_call_target="tpu_custom_call" | custom-call | tf_op jit(solution)/shard_map/sort_samples/pallas_call | solution.py:354
  2.1 5.1 %collective-permute-start.2 = (bf16[256,256]{1,0:T(8,128)(2,1)S(1)}, bf16[256,256]{1,0:T(8,128)(2,1)S(1)}, u32[]{:S(2)}, u32[]{:S(2)}) collective-permute-start(bf16[256,256]{1,0:T(8,128)(2,1)S(1)} %get-tuple-element.20.refs_1_.refs_2_), channel_id=1, source_target_pairs={{0,12},{4,8},{8,4},{12,0},{1,13},{5,9},{9,5},{13,1},{2,14},{6,10},... | collective-permute-start | bytes 393224 | tf_op jit(solution)/shard_map/ppermute | solution.py:368
  7.2 0.0 collective-permute-start.1
  7.3 0.6 %collective-permute-start = (bf16[256,256]{1,0:T(8,128)(2,1)S(1)}, bf16[256,256]{1,0:T(8,128)(2,1)S(1)}, u32[]{:S(2)}, u32[]{:S(2)}) collective-permute-start(bf16[256,256]{1,0:T(8,128)(2,1)S(1)} %get-tuple-element.20.refs_1_.refs_2_), channel_id=1, source_target_pairs={{0,4},{4,0},{8,12},{12,8},{1,5},{5,1},{9,13},{13,9},{2,6},{6,2},{1... | collective-permute-start | bytes 393224 | tf_op jit(solution)/shard_map/ppermute | solution.py:368
  7.9 3.8 %collective-permute-done.2.refs_4_.refs_5_ = bf16[256,256]{1,0:T(8,128)(2,1)S(1)} collective-permute-done((bf16[256,256]{1,0:T(8,128)(2,1)S(1)}, bf16[256,256]{1,0:T(8,128)(2,1)S(1)}, u32[]{:S(2)}, u32[]{:S(2)}) %collective-permute-start.2) | collective-permute-done | bytes 131104 | tf_op jit(solution)/shard_map/ppermute | solution.py:368
  11.7 0.0 collective-permute-start.5
  11.7 1.6 %sort_samples.3 = (bf16[288,256]{1,0:T(8,128)(2,1)S(1)}, bf16[288,256]{1,0:T(8,128)(2,1)S(1)}) custom-call(bf16[500,512]{1,0:T(8,128)(2,1)} %geno_ref.3, bf16[20,512]{1,0:T(8,128)(2,1)} %trait_ref.1, s32[1,512]{1,0:T(1,128)} %bitcast.4), custom_call_target="tpu_custom_call" | custom-call | tf_op jit(solution)/shard_map/sort_samples/pallas_call | solution.py:354
  13.3 5.1 %collective-permute-done.1.refs_3_.refs_4_ = bf16[256,256]{1,0:T(8,128)(2,1)S(1)} collective-permute-done((bf16[256,256]{1,0:T(8,128)(2,1)S(1)}, bf16[256,256]{1,0:T(8,128)(2,1)S(1)}, u32[]{:S(2)}, u32[]{:S(2)}) %collective-permute-start.1) | collective-permute-done | bytes 131104 | tf_op jit(solution)/shard_map/ppermute | solution.py:368
  18.3 0.0 collective-permute-done.refs_2_.refs_3_
  18.3 2.5 %collective-permute-start.8 = (bf16[288,256]{1,0:T(8,128)(2,1)S(1)}, bf16[288,256]{1,0:T(8,128)(2,1)S(1)}, u32[]{:S(2)}, u32[]{:S(2)}) collective-permute-start(bf16[288,256]{1,0:T(8,128)(2,1)S(1)} %get-tuple-element.26.refs_10_), channel_id=1, source_target_pairs={{0,12},{4,8},{8,4},{12,0},{1,13},{5,9},{9,5},{13,1},{2,14},{6,10},... | collective-permute-start | bytes 442376 | tf_op jit(solution)/shard_map/ppermute | solution.py:368
  20.8 0.0 collective-permute-start.7
  20.8 1.9 %collective-permute-start.6 = (bf16[288,256]{1,0:T(8,128)(2,1)S(1)}, bf16[288,256]{1,0:T(8,128)(2,1)S(1)}, u32[]{:S(2)}, u32[]{:S(2)}) collective-permute-start(bf16[288,256]{1,0:T(8,128)(2,1)S(1)} %get-tuple-element.26.refs_10_), channel_id=1, source_target_pairs={{0,4},{4,0},{8,12},{12,8},{1,5},{5,1},{9,13},{13,9},{2,6},{6,2},{1... | collective-permute-start | bytes 442376 | tf_op jit(solution)/shard_map/ppermute | solution.py:368
  22.7 0.0 collective-permute-start.4
  22.7 0.0 collective-permute-done.5.refs_8_.refs_9_
  22.7 0.5 collective-permute-start.3
  23.2 0.8 %collective-permute-done.4.refs_7_.refs_8_ = bf16[256,256]{1,0:T(8,128)(2,1)S(1)} collective-permute-done((bf16[256,256]{1,0:T(8,128)(2,1)S(1)}, bf16[256,256]{1,0:T(8,128)(2,1)S(1)}, u32[]{:S(2)}, u32[]{:S(2)}) %collective-permute-start.4) | collective-permute-done | bytes 131104 | tf_op jit(solution)/shard_map/ppermute | solution.py:372
  24.1 0.2 collective-permute-done.3.refs_6_.refs_7_
  24.2 9.9 %invert_lead.1.refs_1_ = f32[2,256,256]{2,1,0:T(8,128)S(1)} custom-call(f32[2]{0:T(128)} %refs_0_.3, bf16[256,256]{1,0:T(8,128)(2,1)S(1)} %get-tuple-element.20.refs_1_.refs_2_, bf16[256,256]{1,0:T(8,128)(2,1)S(1)} %collective-permute-done.refs_2_.refs_3_, bf16[256,256]{1,0:T(8,128)(2,1)S(1)} %collective-permute-done.1.refs_3_.refs_4_, ...), custom_call_target="tpu_custom_call" | custom-call | tf_op jit(solution)/shard_map/invert_lead/pallas_call | solution.py:378
  34.2 0.0 collective-permute-done.8.refs_13_
  34.2 0.0 collective-permute-done.7.refs_12_
  34.2 0.0 collective-permute-done.6.refs_11_
  34.2 0.4 collective-permute-start.9
  34.6 0.2 collective-permute-start.10
  34.8 0.3 collective-permute-start.11
  35.1 0.5 collective-permute-done.9.refs_15_
  35.6 0.3 collective-permute-done.10.refs_16_
  36.0 0.2 collective-permute-done.11.refs_17_
  36.2 13.5 %solve_tail.1 = (bf16[48,512]{1,0:T(8,128)(2,1)S(1)}, bf16[2,32,512]{2,1,0:T(8,128)(2,1)S(1)}) custom-call(f32[2]{0:T(128)} %refs_0_.3, f32[2,256,256]{2,1,0:T(8,128)S(1)} %invert_lead.1.refs_1_, bf16[256,256]{1,0:T(8,128)(2,1)S(1)} %get-tuple-element.20.refs_1_.refs_2_, bf16[256,256]{1,0:T(8,128)(2,1)S(1)} %collective-permute-done.refs_2_.refs_3_, ...), custom_call_target="tpu_custom_call" | custom-call | tf_op jit(solution)/shard_map/solve_tail/pallas_call | solution.py:390
  49.7 1.1 %collective-permute-start.14 = (bf16[48,512]{1,0:T(8,128)(2,1)S(1)}, bf16[48,512]{1,0:T(8,128)(2,1)S(1)}, u32[]{:S(2)}, u32[]{:S(2)}) collective-permute-start(bf16[48,512]{1,0:T(8,128)(2,1)S(1)} %get-tuple-element.33.refs_0_), channel_id=1, source_target_pairs={{6,0},{4,2},{2,4},{0,6},{14,8},{12,10},{10,12},{8,14},{7,1},{5,3},... | collective-permute-start | bytes 147464 | tf_op jit(solution)/shard_map/ppermute | solution.py:419
  50.8 1.9 %collective-permute-start.13 = (bf16[48,512]{1,0:T(8,128)(2,1)S(1)}, bf16[48,512]{1,0:T(8,128)(2,1)S(1)}, u32[]{:S(2)}, u32[]{:S(2)}) collective-permute-start(bf16[48,512]{1,0:T(8,128)(2,1)S(1)} %get-tuple-element.33.refs_0_), channel_id=1, source_target_pairs={{4,0},{6,2},{0,4},{2,6},{12,8},{14,10},{8,12},{10,14},{5,1},{7,3},... | collective-permute-start | bytes 147464 | tf_op jit(solution)/shard_map/ppermute | solution.py:419
  52.8 0.5 collective-permute-start.12
  53.3 1.9 %collective-permute-done.14.refs_3_ = bf16[48,512]{1,0:T(8,128)(2,1)S(1)} collective-permute-done((bf16[48,512]{1,0:T(8,128)(2,1)S(1)}, bf16[48,512]{1,0:T(8,128)(2,1)S(1)}, u32[]{:S(2)}, u32[]{:S(2)}) %collective-permute-start.14) | collective-permute-done | bytes 49184 | tf_op jit(solution)/shard_map/ppermute | solution.py:419
  55.2 0.6 collective-permute-done.13.refs_2_
  55.7 1.1 %collective-permute-done.12.refs_1_ = bf16[48,512]{1,0:T(8,128)(2,1)S(1)} collective-permute-done((bf16[48,512]{1,0:T(8,128)(2,1)S(1)}, bf16[48,512]{1,0:T(8,128)(2,1)S(1)}, u32[]{:S(2)}, u32[]{:S(2)}) %collective-permute-start.12) | collective-permute-done | bytes 49184 | tf_op jit(solution)/shard_map/ppermute | solution.py:419
  56.8 0.9 %level_one.1 = (bf16[2,1,20,2,128]{4,3,2,1,0:T(2,128)(2,1)}, f32[2,1,2,2,2,20]{5,4,3,2,1,0:T(2,128)}, f32[2,1,2,20]{3,2,1,0:T(2,128)}) custom-call(bf16[2,32,512]{2,1,0:T(8,128)(2,1)S(1)} %get-tuple-element.32.trait_ref, bf16[48,512]{1,0:T(8,128)(2,1)S(1)} %get-tuple-element.33.refs_0_, bf16[48,512]{1,0:T(8,128)(2,1)S(1)} %collective-permute-done.12.refs_1_, ...), custom_call_target="tpu_custom_call" | custom-call | tf_op jit(solution)/shard_map/level_one/pallas_call | solution.py:421
Async XLA Ops:
  2.1 9.6 %collective-permute-start.2 = (bf16[256,256]{1,0:T(8,128)(2,1)S(1)}, bf16[256,256]{1,0:T(8,128)(2,1)S(1)}, u32[]{:S(2)}, u32[]{:S(2)}) collective-permute-start(bf16[256,256]{1,0:T(8,128)(2,1)S(1)} %get-tuple-element.20.refs_1_.refs_2_), channel_id=1, source_target_pairs={{0,12},{4,8},{8,4},{12,0},{1,13},{5,9},{9,5},{13,1},{2,14},{6,10},... | collective-permute-start | bytes 393224 | tf_op jit(solution)/shard_map/ppermute | solution.py:368
  7.2 11.1 %collective-permute-start.1 = (bf16[256,256]{1,0:T(8,128)(2,1)S(1)}, bf16[256,256]{1,0:T(8,128)(2,1)S(1)}, u32[]{:S(2)}, u32[]{:S(2)}) collective-permute-start(bf16[256,256]{1,0:T(8,128)(2,1)S(1)} %get-tuple-element.20.refs_1_.refs_2_), channel_id=1, source_target_pairs={{0,8},{4,12},{8,0},{12,4},{1,9},{5,13},{9,1},{13,5},{2,10},{6,14},... | collective-permute-start | bytes 393224 | tf_op jit(solution)/shard_map/ppermute | solution.py:368
  7.3 11.1 %collective-permute-start = (bf16[256,256]{1,0:T(8,128)(2,1)S(1)}, bf16[256,256]{1,0:T(8,128)(2,1)S(1)}, u32[]{:S(2)}, u32[]{:S(2)}) collective-permute-start(bf16[256,256]{1,0:T(8,128)(2,1)S(1)} %get-tuple-element.20.refs_1_.refs_2_), channel_id=1, source_target_pairs={{0,4},{4,0},{8,12},{12,8},{1,5},{5,1},{9,13},{13,9},{2,6},{6,2},{1... | collective-permute-start | bytes 393224 | tf_op jit(solution)/shard_map/ppermute | solution.py:368
  11.7 11.0 %collective-permute-start.5 = (bf16[256,256]{1,0:T(8,128)(2,1)S(1)}, bf16[256,256]{1,0:T(8,128)(2,1)S(1)}, u32[]{:S(2)}, u32[]{:S(2)}) collective-permute-start(bf16[256,256]{1,0:T(8,128)(2,1)S(1)} %collective-permute-done.2.refs_4_.refs_5_), channel_id=1, source_target_pairs={{0,1},{1,0},{2,3},{3,2},{4,5},{5,4},{6,7},{7,6},{8,9},{9,8},{10,11... | collective-permute-start | bytes 393224 | tf_op jit(solution)/shard_map/ppermute | solution.py:372
  18.3 15.9 %collective-permute-start.8 = (bf16[288,256]{1,0:T(8,128)(2,1)S(1)}, bf16[288,256]{1,0:T(8,128)(2,1)S(1)}, u32[]{:S(2)}, u32[]{:S(2)}) collective-permute-start(bf16[288,256]{1,0:T(8,128)(2,1)S(1)} %get-tuple-element.26.refs_10_), channel_id=1, source_target_pairs={{0,12},{4,8},{8,4},{12,0},{1,13},{5,9},{9,5},{13,1},{2,14},{6,10},... | collective-permute-start | bytes 442376 | tf_op jit(solution)/shard_map/ppermute | solution.py:368
  20.8 13.4 %collective-permute-start.7 = (bf16[288,256]{1,0:T(8,128)(2,1)S(1)}, bf16[288,256]{1,0:T(8,128)(2,1)S(1)}, u32[]{:S(2)}, u32[]{:S(2)}) collective-permute-start(bf16[288,256]{1,0:T(8,128)(2,1)S(1)} %get-tuple-element.26.refs_10_), channel_id=1, source_target_pairs={{0,8},{4,12},{8,0},{12,4},{1,9},{5,13},{9,1},{13,5},{2,10},{6,14},... | collective-permute-start | bytes 442376 | tf_op jit(solution)/shard_map/ppermute | solution.py:368
  20.8 13.4 %collective-permute-start.6 = (bf16[288,256]{1,0:T(8,128)(2,1)S(1)}, bf16[288,256]{1,0:T(8,128)(2,1)S(1)}, u32[]{:S(2)}, u32[]{:S(2)}) collective-permute-start(bf16[288,256]{1,0:T(8,128)(2,1)S(1)} %get-tuple-element.26.refs_10_), channel_id=1, source_target_pairs={{0,4},{4,0},{8,12},{12,8},{1,5},{5,1},{9,13},{13,9},{2,6},{6,2},{1... | collective-permute-start | bytes 442376 | tf_op jit(solution)/shard_map/ppermute | solution.py:368
  22.7 1.3 %collective-permute-start.4 = (bf16[256,256]{1,0:T(8,128)(2,1)S(1)}, bf16[256,256]{1,0:T(8,128)(2,1)S(1)}, u32[]{:S(2)}, u32[]{:S(2)}) collective-permute-start(bf16[256,256]{1,0:T(8,128)(2,1)S(1)} %collective-permute-done.1.refs_3_.refs_4_), channel_id=1, source_target_pairs={{0,1},{1,0},{2,3},{3,2},{4,5},{5,4},{6,7},{7,6},{8,9},{9,8},{10,11... | collective-permute-start | bytes 393224 | tf_op jit(solution)/shard_map/ppermute | solution.py:372
  22.7 1.5 %collective-permute-start.3 = (bf16[256,256]{1,0:T(8,128)(2,1)S(1)}, bf16[256,256]{1,0:T(8,128)(2,1)S(1)}, u32[]{:S(2)}, u32[]{:S(2)}) collective-permute-start(bf16[256,256]{1,0:T(8,128)(2,1)S(1)} %collective-permute-done.refs_2_.refs_3_), channel_id=1, source_target_pairs={{0,1},{1,0},{2,3},{3,2},{4,5},{5,4},{6,7},{7,6},{8,9},{9,8},{10,11... | collective-permute-start | bytes 393224 | tf_op jit(solution)/shard_map/ppermute | solution.py:372
  34.2 1.4 %collective-permute-start.9 = (bf16[288,256]{1,0:T(8,128)(2,1)S(1)}, bf16[288,256]{1,0:T(8,128)(2,1)S(1)}, u32[]{:S(2)}, u32[]{:S(2)}) collective-permute-start(bf16[288,256]{1,0:T(8,128)(2,1)S(1)} %collective-permute-done.6.refs_11_), channel_id=1, source_target_pairs={{0,1},{1,0},{2,3},{3,2},{4,5},{5,4},{6,7},{7,6},{8,9},{9,8},{10,11... | collective-permute-start | bytes 442376 | tf_op jit(solution)/shard_map/ppermute | solution.py:372
  34.6 1.4 %collective-permute-start.10 = (bf16[288,256]{1,0:T(8,128)(2,1)S(1)}, bf16[288,256]{1,0:T(8,128)(2,1)S(1)}, u32[]{:S(2)}, u32[]{:S(2)}) collective-permute-start(bf16[288,256]{1,0:T(8,128)(2,1)S(1)} %collective-permute-done.7.refs_12_), channel_id=1, source_target_pairs={{0,1},{1,0},{2,3},{3,2},{4,5},{5,4},{6,7},{7,6},{8,9},{9,8},{10,11... | collective-permute-start | bytes 442376 | tf_op jit(solution)/shard_map/ppermute | solution.py:372
  34.8 1.4 %collective-permute-start.11 = (bf16[288,256]{1,0:T(8,128)(2,1)S(1)}, bf16[288,256]{1,0:T(8,128)(2,1)S(1)}, u32[]{:S(2)}, u32[]{:S(2)}) collective-permute-start(bf16[288,256]{1,0:T(8,128)(2,1)S(1)} %collective-permute-done.8.refs_13_), channel_id=1, source_target_pairs={{0,1},{1,0},{2,3},{3,2},{4,5},{5,4},{6,7},{7,6},{8,9},{9,8},{10,11... | collective-permute-start | bytes 442376 | tf_op jit(solution)/shard_map/ppermute | solution.py:372
  49.7 5.4 %collective-permute-start.14 = (bf16[48,512]{1,0:T(8,128)(2,1)S(1)}, bf16[48,512]{1,0:T(8,128)(2,1)S(1)}, u32[]{:S(2)}, u32[]{:S(2)}) collective-permute-start(bf16[48,512]{1,0:T(8,128)(2,1)S(1)} %get-tuple-element.33.refs_0_), channel_id=1, source_target_pairs={{6,0},{4,2},{2,4},{0,6},{14,8},{12,10},{10,12},{8,14},{7,1},{5,3},... | collective-permute-start | bytes 147464 | tf_op jit(solution)/shard_map/ppermute | solution.py:419
  50.8 4.9 %collective-permute-start.13 = (bf16[48,512]{1,0:T(8,128)(2,1)S(1)}, bf16[48,512]{1,0:T(8,128)(2,1)S(1)}, u32[]{:S(2)}, u32[]{:S(2)}) collective-permute-start(bf16[48,512]{1,0:T(8,128)(2,1)S(1)} %get-tuple-element.33.refs_0_), channel_id=1, source_target_pairs={{4,0},{6,2},{0,4},{2,6},{12,8},{14,10},{8,12},{10,14},{5,1},{7,3},... | collective-permute-start | bytes 147464 | tf_op jit(solution)/shard_map/ppermute | solution.py:419
  52.8 4.1 %collective-permute-start.12 = (bf16[48,512]{1,0:T(8,128)(2,1)S(1)}, bf16[48,512]{1,0:T(8,128)(2,1)S(1)}, u32[]{:S(2)}, u32[]{:S(2)}) collective-permute-start(bf16[48,512]{1,0:T(8,128)(2,1)S(1)} %get-tuple-element.33.refs_0_), channel_id=1, source_target_pairs={{2,0},{0,2},{6,4},{4,6},{10,8},{8,10},{14,12},{12,14},{3,1},{1,3},... | collective-permute-start | bytes 147464 | tf_op jit(solution)/shard_map/ppermute | solution.py:419

commit v9 on v8

--- a/solution.py
+++ b/solution.py
@@ -189,12 +189,10 @@
     width = others[0].shape[1] // own_count
     _, train = fold_lanes(own_count, width)
     ones_ref[...] = jnp.ones((8, LANES), F32)
-    diagonal = lax.broadcasted_iota(jnp.int32, (LANES, size), 1) - lax.broadcasted_iota(jnp.int32, (LANES, size), 0)
-    for r0 in range(0, size, LANES):
-        rows = slice(r0, r0 + LANES)
-        acc = training_product((others, owns), (others, owns), train, width, rows) / learning_tally
-        for r in range(levels):
-            out_ref[r, rows, :] = acc + jnp.where(diagonal == r0, shrink_ref[r], 0.0)
+    diagonal = lax.broadcasted_iota(jnp.int32, (size, size), 1) == lax.broadcasted_iota(jnp.int32, (size, size), 0)
+    acc = training_product((others, owns), (others, owns), train, width, slice(0, size)) / learning_tally
+    for r in range(levels):
+        out_ref[r] = acc + jnp.where(diagonal, shrink_ref[r], 0.0)
 
     def follow(j, r):
         c0, c1 = j * LANES, (j + 1) * LANES
@@ -224,25 +222,23 @@
     height = size + trait_rows
     held, train = fold_lanes(own_count, width)
     ones_ref[...] = jnp.ones((8, LANES), F32)
-    for r0 in range(0, lead, LANES):
-        rows = slice(r0, r0 + LANES)
-        wide_ref[rows, 0:height] = training_product(first, last, train, width, rows) / learning_tally
-        wide_ref[rows, height:total] = jnp.zeros((LANES, total - height), F32)
+    wide_ref[:, 0:height] = training_product(first, last, train, width, slice(0, lead)) / learning_tally
+    wide_ref[:, height:total] = jnp.zeros((lead, total - height), F32)
+    solved = dot_f32(lead_ref[...].reshape(levels * lead, lead), wide_ref[...])
     for r in range(levels):
-        solved_ref[:, r * total : (r + 1) * total] = dot_f32(lead_ref[r], wide_ref[...])
-    diagonal = lax.broadcasted_iota(jnp.int32, (LANES, height), 1) - lax.broadcasted_iota(
-        jnp.int32, (LANES, height), 0
+        solved_ref[:, r * total : (r + 1) * total] = solved[r * lead : (r + 1) * lead]
+    diagonal = lax.broadcasted_iota(jnp.int32, (size, height), 1) == lax.broadcasted_iota(
+        jnp.int32, (size, height), 0
     )
-    for r0 in range(0, size, LANES):
-        rows = slice(r0, r0 + LANES)
-        side = training_product(last, first, train, width, rows) / learning_tally
-        acc = training_product(last, last, train, width, rows) / learning_tally
-        known = dot_f32(side, solved_ref[...])
-        for r in range(levels):
-            mat_ref[r, rows, 0:height] = (
-                acc + jnp.where(diagonal == r0, shrink_ref[r], 0.0) - known[:, r * total : r * total + height]
-            )
-            mat_ref[r, rows, height:total] = jnp.zeros((LANES, total - height), F32)
+    rows = slice(0, size)
+    side = training_product(last, first, train, width, rows) / learning_tally
+    acc = training_product(last, last, train, width, rows) / learning_tally
+    known = dot_f32(side, solved_ref[...])
+    for r in range(levels):
+        mat_ref[r, :, 0:height] = (
+            acc + jnp.where(diagonal, shrink_ref[r], 0.0) - known[:, r * total : r * total + height]
+        )
+        mat_ref[r, :, height:total] = jnp.zeros((size, total - height), F32)
 
     def follow(j, r):
         c0, c1 = j * LANES, (j + 1) * LANES

time: 57.9 us -> 57 us (0.984)
  Pallas kernels: 27.4 us -> 26.5 us
    pallas_call x1, Pallas kernels: 13.5 us -> 12.9 us  [per_device(): pl.pallas_call(functools.partial(tail_kernel, sources, own_count, learnin...]
where the time goes in v9:
time: 57 us; the launch traced here: 56.8 us
  Pallas kernels  26.5 us (46%)
  starting transfers between devices  15.2 us (27%)
  waiting for transfers between devices  14.5 us (25%)
  between operations  0.69 us (1%)
    pallas_call x1, Pallas kernels, per_device(): pl.pallas_call(functools.partial(tail_kernel, sources, own_count, learnin...  12.9 us
    ppermute x6, starting transfers between devices, fetch(): lax.ppermute(other, 'samples', [(i, i ^ d) for i in range(sources)])  10.2 us
    pallas_call x1, Pallas kernels, per_device(): pl.pallas_call(functools.partial(lead_kernel, sources, own_count, learnin...  9.68 us
    ppermute x6, waiting for transfers between devices, fetch(): lax.ppermute(other, 'samples', [(i, i ^ d) for i in range(sources)])  8.88 us
    ppermute x3, starting transfers between devices, per_device(): lax.ppermute(message, ('samples', 'blocks'), pairs)  3.55 us
    ppermute x3, waiting for transfers between devices, per_device(): lax.ppermute(message, ('samples', 'blocks'), pairs)  3.55 us
    pallas_call x2, Pallas kernels, sort(): pl.pallas_call(kernel, grid=(1,), out_shape=[kept((height, half), BF16, 2...  3.02 us
    ppermute x6, waiting for transfers between devices, swap(): lax.ppermute(x, 'folds', [(i, cores - 1 - i) for i in range(cores)])  2.09 us
  transfers between devices with their start and end apart: 15, of which 10 were waited for; matrix products, arithmetic and copies ran while one was open for 0% of the time, Pallas kernels for 20%

profile of v9, /device:TPU:0, one launch (start us, length us, event | category | flops | bytes accessed | tf_op | source)
XLA Modules:
  0.0 56.8 jit_solution(4772303763640362474)
XLA Ops:
  0.6 1.5 %sort_samples.2 = (bf16[256,256]{1,0:T(8,128)(2,1)S(1)}, bf16[256,256]{1,0:T(8,128)(2,1)S(1)}) custom-call(bf16[500,512]{1,0:T(8,128)(2,1)} %geno_ref.3, s32[1,512]{1,0:T(1,128)} %bitcast.3), custom_call_target="tpu_custom_call" | custom-call | tf_op jit(solution)/shard_map/sort_samples/pallas_call | solution.py:350
  2.1 5.1 %collective-permute-start.2 = (bf16[256,256]{1,0:T(8,128)(2,1)S(1)}, bf16[256,256]{1,0:T(8,128)(2,1)S(1)}, u32[]{:S(2)}, u32[]{:S(2)}) collective-permute-start(bf16[256,256]{1,0:T(8,128)(2,1)S(1)} %get-tuple-element.20.refs_1_.refs_2_), channel_id=1, source_target_pairs={{0,12},{4,8},{8,4},{12,0},{1,13},{5,9},{9,5},{13,1},{2,14},{6,10},... | collective-permute-start | bytes 393224 | tf_op jit(solution)/shard_map/ppermute | solution.py:364
  7.2 0.0 collective-permute-start.1
  7.3 0.6 %collective-permute-start = (bf16[256,256]{1,0:T(8,128)(2,1)S(1)}, bf16[256,256]{1,0:T(8,128)(2,1)S(1)}, u32[]{:S(2)}, u32[]{:S(2)}) collective-permute-start(bf16[256,256]{1,0:T(8,128)(2,1)S(1)} %get-tuple-element.20.refs_1_.refs_2_), channel_id=1, source_target_pairs={{0,4},{4,0},{8,12},{12,8},{1,5},{5,1},{9,13},{13,9},{2,6},{6,2},{1... | collective-permute-start | bytes 393224 | tf_op jit(solution)/shard_map/ppermute | solution.py:364
  7.9 3.8 %collective-permute-done.2.refs_4_.refs_5_ = bf16[256,256]{1,0:T(8,128)(2,1)S(1)} collective-permute-done((bf16[256,256]{1,0:T(8,128)(2,1)S(1)}, bf16[256,256]{1,0:T(8,128)(2,1)S(1)}, u32[]{:S(2)}, u32[]{:S(2)}) %collective-permute-start.2) | collective-permute-done | bytes 131104 | tf_op jit(solution)/shard_map/ppermute | solution.py:364
  11.7 0.0 collective-permute-start.5
  11.7 1.6 %sort_samples.3 = (bf16[288,256]{1,0:T(8,128)(2,1)S(1)}, bf16[288,256]{1,0:T(8,128)(2,1)S(1)}) custom-call(bf16[500,512]{1,0:T(8,128)(2,1)} %geno_ref.3, bf16[20,512]{1,0:T(8,128)(2,1)} %trait_ref.1, s32[1,512]{1,0:T(1,128)} %bitcast.4), custom_call_target="tpu_custom_call" | custom-call | tf_op jit(solution)/shard_map/sort_samples/pallas_call | solution.py:350
  13.3 5.1 %collective-permute-done.1.refs_3_.refs_4_ = bf16[256,256]{1,0:T(8,128)(2,1)S(1)} collective-permute-done((bf16[256,256]{1,0:T(8,128)(2,1)S(1)}, bf16[256,256]{1,0:T(8,128)(2,1)S(1)}, u32[]{:S(2)}, u32[]{:S(2)}) %collective-permute-start.1) | collective-permute-done | bytes 131104 | tf_op jit(solution)/shard_map/ppermute | solution.py:364
  18.3 0.0 collective-permute-done.refs_2_.refs_3_
  18.3 2.5 %collective-permute-start.8 = (bf16[288,256]{1,0:T(8,128)(2,1)S(1)}, bf16[288,256]{1,0:T(8,128)(2,1)S(1)}, u32[]{:S(2)}, u32[]{:S(2)}) collective-permute-start(bf16[288,256]{1,0:T(8,128)(2,1)S(1)} %get-tuple-element.26.refs_10_), channel_id=1, source_target_pairs={{0,12},{4,8},{8,4},{12,0},{1,13},{5,9},{9,5},{13,1},{2,14},{6,10},... | collective-permute-start | bytes 442376 | tf_op jit(solution)/shard_map/ppermute | solution.py:364
  20.8 0.0 collective-permute-start.7
  20.8 1.9 %collective-permute-start.6 = (bf16[288,256]{1,0:T(8,128)(2,1)S(1)}, bf16[288,256]{1,0:T(8,128)(2,1)S(1)}, u32[]{:S(2)}, u32[]{:S(2)}) collective-permute-start(bf16[288,256]{1,0:T(8,128)(2,1)S(1)} %get-tuple-element.26.refs_10_), channel_id=1, source_target_pairs={{0,4},{4,0},{8,12},{12,8},{1,5},{5,1},{9,13},{13,9},{2,6},{6,2},{1... | collective-permute-start | bytes 442376 | tf_op jit(solution)/shard_map/ppermute | solution.py:364
  22.7 0.0 collective-permute-start.4
  22.7 0.0 collective-permute-done.5.refs_8_.refs_9_
  22.7 0.5 collective-permute-start.3
  23.2 0.8 %collective-permute-done.4.refs_7_.refs_8_ = bf16[256,256]{1,0:T(8,128)(2,1)S(1)} collective-permute-done((bf16[256,256]{1,0:T(8,128)(2,1)S(1)}, bf16[256,256]{1,0:T(8,128)(2,1)S(1)}, u32[]{:S(2)}, u32[]{:S(2)}) %collective-permute-start.4) | collective-permute-done | bytes 131104 | tf_op jit(solution)/shard_map/ppermute | solution.py:368
  24.1 0.2 collective-permute-done.3.refs_6_.refs_7_
  24.2 9.7 %invert_lead.1.refs_1_ = f32[2,256,256]{2,1,0:T(8,128)S(1)} custom-call(f32[2]{0:T(128)} %refs_0_.3, bf16[256,256]{1,0:T(8,128)(2,1)S(1)} %get-tuple-element.20.refs_1_.refs_2_, bf16[256,256]{1,0:T(8,128)(2,1)S(1)} %collective-permute-done.refs_2_.refs_3_, bf16[256,256]{1,0:T(8,128)(2,1)S(1)} %collective-permute-done.1.refs_3_.refs_4_, ...), custom_call_target="tpu_custom_call" | custom-call | tf_op jit(solution)/shard_map/invert_lead/pallas_call | solution.py:374
  33.9 0.0 collective-permute-done.8.refs_13_
  33.9 0.0 collective-permute-done.7.refs_12_
  34.0 0.0 collective-permute-done.6.refs_11_
  34.0 0.4 collective-permute-start.9
  34.4 0.2 collective-permute-start.10
  34.5 0.3 collective-permute-start.11
  34.9 0.5 collective-permute-done.9.refs_15_
  35.4 0.3 collective-permute-done.10.refs_16_
  35.7 0.2 collective-permute-done.11.refs_17_
  36.0 12.9 %solve_tail.1 = (bf16[48,512]{1,0:T(8,128)(2,1)S(1)}, bf16[2,32,512]{2,1,0:T(8,128)(2,1)S(1)}) custom-call(f32[2]{0:T(128)} %refs_0_.3, f32[2,256,256]{2,1,0:T(8,128)S(1)} %invert_lead.1.refs_1_, bf16[256,256]{1,0:T(8,128)(2,1)S(1)} %get-tuple-element.20.refs_1_.refs_2_, bf16[256,256]{1,0:T(8,128)(2,1)S(1)} %collective-permute-done.refs_2_.refs_3_, ...), custom_call_target="tpu_custom_call" | custom-call | tf_op jit(solution)/shard_map/solve_tail/pallas_call | solution.py:386
  48.9 1.1 %collective-permute-start.14 = (bf16[48,512]{1,0:T(8,128)(2,1)S(1)}, bf16[48,512]{1,0:T(8,128)(2,1)S(1)}, u32[]{:S(2)}, u32[]{:S(2)}) collective-permute-start(bf16[48,512]{1,0:T(8,128)(2,1)S(1)} %get-tuple-element.33.refs_0_), channel_id=1, source_target_pairs={{6,0},{4,2},{2,4},{0,6},{14,8},{12,10},{10,12},{8,14},{7,1},{5,3},... | collective-permute-start | bytes 147464 | tf_op jit(solution)/shard_map/ppermute | solution.py:415
  50.0 1.9 %collective-permute-start.13 = (bf16[48,512]{1,0:T(8,128)(2,1)S(1)}, bf16[48,512]{1,0:T(8,128)(2,1)S(1)}, u32[]{:S(2)}, u32[]{:S(2)}) collective-permute-start(bf16[48,512]{1,0:T(8,128)(2,1)S(1)} %get-tuple-element.33.refs_0_), channel_id=1, source_target_pairs={{4,0},{6,2},{0,4},{2,6},{12,8},{14,10},{8,12},{10,14},{5,1},{7,3},... | collective-permute-start | bytes 147464 | tf_op jit(solution)/shard_map/ppermute | solution.py:415
  51.9 0.5 collective-permute-start.12
  52.4 1.9 %collective-permute-done.14.refs_3_ = bf16[48,512]{1,0:T(8,128)(2,1)S(1)} collective-permute-done((bf16[48,512]{1,0:T(8,128)(2,1)S(1)}, bf16[48,512]{1,0:T(8,128)(2,1)S(1)}, u32[]{:S(2)}, u32[]{:S(2)}) %collective-permute-start.14) | collective-permute-done | bytes 49184 | tf_op jit(solution)/shard_map/ppermute | solution.py:415
  54.3 0.5 collective-permute-done.13.refs_2_
  54.9 1.1 %collective-permute-done.12.refs_1_ = bf16[48,512]{1,0:T(8,128)(2,1)S(1)} collective-permute-done((bf16[48,512]{1,0:T(8,128)(2,1)S(1)}, bf16[48,512]{1,0:T(8,128)(2,1)S(1)}, u32[]{:S(2)}, u32[]{:S(2)}) %collective-permute-start.12) | collective-permute-done | bytes 49184 | tf_op jit(solution)/shard_map/ppermute | solution.py:415
  56.0 0.9 %level_one.1 = (bf16[2,1,20,2,128]{4,3,2,1,0:T(2,128)(2,1)}, f32[2,1,2,2,2,20]{5,4,3,2,1,0:T(2,128)}, f32[2,1,2,20]{3,2,1,0:T(2,128)}) custom-call(bf16[2,32,512]{2,1,0:T(8,128)(2,1)S(1)} %get-tuple-element.32.trait_ref, bf16[48,512]{1,0:T(8,128)(2,1)S(1)} %get-tuple-element.33.refs_0_, bf16[48,512]{1,0:T(8,128)(2,1)S(1)} %collective-permute-done.12.refs_1_, ...), custom_call_target="tpu_custom_call" | custom-call | tf_op jit(solution)/shard_map/level_one/pallas_call | solution.py:417
Async XLA Ops:
  2.1 9.6 %collective-permute-start.2 = (bf16[256,256]{1,0:T(8,128)(2,1)S(1)}, bf16[256,256]{1,0:T(8,128)(2,1)S(1)}, u32[]{:S(2)}, u32[]{:S(2)}) collective-permute-start(bf16[256,256]{1,0:T(8,128)(2,1)S(1)} %get-tuple-element.20.refs_1_.refs_2_), channel_id=1, source_target_pairs={{0,12},{4,8},{8,4},{12,0},{1,13},{5,9},{9,5},{13,1},{2,14},{6,10},... | collective-permute-start | bytes 393224 | tf_op jit(solution)/shard_map/ppermute | solution.py:364
  7.2 11.1 %collective-permute-start.1 = (bf16[256,256]{1,0:T(8,128)(2,1)S(1)}, bf16[256,256]{1,0:T(8,128)(2,1)S(1)}, u32[]{:S(2)}, u32[]{:S(2)}) collective-permute-start(bf16[256,256]{1,0:T(8,128)(2,1)S(1)} %get-tuple-element.20.refs_1_.refs_2_), channel_id=1, source_target_pairs={{0,8},{4,12},{8,0},{12,4},{1,9},{5,13},{9,1},{13,5},{2,10},{6,14},... | collective-permute-start | bytes 393224 | tf_op jit(solution)/shard_map/ppermute | solution.py:364
  7.3 11.1 %collective-permute-start = (bf16[256,256]{1,0:T(8,128)(2,1)S(1)}, bf16[256,256]{1,0:T(8,128)(2,1)S(1)}, u32[]{:S(2)}, u32[]{:S(2)}) collective-permute-start(bf16[256,256]{1,0:T(8,128)(2,1)S(1)} %get-tuple-element.20.refs_1_.refs_2_), channel_id=1, source_target_pairs={{0,4},{4,0},{8,12},{12,8},{1,5},{5,1},{9,13},{13,9},{2,6},{6,2},{1... | collective-permute-start | bytes 393224 | tf_op jit(solution)/shard_map/ppermute | solution.py:364
  11.7 11.0 %collective-permute-start.5 = (bf16[256,256]{1,0:T(8,128)(2,1)S(1)}, bf16[256,256]{1,0:T(8,128)(2,1)S(1)}, u32[]{:S(2)}, u32[]{:S(2)}) collective-permute-start(bf16[256,256]{1,0:T(8,128)(2,1)S(1)} %collective-permute-done.2.refs_4_.refs_5_), channel_id=1, source_target_pairs={{0,1},{1,0},{2,3},{3,2},{4,5},{5,4},{6,7},{7,6},{8,9},{9,8},{10,11... | collective-permute-start | bytes 393224 | tf_op jit(solution)/shard_map/ppermute | solution.py:368
  18.3 15.6 %collective-permute-start.8 = (bf16[288,256]{1,0:T(8,128)(2,1)S(1)}, bf16[288,256]{1,0:T(8,128)(2,1)S(1)}, u32[]{:S(2)}, u32[]{:S(2)}) collective-permute-start(bf16[288,256]{1,0:T(8,128)(2,1)S(1)} %get-tuple-element.26.refs_10_), channel_id=1, source_target_pairs={{0,12},{4,8},{8,4},{12,0},{1,13},{5,9},{9,5},{13,1},{2,14},{6,10},... | collective-permute-start | bytes 442376 | tf_op jit(solution)/shard_map/ppermute | solution.py:364
  20.8 13.1 %collective-permute-start.7 = (bf16[288,256]{1,0:T(8,128)(2,1)S(1)}, bf16[288,256]{1,0:T(8,128)(2,1)S(1)}, u32[]{:S(2)}, u32[]{:S(2)}) collective-permute-start(bf16[288,256]{1,0:T(8,128)(2,1)S(1)} %get-tuple-element.26.refs_10_), channel_id=1, source_target_pairs={{0,8},{4,12},{8,0},{12,4},{1,9},{5,13},{9,1},{13,5},{2,10},{6,14},... | collective-permute-start | bytes 442376 | tf_op jit(solution)/shard_map/ppermute | solution.py:364
  20.8 13.2 %collective-permute-start.6 = (bf16[288,256]{1,0:T(8,128)(2,1)S(1)}, bf16[288,256]{1,0:T(8,128)(2,1)S(1)}, u32[]{:S(2)}, u32[]{:S(2)}) collective-permute-start(bf16[288,256]{1,0:T(8,128)(2,1)S(1)} %get-tuple-element.26.refs_10_), channel_id=1, source_target_pairs={{0,4},{4,0},{8,12},{12,8},{1,5},{5,1},{9,13},{13,9},{2,6},{6,2},{1... | collective-permute-start | bytes 442376 | tf_op jit(solution)/shard_map/ppermute | solution.py:364
  22.7 1.3 %collective-permute-start.4 = (bf16[256,256]{1,0:T(8,128)(2,1)S(1)}, bf16[256,256]{1,0:T(8,128)(2,1)S(1)}, u32[]{:S(2)}, u32[]{:S(2)}) collective-permute-start(bf16[256,256]{1,0:T(8,128)(2,1)S(1)} %collective-permute-done.1.refs_3_.refs_4_), channel_id=1, source_target_pairs={{0,1},{1,0},{2,3},{3,2},{4,5},{5,4},{6,7},{7,6},{8,9},{9,8},{10,11... | collective-permute-start | bytes 393224 | tf_op jit(solution)/shard_map/ppermute | solution.py:368
  22.7 1.5 %collective-permute-start.3 = (bf16[256,256]{1,0:T(8,128)(2,1)S(1)}, bf16[256,256]{1,0:T(8,128)(2,1)S(1)}, u32[]{:S(2)}, u32[]{:S(2)}) collective-permute-start(bf16[256,256]{1,0:T(8,128)(2,1)S(1)} %collective-permute-done.refs_2_.refs_3_), channel_id=1, source_target_pairs={{0,1},{1,0},{2,3},{3,2},{4,5},{5,4},{6,7},{7,6},{8,9},{9,8},{10,11... | collective-permute-start | bytes 393224 | tf_op jit(solution)/shard_map/ppermute | solution.py:368
  34.0 1.4 %collective-permute-start.9 = (bf16[288,256]{1,0:T(8,128)(2,1)S(1)}, bf16[288,256]{1,0:T(8,128)(2,1)S(1)}, u32[]{:S(2)}, u32[]{:S(2)}) collective-permute-start(bf16[288,256]{1,0:T(8,128)(2,1)S(1)} %collective-permute-done.6.refs_11_), channel_id=1, source_target_pairs={{0,1},{1,0},{2,3},{3,2},{4,5},{5,4},{6,7},{7,6},{8,9},{9,8},{10,11... | collective-permute-start | bytes 442376 | tf_op jit(solution)/shard_map/ppermute | solution.py:368
  34.4 1.4 %collective-permute-start.10 = (bf16[288,256]{1,0:T(8,128)(2,1)S(1)}, bf16[288,256]{1,0:T(8,128)(2,1)S(1)}, u32[]{:S(2)}, u32[]{:S(2)}) collective-permute-start(bf16[288,256]{1,0:T(8,128)(2,1)S(1)} %collective-permute-done.7.refs_12_), channel_id=1, source_target_pairs={{0,1},{1,0},{2,3},{3,2},{4,5},{5,4},{6,7},{7,6},{8,9},{9,8},{10,11... | collective-permute-start | bytes 442376 | tf_op jit(solution)/shard_map/ppermute | solution.py:368
  34.5 1.4 %collective-permute-start.11 = (bf16[288,256]{1,0:T(8,128)(2,1)S(1)}, bf16[288,256]{1,0:T(8,128)(2,1)S(1)}, u32[]{:S(2)}, u32[]{:S(2)}) collective-permute-start(bf16[288,256]{1,0:T(8,128)(2,1)S(1)} %collective-permute-done.8.refs_13_), channel_id=1, source_target_pairs={{0,1},{1,0},{2,3},{3,2},{4,5},{5,4},{6,7},{7,6},{8,9},{9,8},{10,11... | collective-permute-start | bytes 442376 | tf_op jit(solution)/shard_map/ppermute | solution.py:368
  48.9 5.4 %collective-permute-start.14 = (bf16[48,512]{1,0:T(8,128)(2,1)S(1)}, bf16[48,512]{1,0:T(8,128)(2,1)S(1)}, u32[]{:S(2)}, u32[]{:S(2)}) collective-permute-start(bf16[48,512]{1,0:T(8,128)(2,1)S(1)} %get-tuple-element.33.refs_0_), channel_id=1, source_target_pairs={{6,0},{4,2},{2,4},{0,6},{14,8},{12,10},{10,12},{8,14},{7,1},{5,3},... | collective-permute-start | bytes 147464 | tf_op jit(solution)/shard_map/ppermute | solution.py:415
  50.0 4.9 %collective-permute-start.13 = (bf16[48,512]{1,0:T(8,128)(2,1)S(1)}, bf16[48,512]{1,0:T(8,128)(2,1)S(1)}, u32[]{:S(2)}, u32[]{:S(2)}) collective-permute-start(bf16[48,512]{1,0:T(8,128)(2,1)S(1)} %get-tuple-element.33.refs_0_), channel_id=1, source_target_pairs={{4,0},{6,2},{0,4},{2,6},{12,8},{14,10},{8,12},{10,14},{5,1},{7,3},... | collective-permute-start | bytes 147464 | tf_op jit(solution)/shard_map/ppermute | solution.py:415
  51.9 4.1 %collective-permute-start.12 = (bf16[48,512]{1,0:T(8,128)(2,1)S(1)}, bf16[48,512]{1,0:T(8,128)(2,1)S(1)}, u32[]{:S(2)}, u32[]{:S(2)}) collective-permute-start(bf16[48,512]{1,0:T(8,128)(2,1)S(1)} %get-tuple-element.33.refs_0_), channel_id=1, source_target_pairs={{2,0},{0,2},{6,4},{4,6},{10,8},{8,10},{14,12},{12,14},{3,1},{1,3},... | collective-permute-start | bytes 147464 | tf_op jit(solution)/shard_map/ppermute | solution.py:415

commit v10 on v9

--- a/solution.py
+++ b/solution.py
@@ -359,18 +359,20 @@
     other_lead, own_lead = sort(0, lead, False)
     other_tail, own_tail = sort(lead, size + trait_rows, True)
 
-    def fetch(other):
-        return [land(other, 2 * sources)] + [
-            land(lax.ppermute(other, "samples", [(i, i ^ d) for i in range(sources)]), 2 * sources) for d in range(1, sources)
-        ]
+    def move(other, d):
+        return land(lax.ppermute(other, "samples", [(i, i ^ d) for i in range(sources)]), 2 * sources)
+
+    def fetch(other, first, last):
+        return [move(other, d) for d in range(first, last)]
 
     def swap(own, others):
         return [land(own, 2 * sources)] + [land(lax.ppermute(x, "folds", [(i, cores - 1 - i) for i in range(cores)]), 2 * sources) for x in others[1:]]
 
-    others_lead = fetch(other_lead)
+    others_lead = [land(other_lead, 2 * sources)] + fetch(other_lead, 1, sources)
     owns_lead = swap(own_lead, others_lead)
+    others_tail = [land(other_tail, 2 * sources)] + fetch(other_tail, 1, 2)
     other_tail, *others_lead[1:] = lax.optimization_barrier((other_tail, *others_lead[1:]))
-    others_tail = fetch(other_tail)
+    others_tail += fetch(other_tail, 2, sources)
     lead_inverse = pl.pallas_call(
         functools.partial(lead_kernel, sources, own_count, learning_tally),
         out_shape=kept((levels, lead, lead), F32, sources // 2),

time: 57 us -> 57.2 us (level)
  starting transfers between devices: 15.2 us -> 18.4 us
  waiting for transfers between devices: 14.5 us -> 11.4 us
    ppermute x6, starting transfers between devices: 10.2 us -> 13.8 us  [move(): lax.ppermute(other, 'samples', [(i, i ^ d) for i in range(sources)])]
    ppermute x6, waiting for transfers between devices: 8.88 us -> 5.49 us  [move(): lax.ppermute(other, 'samples', [(i, i ^ d) for i in range(sources)])]
where the time goes in v10:
time: 57.2 us; the launch traced here: 57 us
  Pallas kernels  26.5 us (46%)
  starting transfers between devices  18.4 us (32%)
  waiting for transfers between devices  11.4 us (20%)
  between operations  0.68 us (1%)
    ppermute x6, starting transfers between devices, move(): lax.ppermute(other, 'samples', [(i, i ^ d) for i in range(sources)])  13.8 us
    pallas_call x1, Pallas kernels, per_device(): pl.pallas_call(functools.partial(tail_kernel, sources, own_count, learnin...  12.9 us
    pallas_call x1, Pallas kernels, per_device(): pl.pallas_call(functools.partial(lead_kernel, sources, own_count, learnin...  9.68 us
    ppermute x6, waiting for transfers between devices, move(): lax.ppermute(other, 'samples', [(i, i ^ d) for i in range(sources)])  5.49 us
    ppermute x3, waiting for transfers between devices, per_device(): lax.ppermute(message, ('samples', 'blocks'), pairs)  3.56 us
    ppermute x3, starting transfers between devices, per_device(): lax.ppermute(message, ('samples', 'blocks'), pairs)  3.55 us
    pallas_call x2, Pallas kernels, sort(): pl.pallas_call(kernel, grid=(1,), out_shape=[kept((height, half), BF16, 2...  3.02 us
    ppermute x6, waiting for transfers between devices, swap(): lax.ppermute(x, 'folds', [(i, cores - 1 - i) for i in range(cores)])  2.39 us
  transfers between devices with their start and end apart: 15, of which 10 were waited for; matrix products, arithmetic and copies ran while one was open for 0% of the time, Pallas kernels for 20%

profile of v10, /device:TPU:0, one launch (start us, length us, event | category | flops | bytes accessed | tf_op | source)
XLA Modules:
  0.0 57.0 jit_solution(14656856928553136016)
XLA Ops:
  0.6 1.5 %sort_samples.2 = (bf16[256,256]{1,0:T(8,128)(2,1)S(1)}, bf16[256,256]{1,0:T(8,128)(2,1)S(1)}) custom-call(bf16[500,512]{1,0:T(8,128)(2,1)} %geno_ref.3, s32[1,512]{1,0:T(1,128)} %bitcast.3), custom_call_target="tpu_custom_call" | custom-call | tf_op jit(solution)/shard_map/sort_samples/pallas_call | solution.py:350
  2.1 5.1 %collective-permute-start.2 = (bf16[256,256]{1,0:T(8,128)(2,1)S(1)}, bf16[256,256]{1,0:T(8,128)(2,1)S(1)}, u32[]{:S(2)}, u32[]{:S(2)}) collective-permute-start(bf16[256,256]{1,0:T(8,128)(2,1)S(1)} %get-tuple-element.20.refs_1_.refs_2_), channel_id=1, source_target_pairs={{0,12},{4,8},{8,4},{12,0},{1,13},{5,9},{9,5},{13,1},{2,14},{6,10},... | collective-permute-start | bytes 393224 | tf_op jit(solution)/shard_map/ppermute | solution.py:363
  7.2 0.0 collective-permute-start.1
  7.3 0.6 %collective-permute-start = (bf16[256,256]{1,0:T(8,128)(2,1)S(1)}, bf16[256,256]{1,0:T(8,128)(2,1)S(1)}, u32[]{:S(2)}, u32[]{:S(2)}) collective-permute-start(bf16[256,256]{1,0:T(8,128)(2,1)S(1)} %get-tuple-element.20.refs_1_.refs_2_), channel_id=1, source_target_pairs={{0,4},{4,0},{8,12},{12,8},{1,5},{5,1},{9,13},{13,9},{2,6},{6,2},{1... | collective-permute-start | bytes 393224 | tf_op jit(solution)/shard_map/ppermute | solution.py:363
  7.9 3.8 %collective-permute-done.2.refs_4_.refs_5_ = bf16[256,256]{1,0:T(8,128)(2,1)S(1)} collective-permute-done((bf16[256,256]{1,0:T(8,128)(2,1)S(1)}, bf16[256,256]{1,0:T(8,128)(2,1)S(1)}, u32[]{:S(2)}, u32[]{:S(2)}) %collective-permute-start.2) | collective-permute-done | bytes 131104 | tf_op jit(solution)/shard_map/ppermute | solution.py:363
  11.7 0.0 collective-permute-start.5
  11.7 1.6 %sort_samples.3 = (bf16[288,256]{1,0:T(8,128)(2,1)S(1)}, bf16[288,256]{1,0:T(8,128)(2,1)S(1)}) custom-call(bf16[500,512]{1,0:T(8,128)(2,1)} %geno_ref.3, bf16[20,512]{1,0:T(8,128)(2,1)} %trait_ref.1, s32[1,512]{1,0:T(1,128)} %bitcast.4), custom_call_target="tpu_custom_call" | custom-call | tf_op jit(solution)/shard_map/sort_samples/pallas_call | solution.py:350
  13.3 5.4 %collective-permute-start.6 = (bf16[288,256]{1,0:T(8,128)(2,1)S(1)}, bf16[288,256]{1,0:T(8,128)(2,1)S(1)}, u32[]{:S(2)}, u32[]{:S(2)}) collective-permute-start(bf16[288,256]{1,0:T(8,128)(2,1)S(1)} %get-tuple-element.26.refs_10_), channel_id=1, source_target_pairs={{0,4},{4,0},{8,12},{12,8},{1,5},{5,1},{9,13},{13,9},{2,6},{6,2},{1... | collective-permute-start | bytes 442376 | tf_op jit(solution)/shard_map/ppermute | solution.py:363
  18.6 0.0 collective-permute-done.1.refs_3_.refs_4_
  18.6 0.0 collective-permute-done.refs_2_.refs_3_
  18.6 2.7 %collective-permute-start.8 = (bf16[288,256]{1,0:T(8,128)(2,1)S(1)}, bf16[288,256]{1,0:T(8,128)(2,1)S(1)}, u32[]{:S(2)}, u32[]{:S(2)}) collective-permute-start(bf16[288,256]{1,0:T(8,128)(2,1)S(1)} %get-tuple-element.26.refs_10_), channel_id=1, source_target_pairs={{0,12},{4,8},{8,4},{12,0},{1,13},{5,9},{9,5},{13,1},{2,14},{6,10},... | collective-permute-start | bytes 442376 | tf_op jit(solution)/shard_map/ppermute | solution.py:363
  21.3 0.0 collective-permute-start.7
  21.3 0.0 collective-permute-start.4
  21.3 0.0 collective-permute-done.5.refs_8_.refs_9_
  21.3 0.5 collective-permute-start.3
  21.8 0.8 %collective-permute-done.4.refs_7_.refs_8_ = bf16[256,256]{1,0:T(8,128)(2,1)S(1)} collective-permute-done((bf16[256,256]{1,0:T(8,128)(2,1)S(1)}, bf16[256,256]{1,0:T(8,128)(2,1)S(1)}, u32[]{:S(2)}, u32[]{:S(2)}) %collective-permute-start.4) | collective-permute-done | bytes 131104 | tf_op jit(solution)/shard_map/ppermute | solution.py:369
  22.6 0.2 collective-permute-done.3.refs_6_.refs_7_
  22.8 9.7 %invert_lead.1.refs_1_ = f32[2,256,256]{2,1,0:T(8,128)S(1)} custom-call(f32[2]{0:T(128)} %refs_0_.3, bf16[256,256]{1,0:T(8,128)(2,1)S(1)} %get-tuple-element.20.refs_1_.refs_2_, bf16[256,256]{1,0:T(8,128)(2,1)S(1)} %collective-permute-done.refs_2_.refs_3_, bf16[256,256]{1,0:T(8,128)(2,1)S(1)} %collective-permute-done.1.refs_3_.refs_4_, ...), custom_call_target="tpu_custom_call" | custom-call | tf_op jit(solution)/shard_map/invert_lead/pallas_call | solution.py:376
  32.5 0.0 collective-permute-done.6.refs_11_
  32.5 0.0 collective-permute-done.8.refs_13_
  32.5 1.7 %collective-permute-done.7.refs_12_ = bf16[288,256]{1,0:T(8,128)(2,1)S(1)} collective-permute-done((bf16[288,256]{1,0:T(8,128)(2,1)S(1)}, bf16[288,256]{1,0:T(8,128)(2,1)S(1)}, u32[]{:S(2)}, u32[]{:S(2)}) %collective-permute-start.7) | collective-permute-done | bytes 147488 | tf_op jit(solution)/shard_map/ppermute | solution.py:363
  34.2 0.0 collective-permute-start.9
  34.2 0.5 collective-permute-start.10
  34.7 0.0 collective-permute-start.11
  34.7 0.9 %collective-permute-done.9.refs_15_ = bf16[288,256]{1,0:T(8,128)(2,1)S(1)} collective-permute-done((bf16[288,256]{1,0:T(8,128)(2,1)S(1)}, bf16[288,256]{1,0:T(8,128)(2,1)S(1)}, u32[]{:S(2)}, u32[]{:S(2)}) %collective-permute-start.9) | collective-permute-done | bytes 147488 | tf_op jit(solution)/shard_map/ppermute | solution.py:369
  35.6 0.2 collective-permute-done.10.refs_16_
  35.8 0.3 collective-permute-done.11.refs_17_
  36.1 12.9 %solve_tail.1 = (bf16[48,512]{1,0:T(8,128)(2,1)S(1)}, bf16[2,32,512]{2,1,0:T(8,128)(2,1)S(1)}) custom-call(f32[2]{0:T(128)} %refs_0_.3, f32[2,256,256]{2,1,0:T(8,128)S(1)} %invert_lead.1.refs_1_, bf16[256,256]{1,0:T(8,128)(2,1)S(1)} %get-tuple-element.20.refs_1_.refs_2_, bf16[256,256]{1,0:T(8,128)(2,1)S(1)} %collective-permute-done.refs_2_.refs_3_, ...), custom_call_target="tpu_custom_call" | custom-call | tf_op jit(solution)/shard_map/solve_tail/pallas_call | solution.py:388
  49.0 1.1 %collective-permute-start.14 = (bf16[48,512]{1,0:T(8,128)(2,1)S(1)}, bf16[48,512]{1,0:T(8,128)(2,1)S(1)}, u32[]{:S(2)}, u32[]{:S(2)}) collective-permute-start(bf16[48,512]{1,0:T(8,128)(2,1)S(1)} %get-tuple-element.33.refs_0_), channel_id=1, source_target_pairs={{6,0},{4,2},{2,4},{0,6},{14,8},{12,10},{10,12},{8,14},{7,1},{5,3},... | collective-permute-start | bytes 147464 | tf_op jit(solution)/shard_map/ppermute | solution.py:417
  50.2 1.9 %collective-permute-start.13 = (bf16[48,512]{1,0:T(8,128)(2,1)S(1)}, bf16[48,512]{1,0:T(8,128)(2,1)S(1)}, u32[]{:S(2)}, u32[]{:S(2)}) collective-permute-start(bf16[48,512]{1,0:T(8,128)(2,1)S(1)} %get-tuple-element.33.refs_0_), channel_id=1, source_target_pairs={{4,0},{6,2},{0,4},{2,6},{12,8},{14,10},{8,12},{10,14},{5,1},{7,3},... | collective-permute-start | bytes 147464 | tf_op jit(solution)/shard_map/ppermute | solution.py:417
  52.0 0.5 collective-permute-start.12
  52.6 1.8 %collective-permute-done.14.refs_3_ = bf16[48,512]{1,0:T(8,128)(2,1)S(1)} collective-permute-done((bf16[48,512]{1,0:T(8,128)(2,1)S(1)}, bf16[48,512]{1,0:T(8,128)(2,1)S(1)}, u32[]{:S(2)}, u32[]{:S(2)}) %collective-permute-start.14) | collective-permute-done | bytes 49184 | tf_op jit(solution)/shard_map/ppermute | solution.py:417
  54.4 0.6 collective-permute-done.13.refs_2_
  54.9 1.2 %collective-permute-done.12.refs_1_ = bf16[48,512]{1,0:T(8,128)(2,1)S(1)} collective-permute-done((bf16[48,512]{1,0:T(8,128)(2,1)S(1)}, bf16[48,512]{1,0:T(8,128)(2,1)S(1)}, u32[]{:S(2)}, u32[]{:S(2)}) %collective-permute-start.12) | collective-permute-done | bytes 49184 | tf_op jit(solution)/shard_map/ppermute | solution.py:417
  56.1 0.9 %level_one.1 = (bf16[2,1,20,2,128]{4,3,2,1,0:T(2,128)(2,1)}, f32[2,1,2,2,2,20]{5,4,3,2,1,0:T(2,128)}, f32[2,1,2,20]{3,2,1,0:T(2,128)}) custom-call(bf16[2,32,512]{2,1,0:T(8,128)(2,1)S(1)} %get-tuple-element.32.trait_ref, bf16[48,512]{1,0:T(8,128)(2,1)S(1)} %get-tuple-element.33.refs_0_, bf16[48,512]{1,0:T(8,128)(2,1)S(1)} %collective-permute-done.12.refs_1_, ...), custom_call_target="tpu_custom_call" | custom-call | tf_op jit(solution)/shard_map/level_one/pallas_call | solution.py:419
Async XLA Ops:
  2.1 9.6 %collective-permute-start.2 = (bf16[256,256]{1,0:T(8,128)(2,1)S(1)}, bf16[256,256]{1,0:T(8,128)(2,1)S(1)}, u32[]{:S(2)}, u32[]{:S(2)}) collective-permute-start(bf16[256,256]{1,0:T(8,128)(2,1)S(1)} %get-tuple-element.20.refs_1_.refs_2_), channel_id=1, source_target_pairs={{0,12},{4,8},{8,4},{12,0},{1,13},{5,9},{9,5},{13,1},{2,14},{6,10},... | collective-permute-start | bytes 393224 | tf_op jit(solution)/shard_map/ppermute | solution.py:363
  7.2 11.4 %collective-permute-start.1 = (bf16[256,256]{1,0:T(8,128)(2,1)S(1)}, bf16[256,256]{1,0:T(8,128)(2,1)S(1)}, u32[]{:S(2)}, u32[]{:S(2)}) collective-permute-start(bf16[256,256]{1,0:T(8,128)(2,1)S(1)} %get-tuple-element.20.refs_1_.refs_2_), channel_id=1, source_target_pairs={{0,8},{4,12},{8,0},{12,4},{1,9},{5,13},{9,1},{13,5},{2,10},{6,14},... | collective-permute-start | bytes 393224 | tf_op jit(solution)/shard_map/ppermute | solution.py:363
  7.3 11.4 %collective-permute-start = (bf16[256,256]{1,0:T(8,128)(2,1)S(1)}, bf16[256,256]{1,0:T(8,128)(2,1)S(1)}, u32[]{:S(2)}, u32[]{:S(2)}) collective-permute-start(bf16[256,256]{1,0:T(8,128)(2,1)S(1)} %get-tuple-element.20.refs_1_.refs_2_), channel_id=1, source_target_pairs={{0,4},{4,0},{8,12},{12,8},{1,5},{5,1},{9,13},{13,9},{2,6},{6,2},{1... | collective-permute-start | bytes 393224 | tf_op jit(solution)/shard_map/ppermute | solution.py:363
  11.7 9.6 %collective-permute-start.5 = (bf16[256,256]{1,0:T(8,128)(2,1)S(1)}, bf16[256,256]{1,0:T(8,128)(2,1)S(1)}, u32[]{:S(2)}, u32[]{:S(2)}) collective-permute-start(bf16[256,256]{1,0:T(8,128)(2,1)S(1)} %collective-permute-done.2.refs_4_.refs_5_), channel_id=1, source_target_pairs={{0,1},{1,0},{2,3},{3,2},{4,5},{5,4},{6,7},{7,6},{8,9},{9,8},{10,11... | collective-permute-start | bytes 393224 | tf_op jit(solution)/shard_map/ppermute | solution.py:369
  13.3 19.3 %collective-permute-start.6 = (bf16[288,256]{1,0:T(8,128)(2,1)S(1)}, bf16[288,256]{1,0:T(8,128)(2,1)S(1)}, u32[]{:S(2)}, u32[]{:S(2)}) collective-permute-start(bf16[288,256]{1,0:T(8,128)(2,1)S(1)} %get-tuple-element.26.refs_10_), channel_id=1, source_target_pairs={{0,4},{4,0},{8,12},{12,8},{1,5},{5,1},{9,13},{13,9},{2,6},{6,2},{1... | collective-permute-start | bytes 442376 | tf_op jit(solution)/shard_map/ppermute | solution.py:363
  18.6 13.9 %collective-permute-start.8 = (bf16[288,256]{1,0:T(8,128)(2,1)S(1)}, bf16[288,256]{1,0:T(8,128)(2,1)S(1)}, u32[]{:S(2)}, u32[]{:S(2)}) collective-permute-start(bf16[288,256]{1,0:T(8,128)(2,1)S(1)} %get-tuple-element.26.refs_10_), channel_id=1, source_target_pairs={{0,12},{4,8},{8,4},{12,0},{1,13},{5,9},{9,5},{13,1},{2,14},{6,10},... | collective-permute-start | bytes 442376 | tf_op jit(solution)/shard_map/ppermute | solution.py:363
  21.3 12.9 %collective-permute-start.7 = (bf16[288,256]{1,0:T(8,128)(2,1)S(1)}, bf16[288,256]{1,0:T(8,128)(2,1)S(1)}, u32[]{:S(2)}, u32[]{:S(2)}) collective-permute-start(bf16[288,256]{1,0:T(8,128)(2,1)S(1)} %get-tuple-element.26.refs_10_), channel_id=1, source_target_pairs={{0,8},{4,12},{8,0},{12,4},{1,9},{5,13},{9,1},{13,5},{2,10},{6,14},... | collective-permute-start | bytes 442376 | tf_op jit(solution)/shard_map/ppermute | solution.py:363
  21.3 1.3 %collective-permute-start.4 = (bf16[256,256]{1,0:T(8,128)(2,1)S(1)}, bf16[256,256]{1,0:T(8,128)(2,1)S(1)}, u32[]{:S(2)}, u32[]{:S(2)}) collective-permute-start(bf16[256,256]{1,0:T(8,128)(2,1)S(1)} %collective-permute-done.1.refs_3_.refs_4_), channel_id=1, source_target_pairs={{0,1},{1,0},{2,3},{3,2},{4,5},{5,4},{6,7},{7,6},{8,9},{9,8},{10,11... | collective-permute-start | bytes 393224 | tf_op jit(solution)/shard_map/ppermute | solution.py:369
  21.3 1.5 %collective-permute-start.3 = (bf16[256,256]{1,0:T(8,128)(2,1)S(1)}, bf16[256,256]{1,0:T(8,128)(2,1)S(1)}, u32[]{:S(2)}, u32[]{:S(2)}) collective-permute-start(bf16[256,256]{1,0:T(8,128)(2,1)S(1)} %collective-permute-done.refs_2_.refs_3_), channel_id=1, source_target_pairs={{0,1},{1,0},{2,3},{3,2},{4,5},{5,4},{6,7},{7,6},{8,9},{9,8},{10,11... | collective-permute-start | bytes 393224 | tf_op jit(solution)/shard_map/ppermute | solution.py:369
  34.2 1.4 %collective-permute-start.9 = (bf16[288,256]{1,0:T(8,128)(2,1)S(1)}, bf16[288,256]{1,0:T(8,128)(2,1)S(1)}, u32[]{:S(2)}, u32[]{:S(2)}) collective-permute-start(bf16[288,256]{1,0:T(8,128)(2,1)S(1)} %collective-permute-done.6.refs_11_), channel_id=1, source_target_pairs={{0,1},{1,0},{2,3},{3,2},{4,5},{5,4},{6,7},{7,6},{8,9},{9,8},{10,11... | collective-permute-start | bytes 442376 | tf_op jit(solution)/shard_map/ppermute | solution.py:369
  34.2 1.6 %collective-permute-start.10 = (bf16[288,256]{1,0:T(8,128)(2,1)S(1)}, bf16[288,256]{1,0:T(8,128)(2,1)S(1)}, u32[]{:S(2)}, u32[]{:S(2)}) collective-permute-start(bf16[288,256]{1,0:T(8,128)(2,1)S(1)} %collective-permute-done.7.refs_12_), channel_id=1, source_target_pairs={{0,1},{1,0},{2,3},{3,2},{4,5},{5,4},{6,7},{7,6},{8,9},{9,8},{10,11... | collective-permute-start | bytes 442376 | tf_op jit(solution)/shard_map/ppermute | solution.py:369
  34.7 1.4 %collective-permute-start.11 = (bf16[288,256]{1,0:T(8,128)(2,1)S(1)}, bf16[288,256]{1,0:T(8,128)(2,1)S(1)}, u32[]{:S(2)}, u32[]{:S(2)}) collective-permute-start(bf16[288,256]{1,0:T(8,128)(2,1)S(1)} %collective-permute-done.8.refs_13_), channel_id=1, source_target_pairs={{0,1},{1,0},{2,3},{3,2},{4,5},{5,4},{6,7},{7,6},{8,9},{9,8},{10,11... | collective-permute-start | bytes 442376 | tf_op jit(solution)/shard_map/ppermute | solution.py:369
  49.0 5.3 %collective-permute-start.14 = (bf16[48,512]{1,0:T(8,128)(2,1)S(1)}, bf16[48,512]{1,0:T(8,128)(2,1)S(1)}, u32[]{:S(2)}, u32[]{:S(2)}) collective-permute-start(bf16[48,512]{1,0:T(8,128)(2,1)S(1)} %get-tuple-element.33.refs_0_), channel_id=1, source_target_pairs={{6,0},{4,2},{2,4},{0,6},{14,8},{12,10},{10,12},{8,14},{7,1},{5,3},... | collective-permute-start | bytes 147464 | tf_op jit(solution)/shard_map/ppermute | solution.py:417
  50.2 4.8 %collective-permute-start.13 = (bf16[48,512]{1,0:T(8,128)(2,1)S(1)}, bf16[48,512]{1,0:T(8,128)(2,1)S(1)}, u32[]{:S(2)}, u32[]{:S(2)}) collective-permute-start(bf16[48,512]{1,0:T(8,128)(2,1)S(1)} %get-tuple-element.33.refs_0_), channel_id=1, source_target_pairs={{4,0},{6,2},{0,4},{2,6},{12,8},{14,10},{8,12},{10,14},{5,1},{7,3},... | collective-permute-start | bytes 147464 | tf_op jit(solution)/shard_map/ppermute | solution.py:417
  52.0 4.1 %collective-permute-start.12 = (bf16[48,512]{1,0:T(8,128)(2,1)S(1)}, bf16[48,512]{1,0:T(8,128)(2,1)S(1)}, u32[]{:S(2)}, u32[]{:S(2)}) collective-permute-start(bf16[48,512]{1,0:T(8,128)(2,1)S(1)} %get-tuple-element.33.refs_0_), channel_id=1, source_target_pairs={{2,0},{0,2},{6,4},{4,6},{10,8},{8,10},{14,12},{12,14},{3,1},{1,3},... | collective-permute-start | bytes 147464 | tf_op jit(solution)/shard_map/ppermute | solution.py:417

commit v11 on v10

--- a/solution.py
+++ b/solution.py
@@ -370,9 +370,9 @@
 
     others_lead = [land(other_lead, 2 * sources)] + fetch(other_lead, 1, sources)
     owns_lead = swap(own_lead, others_lead)
-    others_tail = [land(other_tail, 2 * sources)] + fetch(other_tail, 1, 2)
+    others_tail = [land(other_tail, 2 * sources)] + fetch(other_tail, 1, 3)
     other_tail, *others_lead[1:] = lax.optimization_barrier((other_tail, *others_lead[1:]))
-    others_tail += fetch(other_tail, 2, sources)
+    others_tail += fetch(other_tail, 3, sources)
     lead_inverse = pl.pallas_call(
         functools.partial(lead_kernel, sources, own_count, learning_tally),
         out_shape=kept((levels, lead, lead), F32, sources // 2),

time: 57.2 us -> 55.7 us (0.974)
  waiting for transfers between devices: 11.4 us -> 9.48 us
    ppermute x6, waiting for transfers between devices: 5.49 us -> 3.82 us  [move(): lax.ppermute(other, 'samples', [(i, i ^ d) for i in range(sources)])]
  transfers between devices with their start and end apart: 15 -> 15, of which waited for: 10 -> 9; matrix products, arithmetic and copies ran while one was open for 0% -> 0% of each run, Pallas kernels for 20% -> 20%
where the time goes in v11:
time: 55.7 us; the launch traced here: 55.5 us
  Pallas kernels  26.5 us (48%)
  starting transfers between devices  18.9 us (34%)
  waiting for transfers between devices  9.48 us (17%)
  between operations  0.69 us (1%)
    ppermute x6, starting transfers between devices, move(): lax.ppermute(other, 'samples', [(i, i ^ d) for i in range(sources)])  13.9 us
    pallas_call x1, Pallas kernels, per_device(): pl.pallas_call(functools.partial(tail_kernel, sources, own_count, learnin...  12.9 us
    pallas_call x1, Pallas kernels, per_device(): pl.pallas_call(functools.partial(lead_kernel, sources, own_count, learnin...  9.68 us
    ppermute x6, waiting for transfers between devices, move(): lax.ppermute(other, 'samples', [(i, i ^ d) for i in range(sources)])  3.82 us
    ppermute x3, waiting for transfers between devices, per_device(): lax.ppermute(message, ('samples', 'blocks'), pairs)  3.57 us
    ppermute x3, starting transfers between devices, per_device(): lax.ppermute(message, ('samples', 'blocks'), pairs)  3.55 us
    pallas_call x2, Pallas kernels, sort(): pl.pallas_call(kernel, grid=(1,), out_shape=[kept((height, half), BF16, 2...  3.02 us
    ppermute x6, waiting for transfers between devices, swap(): lax.ppermute(x, 'folds', [(i, cores - 1 - i) for i in range(cores)])  2.09 us
  transfers between devices with their start and end apart: 15, of which 9 were waited for; matrix products, arithmetic and copies ran while one was open for 0% of the time, Pallas kernels for 20%

profile of v11, /device:TPU:0, one launch (start us, length us, event | category | flops | bytes accessed | tf_op | source)
XLA Modules:
  0.0 55.5 jit_solution(7129056040947591959)
XLA Ops:
  0.6 1.5 %sort_samples.2 = (bf16[256,256]{1,0:T(8,128)(2,1)S(1)}, bf16[256,256]{1,0:T(8,128)(2,1)S(1)}) custom-call(bf16[500,512]{1,0:T(8,128)(2,1)} %geno_ref.3, s32[1,512]{1,0:T(1,128)} %bitcast.3), custom_call_target="tpu_custom_call" | custom-call | tf_op jit(solution)/shard_map/sort_samples/pallas_call | solution.py:350
  2.1 5.1 %collective-permute-start.2 = (bf16[256,256]{1,0:T(8,128)(2,1)S(1)}, bf16[256,256]{1,0:T(8,128)(2,1)S(1)}, u32[]{:S(2)}, u32[]{:S(2)}) collective-permute-start(bf16[256,256]{1,0:T(8,128)(2,1)S(1)} %get-tuple-element.20.refs_1_.refs_2_), channel_id=1, source_target_pairs={{0,12},{4,8},{8,4},{12,0},{1,13},{5,9},{9,5},{13,1},{2,14},{6,10},... | collective-permute-start | bytes 393224 | tf_op jit(solution)/shard_map/ppermute | solution.py:363
  7.2 0.0 collective-permute-start.1
  7.3 0.6 %collective-permute-start = (bf16[256,256]{1,0:T(8,128)(2,1)S(1)}, bf16[256,256]{1,0:T(8,128)(2,1)S(1)}, u32[]{:S(2)}, u32[]{:S(2)}) collective-permute-start(bf16[256,256]{1,0:T(8,128)(2,1)S(1)} %get-tuple-element.20.refs_1_.refs_2_), channel_id=1, source_target_pairs={{0,4},{4,0},{8,12},{12,8},{1,5},{5,1},{9,13},{13,9},{2,6},{6,2},{1... | collective-permute-start | bytes 393224 | tf_op jit(solution)/shard_map/ppermute | solution.py:363
  7.9 3.8 %collective-permute-done.2.refs_4_.refs_5_ = bf16[256,256]{1,0:T(8,128)(2,1)S(1)} collective-permute-done((bf16[256,256]{1,0:T(8,128)(2,1)S(1)}, bf16[256,256]{1,0:T(8,128)(2,1)S(1)}, u32[]{:S(2)}, u32[]{:S(2)}) %collective-permute-start.2) | collective-permute-done | bytes 131104 | tf_op jit(solution)/shard_map/ppermute | solution.py:363
  11.7 0.0 collective-permute-start.5
  11.7 1.6 %sort_samples.3 = (bf16[288,256]{1,0:T(8,128)(2,1)S(1)}, bf16[288,256]{1,0:T(8,128)(2,1)S(1)}) custom-call(bf16[500,512]{1,0:T(8,128)(2,1)} %geno_ref.3, bf16[20,512]{1,0:T(8,128)(2,1)} %trait_ref.1, s32[1,512]{1,0:T(1,128)} %bitcast.4), custom_call_target="tpu_custom_call" | custom-call | tf_op jit(solution)/shard_map/sort_samples/pallas_call | solution.py:350
  13.3 6.6 %collective-permute-start.7 = (bf16[288,256]{1,0:T(8,128)(2,1)S(1)}, bf16[288,256]{1,0:T(8,128)(2,1)S(1)}, u32[]{:S(2)}, u32[]{:S(2)}) collective-permute-start(bf16[288,256]{1,0:T(8,128)(2,1)S(1)} %get-tuple-element.26.refs_10_), channel_id=1, source_target_pairs={{0,8},{4,12},{8,0},{12,4},{1,9},{5,13},{9,1},{13,5},{2,10},{6,14},... | collective-permute-start | bytes 442376 | tf_op jit(solution)/shard_map/ppermute | solution.py:363
  19.8 0.0 collective-permute-start.6
  19.8 0.0 collective-permute-done.1.refs_3_.refs_4_
  19.8 0.0 collective-permute-done.refs_2_.refs_3_
  19.8 1.5 %collective-permute-start.8 = (bf16[288,256]{1,0:T(8,128)(2,1)S(1)}, bf16[288,256]{1,0:T(8,128)(2,1)S(1)}, u32[]{:S(2)}, u32[]{:S(2)}) collective-permute-start(bf16[288,256]{1,0:T(8,128)(2,1)S(1)} %get-tuple-element.26.refs_10_), channel_id=1, source_target_pairs={{0,12},{4,8},{8,4},{12,0},{1,13},{5,9},{9,5},{13,1},{2,14},{6,10},... | collective-permute-start | bytes 442376 | tf_op jit(solution)/shard_map/ppermute | solution.py:363
  21.4 0.0 collective-permute-start.4
  21.4 0.0 collective-permute-done.5.refs_8_.refs_9_
  21.4 0.5 collective-permute-start.3
  21.9 0.8 %collective-permute-done.4.refs_7_.refs_8_ = bf16[256,256]{1,0:T(8,128)(2,1)S(1)} collective-permute-done((bf16[256,256]{1,0:T(8,128)(2,1)S(1)}, bf16[256,256]{1,0:T(8,128)(2,1)S(1)}, u32[]{:S(2)}, u32[]{:S(2)}) %collective-permute-start.4) | collective-permute-done | bytes 131104 | tf_op jit(solution)/shard_map/ppermute | solution.py:369
  22.7 0.2 collective-permute-done.3.refs_6_.refs_7_
  22.9 9.7 %invert_lead.1.refs_1_ = f32[2,256,256]{2,1,0:T(8,128)S(1)} custom-call(f32[2]{0:T(128)} %refs_0_.3, bf16[256,256]{1,0:T(8,128)(2,1)S(1)} %get-tuple-element.20.refs_1_.refs_2_, bf16[256,256]{1,0:T(8,128)(2,1)S(1)} %collective-permute-done.refs_2_.refs_3_, bf16[256,256]{1,0:T(8,128)(2,1)S(1)} %collective-permute-done.1.refs_3_.refs_4_, ...), custom_call_target="tpu_custom_call" | custom-call | tf_op jit(solution)/shard_map/invert_lead/pallas_call | solution.py:376
  32.6 0.0 collective-permute-done.7.refs_12_
  32.6 0.0 collective-permute-done.6.refs_11_
  32.6 0.0 collective-permute-done.8.refs_13_
  32.6 0.4 collective-permute-start.9
  33.0 0.2 collective-permute-start.10
  33.2 0.3 collective-permute-start.11
  33.5 0.5 collective-permute-done.9.refs_15_
  34.1 0.3 collective-permute-done.10.refs_16_
  34.4 0.2 collective-permute-done.11.refs_17_
  34.6 12.9 %solve_tail.1 = (bf16[48,512]{1,0:T(8,128)(2,1)S(1)}, bf16[2,32,512]{2,1,0:T(8,128)(2,1)S(1)}) custom-call(f32[2]{0:T(128)} %refs_0_.3, f32[2,256,256]{2,1,0:T(8,128)S(1)} %invert_lead.1.refs_1_, bf16[256,256]{1,0:T(8,128)(2,1)S(1)} %get-tuple-element.20.refs_1_.refs_2_, bf16[256,256]{1,0:T(8,128)(2,1)S(1)} %collective-permute-done.refs_2_.refs_3_, ...), custom_call_target="tpu_custom_call" | custom-call | tf_op jit(solution)/shard_map/solve_tail/pallas_call | solution.py:388
  47.5 2.7 %collective-permute-start.14 = (bf16[48,512]{1,0:T(8,128)(2,1)S(1)}, bf16[48,512]{1,0:T(8,128)(2,1)S(1)}, u32[]{:S(2)}, u32[]{:S(2)}) collective-permute-start(bf16[48,512]{1,0:T(8,128)(2,1)S(1)} %get-tuple-element.33.refs_0_), channel_id=1, source_target_pairs={{6,0},{4,2},{2,4},{0,6},{14,8},{12,10},{10,12},{8,14},{7,1},{5,3},... | collective-permute-start | bytes 147464 | tf_op jit(solution)/shard_map/ppermute | solution.py:417
  50.2 0.3 collective-permute-start.13
  50.5 0.5 collective-permute-start.12
  51.1 1.5 %collective-permute-done.14.refs_3_ = bf16[48,512]{1,0:T(8,128)(2,1)S(1)} collective-permute-done((bf16[48,512]{1,0:T(8,128)(2,1)S(1)}, bf16[48,512]{1,0:T(8,128)(2,1)S(1)}, u32[]{:S(2)}, u32[]{:S(2)}) %collective-permute-start.14) | collective-permute-done | bytes 49184 | tf_op jit(solution)/shard_map/ppermute | solution.py:417
  52.6 1.8 %collective-permute-done.13.refs_2_ = bf16[48,512]{1,0:T(8,128)(2,1)S(1)} collective-permute-done((bf16[48,512]{1,0:T(8,128)(2,1)S(1)}, bf16[48,512]{1,0:T(8,128)(2,1)S(1)}, u32[]{:S(2)}, u32[]{:S(2)}) %collective-permute-start.13) | collective-permute-done | bytes 49184 | tf_op jit(solution)/shard_map/ppermute | solution.py:417
  54.3 0.3 collective-permute-done.12.refs_1_
  54.6 0.9 %level_one.1 = (bf16[2,1,20,2,128]{4,3,2,1,0:T(2,128)(2,1)}, f32[2,1,2,2,2,20]{5,4,3,2,1,0:T(2,128)}, f32[2,1,2,20]{3,2,1,0:T(2,128)}) custom-call(bf16[2,32,512]{2,1,0:T(8,128)(2,1)S(1)} %get-tuple-element.32.trait_ref, bf16[48,512]{1,0:T(8,128)(2,1)S(1)} %get-tuple-element.33.refs_0_, bf16[48,512]{1,0:T(8,128)(2,1)S(1)} %collective-permute-done.12.refs_1_, ...), custom_call_target="tpu_custom_call" | custom-call | tf_op jit(solution)/shard_map/level_one/pallas_call | solution.py:419
Async XLA Ops:
  2.1 9.6 %collective-permute-start.2 = (bf16[256,256]{1,0:T(8,128)(2,1)S(1)}, bf16[256,256]{1,0:T(8,128)(2,1)S(1)}, u32[]{:S(2)}, u32[]{:S(2)}) collective-permute-start(bf16[256,256]{1,0:T(8,128)(2,1)S(1)} %get-tuple-element.20.refs_1_.refs_2_), channel_id=1, source_target_pairs={{0,12},{4,8},{8,4},{12,0},{1,13},{5,9},{9,5},{13,1},{2,14},{6,10},... | collective-permute-start | bytes 393224 | tf_op jit(solution)/shard_map/ppermute | solution.py:363
  7.2 12.6 %collective-permute-start.1 = (bf16[256,256]{1,0:T(8,128)(2,1)S(1)}, bf16[256,256]{1,0:T(8,128)(2,1)S(1)}, u32[]{:S(2)}, u32[]{:S(2)}) collective-permute-start(bf16[256,256]{1,0:T(8,128)(2,1)S(1)} %get-tuple-element.20.refs_1_.refs_2_), channel_id=1, source_target_pairs={{0,8},{4,12},{8,0},{12,4},{1,9},{5,13},{9,1},{13,5},{2,10},{6,14},... | collective-permute-start | bytes 393224 | tf_op jit(solution)/shard_map/ppermute | solution.py:363
  7.3 12.6 %collective-permute-start = (bf16[256,256]{1,0:T(8,128)(2,1)S(1)}, bf16[256,256]{1,0:T(8,128)(2,1)S(1)}, u32[]{:S(2)}, u32[]{:S(2)}) collective-permute-start(bf16[256,256]{1,0:T(8,128)(2,1)S(1)} %get-tuple-element.20.refs_1_.refs_2_), channel_id=1, source_target_pairs={{0,4},{4,0},{8,12},{12,8},{1,5},{5,1},{9,13},{13,9},{2,6},{6,2},{1... | collective-permute-start | bytes 393224 | tf_op jit(solution)/shard_map/ppermute | solution.py:363
  11.7 9.7 %collective-permute-start.5 = (bf16[256,256]{1,0:T(8,128)(2,1)S(1)}, bf16[256,256]{1,0:T(8,128)(2,1)S(1)}, u32[]{:S(2)}, u32[]{:S(2)}) collective-permute-start(bf16[256,256]{1,0:T(8,128)(2,1)S(1)} %collective-permute-done.2.refs_4_.refs_5_), channel_id=1, source_target_pairs={{0,1},{1,0},{2,3},{3,2},{4,5},{5,4},{6,7},{7,6},{8,9},{9,8},{10,11... | collective-permute-start | bytes 393224 | tf_op jit(solution)/shard_map/ppermute | solution.py:369
  13.3 19.3 %collective-permute-start.7 = (bf16[288,256]{1,0:T(8,128)(2,1)S(1)}, bf16[288,256]{1,0:T(8,128)(2,1)S(1)}, u32[]{:S(2)}, u32[]{:S(2)}) collective-permute-start(bf16[288,256]{1,0:T(8,128)(2,1)S(1)} %get-tuple-element.26.refs_10_), channel_id=1, source_target_pairs={{0,8},{4,12},{8,0},{12,4},{1,9},{5,13},{9,1},{13,5},{2,10},{6,14},... | collective-permute-start | bytes 442376 | tf_op jit(solution)/shard_map/ppermute | solution.py:363
  19.8 12.8 %collective-permute-start.6 = (bf16[288,256]{1,0:T(8,128)(2,1)S(1)}, bf16[288,256]{1,0:T(8,128)(2,1)S(1)}, u32[]{:S(2)}, u32[]{:S(2)}) collective-permute-start(bf16[288,256]{1,0:T(8,128)(2,1)S(1)} %get-tuple-element.26.refs_10_), channel_id=1, source_target_pairs={{0,4},{4,0},{8,12},{12,8},{1,5},{5,1},{9,13},{13,9},{2,6},{6,2},{1... | collective-permute-start | bytes 442376 | tf_op jit(solution)/shard_map/ppermute | solution.py:363
  19.8 12.8 %collective-permute-start.8 = (bf16[288,256]{1,0:T(8,128)(2,1)S(1)}, bf16[288,256]{1,0:T(8,128)(2,1)S(1)}, u32[]{:S(2)}, u32[]{:S(2)}) collective-permute-start(bf16[288,256]{1,0:T(8,128)(2,1)S(1)} %get-tuple-element.26.refs_10_), channel_id=1, source_target_pairs={{0,12},{4,8},{8,4},{12,0},{1,13},{5,9},{9,5},{13,1},{2,14},{6,10},... | collective-permute-start | bytes 442376 | tf_op jit(solution)/shard_map/ppermute | solution.py:363
  21.4 1.3 %collective-permute-start.4 = (bf16[256,256]{1,0:T(8,128)(2,1)S(1)}, bf16[256,256]{1,0:T(8,128)(2,1)S(1)}, u32[]{:S(2)}, u32[]{:S(2)}) collective-permute-start(bf16[256,256]{1,0:T(8,128)(2,1)S(1)} %collective-permute-done.1.refs_3_.refs_4_), channel_id=1, source_target_pairs={{0,1},{1,0},{2,3},{3,2},{4,5},{5,4},{6,7},{7,6},{8,9},{9,8},{10,11... | collective-permute-start | bytes 393224 | tf_op jit(solution)/shard_map/ppermute | solution.py:369
  21.4 1.5 %collective-permute-start.3 = (bf16[256,256]{1,0:T(8,128)(2,1)S(1)}, bf16[256,256]{1,0:T(8,128)(2,1)S(1)}, u32[]{:S(2)}, u32[]{:S(2)}) collective-permute-start(bf16[256,256]{1,0:T(8,128)(2,1)S(1)} %collective-permute-done.refs_2_.refs_3_), channel_id=1, source_target_pairs={{0,1},{1,0},{2,3},{3,2},{4,5},{5,4},{6,7},{7,6},{8,9},{9,8},{10,11... | collective-permute-start | bytes 393224 | tf_op jit(solution)/shard_map/ppermute | solution.py:369
  32.6 1.4 %collective-permute-start.9 = (bf16[288,256]{1,0:T(8,128)(2,1)S(1)}, bf16[288,256]{1,0:T(8,128)(2,1)S(1)}, u32[]{:S(2)}, u32[]{:S(2)}) collective-permute-start(bf16[288,256]{1,0:T(8,128)(2,1)S(1)} %collective-permute-done.6.refs_11_), channel_id=1, source_target_pairs={{0,1},{1,0},{2,3},{3,2},{4,5},{5,4},{6,7},{7,6},{8,9},{9,8},{10,11... | collective-permute-start | bytes 442376 | tf_op jit(solution)/shard_map/ppermute | solution.py:369
  33.0 1.4 %collective-permute-start.10 = (bf16[288,256]{1,0:T(8,128)(2,1)S(1)}, bf16[288,256]{1,0:T(8,128)(2,1)S(1)}, u32[]{:S(2)}, u32[]{:S(2)}) collective-permute-start(bf16[288,256]{1,0:T(8,128)(2,1)S(1)} %collective-permute-done.7.refs_12_), channel_id=1, source_target_pairs={{0,1},{1,0},{2,3},{3,2},{4,5},{5,4},{6,7},{7,6},{8,9},{9,8},{10,11... | collective-permute-start | bytes 442376 | tf_op jit(solution)/shard_map/ppermute | solution.py:369
  33.2 1.4 %collective-permute-start.11 = (bf16[288,256]{1,0:T(8,128)(2,1)S(1)}, bf16[288,256]{1,0:T(8,128)(2,1)S(1)}, u32[]{:S(2)}, u32[]{:S(2)}) collective-permute-start(bf16[288,256]{1,0:T(8,128)(2,1)S(1)} %collective-permute-done.8.refs_13_), channel_id=1, source_target_pairs={{0,1},{1,0},{2,3},{3,2},{4,5},{5,4},{6,7},{7,6},{8,9},{9,8},{10,11... | collective-permute-start | bytes 442376 | tf_op jit(solution)/shard_map/ppermute | solution.py:369
  47.5 5.1 %collective-permute-start.14 = (bf16[48,512]{1,0:T(8,128)(2,1)S(1)}, bf16[48,512]{1,0:T(8,128)(2,1)S(1)}, u32[]{:S(2)}, u32[]{:S(2)}) collective-permute-start(bf16[48,512]{1,0:T(8,128)(2,1)S(1)} %get-tuple-element.33.refs_0_), channel_id=1, source_target_pairs={{6,0},{4,2},{2,4},{0,6},{14,8},{12,10},{10,12},{8,14},{7,1},{5,3},... | collective-permute-start | bytes 147464 | tf_op jit(solution)/shard_map/ppermute | solution.py:417
  50.2 4.1 %collective-permute-start.13 = (bf16[48,512]{1,0:T(8,128)(2,1)S(1)}, bf16[48,512]{1,0:T(8,128)(2,1)S(1)}, u32[]{:S(2)}, u32[]{:S(2)}) collective-permute-start(bf16[48,512]{1,0:T(8,128)(2,1)S(1)} %get-tuple-element.33.refs_0_), channel_id=1, source_target_pairs={{4,0},{6,2},{0,4},{2,6},{12,8},{14,10},{8,12},{10,14},{5,1},{7,3},... | collective-permute-start | bytes 147464 | tf_op jit(solution)/shard_map/ppermute | solution.py:417
  50.5 4.1 %collective-permute-start.12 = (bf16[48,512]{1,0:T(8,128)(2,1)S(1)}, bf16[48,512]{1,0:T(8,128)(2,1)S(1)}, u32[]{:S(2)}, u32[]{:S(2)}) collective-permute-start(bf16[48,512]{1,0:T(8,128)(2,1)S(1)} %get-tuple-element.33.refs_0_), channel_id=1, source_target_pairs={{2,0},{0,2},{6,4},{4,6},{10,8},{8,10},{14,12},{12,14},{3,1},{1,3},... | collective-permute-start | bytes 147464 | tf_op jit(solution)/shard_map/ppermute | solution.py:417
